TPU v7x, 32 devices: a whole 2x2x4 slice. The times are simulated.
32 devices in a mesh: dp: 16 (over z, x, core), inner: 2 (over y).
Axes of the slice: x: 2, y: 2, z: 4, core: 2. Of those that a mesh axis runs over, the one named last changes fastest.
Arguments:
- tokens: bfloat16 [65536, 768], P(('dp', 'inner')), may hold values from -6 to 6
- weight_qkv: bfloat16 [768, 2304], P(('dp', 'inner')), may hold values from -0.21875 to 0.21875
- bias_qv: bfloat16 [1536], P(('dp', 'inner')), may hold values from -1.1953125 to 1.1953125
- weight_out: bfloat16 [768, 768], P(('dp', 'inner')), may hold values from -1 to 1
- bias_out: bfloat16 [768], P(('dp', 'inner')), may hold values from -1.1953125 to 1.1953125
- gain_one: bfloat16 [768], P(('dp', 'inner')), may hold values from 0.5 to 1.5
- shift_one: bfloat16 [768], P(('dp', 'inner')), may hold values from -1.1953125 to 1.1953125
- weight_in: bfloat16 [768, 3072], P(('dp', 'inner')), may hold values from -0.21875 to 0.21875
- bias_in: bfloat16 [3072], P(('dp', 'inner')), may hold values from -1.1953125 to 1.1953125
- weight_fin: bfloat16 [3072, 768], P(('dp', 'inner')), may hold values from -0.109375 to 0.109375
- bias_fin: bfloat16 [768], P(('dp', 'inner')), may hold values from -1.1953125 to 1.1953125
- gain_two: bfloat16 [768], P(('dp', 'inner')), may hold values from 0.5 to 1.5
- shift_two: bfloat16 [768], P(('dp', 'inner')), may hold values from -1.1953125 to 1.1953125
- segments: int32 [128, 512], P(('dp', 'inner')), may hold values from 0 to 7, never falling along the last dimension, each value on 1 to 128 neighbouring positions
- cotangent: bfloat16 [65536, 768], P(('dp', 'inner')), may hold values from -6 to 6
Outputs:
- output: bfloat16 [65536, 768], P(('dp', 'inner'))
- grad_tokens: float32 [65536, 768], P(('dp', 'inner'))
- grad_weight_qkv: float32 [768, 2304], P(('dp', 'inner'))
- grad_bias_qv: float32 [1536], P(('dp', 'inner'))
- grad_weight_out: float32 [768, 768], P(('dp', 'inner'))
- grad_bias_out: float32 [768], P(('dp', 'inner'))
- grad_gain_one: float32 [768], P(('dp', 'inner'))
- grad_shift_one: float32 [768], P(('dp', 'inner'))
- grad_weight_in: float32 [768, 3072], P(('dp', 'inner'))
- grad_bias_in: float32 [3072], P(('dp', 'inner'))
- grad_weight_fin: float32 [3072, 768], P(('dp', 'inner'))
- grad_bias_fin: float32 [768], P(('dp', 'inner'))
- grad_gain_two: float32 [768], P(('dp', 'inner'))
- grad_shift_two: float32 [768], P(('dp', 'inner'))
Inputs may be any that keep to these rules, and one draw needn't show every extreme that they name: `segments`: along each row the pair number never falls; each of the 8 pairs has 1 to 128 tokens, and some pair has exactly 128.
All inputs are finite; a program needn't handle non-finite values.
Results may differ from a plain program's by a relative error of at most 0.013.
Values may be sent and summed in bfloat16 or wider, within the bound.
A program may use at most 256 MiB of HBM per device.

v0:
```python
import jax
import jax.numpy as jnp
from jax import lax
from jax.sharding import PartitionSpec as P

HEAD_DIM = 64


EPSILON = 1e-06
NEG_FILL = -1e30


def product(left, right):
    return jnp.dot(left, right, preferred_element_type=jnp.float32)


def product_over_rows(left, right):
    return lax.dot_general(
        left, right, (((0,), (0,)), ((), ())), preferred_element_type=jnp.float32
    )


def product_transposed(left, right):
    return lax.dot_general(
        left, right, (((1,), (1,)), ((), ())), preferred_element_type=jnp.float32
    )


def gelu_exact(inputs):
    return jax.nn.gelu(inputs, approximate=False)


def normalize(summed):
    center = summed - jnp.mean(summed, axis=-1, keepdims=True)
    inverse = lax.rsqrt(jnp.mean(center * center, axis=-1, keepdims=True) + EPSILON)
    return (center * inverse, inverse)


def normalize_back(grad_normed, normed, inverse):
    mean_grad = jnp.mean(grad_normed, axis=-1, keepdims=True)
    mean_cross = jnp.mean(grad_normed * normed, axis=-1, keepdims=True)
    return inverse * (grad_normed - mean_grad - normed * mean_cross)


def gather_attention(weight_qkv, bias_qv, weight_out, bias_out, gain_one, shift_one):
    return (
        lax.all_gather(weight_qkv, ("dp", "inner"), axis=0, tiled=True),
        lax.all_gather(bias_qv, ("dp", "inner"), axis=0, tiled=True),
        lax.all_gather(weight_out, ("dp", "inner"), axis=0, tiled=True),
        lax.all_gather(bias_out, ("dp", "inner"), axis=0, tiled=True),
        lax.all_gather(gain_one, ("dp", "inner"), axis=0, tiled=True),
        lax.all_gather(shift_one, ("dp", "inner"), axis=0, tiled=True),
    )


def gather_feed(weight_in, bias_in, weight_fin, bias_fin, gain_two, shift_two):
    return (
        lax.all_gather(weight_in, ("dp", "inner"), axis=0, tiled=True),
        lax.all_gather(bias_in, ("dp", "inner"), axis=0, tiled=True),
        lax.all_gather(weight_fin, ("dp", "inner"), axis=0, tiled=True),
        lax.all_gather(bias_fin, ("dp", "inner"), axis=0, tiled=True),
        lax.all_gather(gain_two, ("dp", "inner"), axis=0, tiled=True),
        lax.all_gather(shift_two, ("dp", "inner"), axis=0, tiled=True),
    )


def reduce_feed(grads):
    return (
        lax.psum_scatter(grads[0], ("dp", "inner"), scatter_dimension=0, tiled=True),
        lax.psum_scatter(grads[1], ("dp", "inner"), scatter_dimension=0, tiled=True),
        lax.psum_scatter(grads[2], ("dp", "inner"), scatter_dimension=0, tiled=True),
        lax.psum_scatter(grads[3], ("dp", "inner"), scatter_dimension=0, tiled=True),
        lax.psum_scatter(grads[4], ("dp", "inner"), scatter_dimension=0, tiled=True),
        lax.psum_scatter(grads[5], ("dp", "inner"), scatter_dimension=0, tiled=True),
    )


def reduce_attention(grads):
    return (
        lax.psum_scatter(grads[0], ("dp", "inner"), scatter_dimension=0, tiled=True),
        lax.psum_scatter(grads[1], ("dp", "inner"), scatter_dimension=0, tiled=True),
        lax.psum_scatter(grads[2], ("dp", "inner"), scatter_dimension=0, tiled=True),
        lax.psum_scatter(grads[3], ("dp", "inner"), scatter_dimension=0, tiled=True),
        lax.psum_scatter(grads[4], ("dp", "inner"), scatter_dimension=0, tiled=True),
        lax.psum_scatter(grads[5], ("dp", "inner"), scatter_dimension=0, tiled=True),
    )


def split_heads(rows):
    return rows.reshape(rows.shape[0], rows.shape[1] // HEAD_DIM, HEAD_DIM)


def masked_scores(queries, key_rows, segment_row):
    scores = jnp.einsum(
        "qhd,khd->hqk",
        split_heads(queries),
        split_heads(key_rows),
        preferred_element_type=jnp.float32,
    ) * HEAD_DIM ** (-0.5)
    same_pair = segment_row[:, None] == segment_row[None, :]
    return jnp.where(same_pair[None], scores, NEG_FILL)


def attend(inputs):
    queries, key_rows, values, segment_row = inputs
    scores = masked_scores(queries, key_rows, segment_row)
    maxima = jnp.max(scores, axis=-1, keepdims=True)
    exponent = jnp.exp(scores - maxima)
    totals = jnp.sum(exponent, axis=-1, keepdims=True)
    attn_probs = exponent / totals
    context = jnp.einsum(
        "hqk,khd->qhd",
        attn_probs.astype(jnp.bfloat16),
        split_heads(values),
        preferred_element_type=jnp.float32,
    )
    return (context.reshape(queries.shape).astype(jnp.bfloat16), maxima + jnp.log(totals))


def attend_back(inputs):
    queries, key_rows, values, segment_row, log_total, grad_context = inputs
    scores = masked_scores(queries, key_rows, segment_row)
    attn_probs = jnp.exp(scores - log_total)
    grad_heads = split_heads(grad_context)
    grad_probs = jnp.einsum(
        "qhd,khd->hqk", grad_heads, split_heads(values), preferred_element_type=jnp.float32
    )
    grad_values = jnp.einsum(
        "hqk,qhd->khd",
        attn_probs.astype(jnp.bfloat16),
        grad_heads,
        preferred_element_type=jnp.float32,
    )
    row_dots = jnp.sum(attn_probs * grad_probs, axis=-1, keepdims=True)
    grad_scores = (attn_probs * (grad_probs - row_dots)).astype(jnp.bfloat16)
    factor = HEAD_DIM ** (-0.5)
    grad_queries = (
        jnp.einsum(
            "hqk,khd->qhd", grad_scores, split_heads(key_rows), preferred_element_type=jnp.float32
        )
        * factor
    )
    grad_keys = (
        jnp.einsum(
            "hqk,qhd->khd", grad_scores, split_heads(queries), preferred_element_type=jnp.float32
        )
        * factor
    )
    length = queries.shape[0]
    return jnp.concatenate(
        [
            grad_queries.reshape(length, -1),
            grad_keys.reshape(length, -1),
            grad_values.reshape(length, -1),
        ],
        axis=1,
    ).astype(jnp.bfloat16)


def project(tokens, weight_qkv, bias_qv):
    model_width = tokens.shape[1]
    joined = product(tokens, weight_qkv)
    biases = bias_qv.astype(jnp.float32)
    queries = (joined[:, :model_width] + biases[:model_width]).astype(jnp.bfloat16)
    key_rows = joined[:, model_width : 2 * model_width].astype(jnp.bfloat16)
    values = (joined[:, 2 * model_width :] + biases[model_width:]).astype(jnp.bfloat16)
    return (queries, key_rows, values)


def shards(
    tokens,
    weight_qkv,
    bias_qv,
    weight_out,
    bias_out,
    gain_one,
    shift_one,
    weight_in,
    bias_in,
    weight_fin,
    bias_fin,
    gain_two,
    shift_two,
    segments,
    cotangent,
):
    sequence_count = segments.shape[0]
    length = segments.shape[1]
    model_width = tokens.shape[1]
    sequence_shape = (sequence_count, length, model_width)
    attn_full = gather_attention(weight_qkv, bias_qv, weight_out, bias_out, gain_one, shift_one)
    queries, key_rows, values = project(tokens, attn_full[0], attn_full[1])
    query_seqs = queries.reshape(sequence_shape)
    key_seqs = key_rows.reshape(sequence_shape)
    value_seqs = values.reshape(sequence_shape)
    context, log_total = lax.map(attend, (query_seqs, key_seqs, value_seqs, segments))
    context = context.reshape(tokens.shape)
    attn_branch = product(context, attn_full[2]) + attn_full[3].astype(jnp.float32)
    normed_one, inverse_one = normalize(tokens.astype(jnp.float32) + attn_branch)
    gain_full_one = attn_full[4].astype(jnp.float32)
    hidden = normed_one * gain_full_one + attn_full[5].astype(jnp.float32)
    hidden_low = hidden.astype(jnp.bfloat16)
    ffn_full = gather_feed(weight_in, bias_in, weight_fin, bias_fin, gain_two, shift_two)
    pre_act = product(hidden_low, ffn_full[0]) + ffn_full[1].astype(jnp.float32)
    activated_float, gelu_pull = jax.vjp(gelu_exact, pre_act)
    activated = activated_float.astype(jnp.bfloat16)
    ffn_branch = product(activated, ffn_full[2]) + ffn_full[3].astype(jnp.float32)
    normed_two, inverse_two = normalize(hidden + ffn_branch)
    gain_full_two = ffn_full[4].astype(jnp.float32)
    output = (normed_two * gain_full_two + ffn_full[5].astype(jnp.float32)).astype(jnp.bfloat16)
    grad_out = cotangent.astype(jnp.float32)
    grad_gain_two = jnp.sum(grad_out * normed_two, axis=0)
    grad_shift_two = jnp.sum(grad_out, axis=0)
    grad_sum_two = normalize_back(grad_out * gain_full_two, normed_two, inverse_two)
    grad_ffn = grad_sum_two.astype(jnp.bfloat16)
    ffn_back = gather_feed(weight_in, bias_in, weight_fin, bias_fin, gain_two, shift_two)
    grad_weight_fin = product_over_rows(activated, grad_ffn)
    grad_bias_fin = jnp.sum(grad_ffn.astype(jnp.float32), axis=0)
    grad_active = product_transposed(grad_ffn, ffn_back[2])
    grad_pre = gelu_pull(grad_active)[0].astype(jnp.bfloat16)
    grad_bias_in = jnp.sum(grad_pre.astype(jnp.float32), axis=0)
    grad_weight_in = product_over_rows(hidden_low, grad_pre)
    grad_hidden = grad_sum_two + product_transposed(grad_pre, ffn_back[0])
    ffn_shards = reduce_feed(
        (
            grad_weight_in,
            grad_bias_in,
            grad_weight_fin,
            grad_bias_fin,
            grad_gain_two,
            grad_shift_two,
        )
    )
    grad_gain_one = jnp.sum(grad_hidden * normed_one, axis=0)
    grad_shift_one = jnp.sum(grad_hidden, axis=0)
    grad_sum_one = normalize_back(grad_hidden * gain_full_one, normed_one, inverse_one)
    grad_attn = grad_sum_one.astype(jnp.bfloat16)
    attn_back = gather_attention(weight_qkv, bias_qv, weight_out, bias_out, gain_one, shift_one)
    grad_weight_out = product_over_rows(context, grad_attn)
    grad_bias_out = jnp.sum(grad_attn.astype(jnp.float32), axis=0)
    grad_context = product_transposed(grad_attn, attn_back[2]).astype(jnp.bfloat16)
    grad_joined = lax.map(
        attend_back,
        (
            query_seqs,
            key_seqs,
            value_seqs,
            segments,
            log_total,
            grad_context.reshape(sequence_shape),
        ),
    )
    grad_joined = grad_joined.reshape(tokens.shape[0], 3 * model_width)
    grad_bias_qv = jnp.concatenate(
        [
            jnp.sum(grad_joined[:, :model_width].astype(jnp.float32), axis=0),
            jnp.sum(grad_joined[:, 2 * model_width :].astype(jnp.float32), axis=0),
        ]
    )
    grad_weight_qkv = product_over_rows(tokens, grad_joined)
    grad_tokens = grad_sum_one + product_transposed(grad_joined, attn_back[0])
    attn_shards = reduce_attention(
        (
            grad_weight_qkv,
            grad_bias_qv,
            grad_weight_out,
            grad_bias_out,
            grad_gain_one,
            grad_shift_one,
        )
    )
    return (
        output,
        grad_tokens,
        attn_shards[0],
        attn_shards[1],
        attn_shards[2],
        attn_shards[3],
        attn_shards[4],
        attn_shards[5],
        ffn_shards[0],
        ffn_shards[1],
        ffn_shards[2],
        ffn_shards[3],
        ffn_shards[4],
        ffn_shards[5],
    )


def solution(mesh):
    in_specs = (
        P(("dp", "inner"), None),
        P(("dp", "inner"), None),
        P(("dp", "inner")),
        P(("dp", "inner"), None),
        P(("dp", "inner")),
        P(("dp", "inner")),
        P(("dp", "inner")),
        P(("dp", "inner"), None),
        P(("dp", "inner")),
        P(("dp", "inner"), None),
        P(("dp", "inner")),
        P(("dp", "inner")),
        P(("dp", "inner")),
        P(("dp", "inner"), None),
        P(("dp", "inner"), None),
    )
    out_specs = (
        P(("dp", "inner"), None),
        P(("dp", "inner"), None),
        P(("dp", "inner"), None),
        P(("dp", "inner")),
        P(("dp", "inner"), None),
        P(("dp", "inner")),
        P(("dp", "inner")),
        P(("dp", "inner")),
        P(("dp", "inner"), None),
        P(("dp", "inner")),
        P(("dp", "inner"), None),
        P(("dp", "inner")),
        P(("dp", "inner")),
        P(("dp", "inner")),
    )
    return jax.shard_map(shards, mesh=mesh, in_specs=in_specs, out_specs=out_specs, check_vma=False)
```

profile of v0, /device:TPU:0, one launch (start us, length us, event | category | flops | bytes accessed | tf_op | source)
XLA Modules:
  0.0 987.5 jit_solution(10293317913388309445)
XLA Ops:
  16.8 42.5 %all-reduce.17 = (bf16[1536]{0:T(1024)(128)(2,1)S(1)}, bf16[768]{0:T(1024)(128)(2,1)S(1)}, bf16[768]{0:T(1024)(128)(2,1)S(1)}, bf16[768]{0:T(1024)(128)(2,1)S(1)...) all-reduce(bf16[1536]{0:T(1024)(128)(2,1)S(1)} %dynamic-update-slic, ...), channel_id=1, replica_groups=mesh['dp'=16,'inner'=2] {'dp','inner'}, use_global_device_ids=true, to_apply=%add | all-reduce | flops 9216 | bytes 36864
  73.9 10.7 %fusion.45 = f32[2048,2304]{1,0:T(8,128)S(1)} fusion(bf16[2048,768]{1,0:T(8,128)(2,1)} %param.19, bf16[768,2304]{1,0:T(8,128)(2,1)} %all-gather.5.cloned.1.call-done), kind=kOutput, calls=%fused_computation.109 | convolution fusion | flops 7247757312 | bytes 25559040 | tf_op jit(solution)/shard_map/dot_general | solution.py:14
  100.5 55.5 %while.22 = (s32[]{:T(128)}, bf16[4,512,768]{2,1,0:T(8,128)(2,1)}, f32[4,12,512,1]{2,1,3,0:T(8,128)}, bf16[4,512,768]{1,2,0:T(8,128)(2,1)}, s32[4,512]{1,0:T(4,1...) while((s32[]{:T(128)}, bf16[4,512,768]{2,1,0:T(8,128)(2,1)}, ...), condition=%wide.region_3.4_spmd, body=%wide.region_0.3_spmd.sunk | while | flops 843704320 | bytes 50019424 | solution.py:196
  166.9 28.6 %all-gather.9.cloned.1.call-done = bf16[768,3072]{1,0:T(8,128)(2,1)} async-done(((bf16[24,3072]{1,0:T(8,128)(2,1)}), bf16[768,3072]{1,0:T(8,128)(2,1)}) %all-gather.9.cloned.1.call-update) | async-done | bytes 4718608 | tf_op jit(solution)/shard_map/all_gather | solution.py:58
  195.5 70.1 %multiply_convert_fusion.3 = (bf16[2048,3072]{1,0:T(8,128)(2,1)}, f32[2048,3072]{1,0:T(8,128)}, f32[2048,3072]{1,0:T(8,128)}) fusion(f32[3072]{0:T(1024)S(1)} %copy-done.25, bf16[768,3072]{1,0:T(8,128)(2,1)} %all-gather.9.cloned.1.call-done, bf16[2048,768]{0,1:T(8,128)(2,1)S(1)} %fusion.38.clone.4), kind=kOutput, calls=%fused_computation.40 | convolution fusion | flops 10078912512 | bytes 70791168 | tf_op jit(solution)/shard_map/dot_general | solution.py:14
  265.7 18.0 %fusion.43 = (f32[2048]{0:T(1024)S(1)}, f32[2048,768]{0,1:T(8,128)}) fusion(f32[768]{0:T(1024)S(1)} %copy-done.27, bf16[2048,3072]{1,0:T(8,128)(2,1)} %get-tuple-element.244, bf16[3072,768]{1,0:T(8,128)(2,1)} %all-gather.11.cloned.1.call-done, f32[768]{0:T(1024)S(1)} %copy-done.20, f32[768]{0:T(1024)S(1)} %copy-done.14, f32[2048]{0:T(1024)S(1)} %copy-done.11, ...), kind=kOutput, calls=%fused_computation.107 | convolution fusion | flops 9674684416 | bytes 29918208 | tf_op jit(solution)/shard_map/dot_general | solution.py:14
  297.9 33.7 %convert_reduce_fusion = (f32[3072]{0:T(1024)}, bf16[2048,3072]{1,0:T(8,128)(2,1)}) fusion(f32[2048,3072]{1,0:T(8,128)} %get-tuple-element.245, bf16[2048,768]{0,1:T(8,128)(2,1)} %get-tuple-element.241, bf16[3072,768]{1,0:T(8,128)(2,1)} %all-gather.11.cloned.1.call-done, f32[2048,3072]{1,0:T(8,128)} %get-tuple-element.261, f32[3072]{0:T(1024)S(1)} %copy-done.25), kind=kOutput, calls=%fused_computation.38 | convolution fusion | flops 9770628096 | bytes 70803456 | tf_op jit(solution)/shard_map/dot_general | solution.py:24
  331.5 21.1 %multiply_reduce_fusion.1 = (f32[768]{0:T(1024)}, f32[2048]{0:T(1024)S(1)}, f32[2048]{0:T(1024)S(1)}, f32[768]{0:T(1024)}, f32[2048,768]{0,1:T(8,128)S(1)}) fusion(f32[2048,768]{0,1:T(8,128)} %copy-done.1, f32[2048]{0:T(1024)S(1)} %copy-done.11, f32[2048]{0:T(1024)S(1)} %copy-done.8, f32[768]{0:T(1024)S(1)} %copy-done.14, ...), kind=kOutput, calls=%fused_computation.70 | convolution fusion | flops 9691981824 | bytes 39399424 | tf_op jit(solution)/shard_map/dot_general | solution.py:24
  364.8 7.2 convolution_convert_fusion
  372.0 185.1 %while.23 = (s32[]{:T(128)}, bf16[4,512,2304]{2,1,0:T(8,128)(2,1)}, bf16[4,512,768]{1,2,0:T(8,128)(2,1)}, s32[4,512]{1,0:T(4,128)}, bf16[4,512,768]{1,2,0:T(8,12...) while((s32[]{:T(128)}, bf16[4,512,2304]{2,1,0:T(8,128)(2,1)}, ...), condition=%wide.region_14.15_spmd, body=%wide.region_12.14_spmd.sunk | while | flops 2069751808 | bytes 163232432 | solution.py:242
  386.3 11.1 %multiply_reduce_fusion.7 = (f32[12,512]{1,0:T(8,128)S(1)}, f32[12,512,512]{1,2,0:T(8,128)}) fusion(f32[12,512,512]{1,2,0:T(8,128)} %fusion.115, f32[12,512]{1,0:T(8,128)S(1)} %dynamic-slice_bitcast_fusion.2, pred[512,512]{0,1:T(8,128)(4,1)S(1)} %broadcast_compare_fusion.5, bf16[512,12,64]{0,2,1:T(8,128)(2,1)S(1)} %bitcast.129, ...), kind=kOutput, calls=%fused_computation.17.clone.1 | convolution fusion | flops 418375680 | bytes 27049984 | tf_op jit(solution)/shard_map/while/body/eval_jaxpr/qhd,khd->hqk/dot_general | solution.py:125
  399.2 7.0 multiply_convert_fusion.7
  432.8 11.0 %multiply_reduce_fusion.7 = (f32[12,512]{1,0:T(8,128)S(1)}, f32[12,512,512]{1,2,0:T(8,128)}) fusion(f32[12,512,512]{1,2,0:T(8,128)} %fusion.115, f32[12,512]{1,0:T(8,128)S(1)} %dynamic-slice_bitcast_fusion.2, pred[512,512]{0,1:T(8,128)(4,1)S(1)} %broadcast_compare_fusion.5, bf16[512,12,64]{0,2,1:T(8,128)(2,1)S(1)} %bitcast.129, ...), kind=kOutput, calls=%fused_computation.17.clone.1 | convolution fusion | flops 418375680 | bytes 27049984 | tf_op jit(solution)/shard_map/while/body/eval_jaxpr/qhd,khd->hqk/dot_general | solution.py:125
  479.1 11.0 %multiply_reduce_fusion.7 = (f32[12,512]{1,0:T(8,128)S(1)}, f32[12,512,512]{1,2,0:T(8,128)}) fusion(f32[12,512,512]{1,2,0:T(8,128)} %fusion.115, f32[12,512]{1,0:T(8,128)S(1)} %dynamic-slice_bitcast_fusion.2, pred[512,512]{0,1:T(8,128)(4,1)S(1)} %broadcast_compare_fusion.5, bf16[512,12,64]{0,2,1:T(8,128)(2,1)S(1)} %bitcast.129, ...), kind=kOutput, calls=%fused_computation.17.clone.1 | convolution fusion | flops 418375680 | bytes 27049984 | tf_op jit(solution)/shard_map/while/body/eval_jaxpr/qhd,khd->hqk/dot_general | solution.py:125
  525.2 11.0 %multiply_reduce_fusion.7 = (f32[12,512]{1,0:T(8,128)S(1)}, f32[12,512,512]{1,2,0:T(8,128)}) fusion(f32[12,512,512]{1,2,0:T(8,128)} %fusion.115, f32[12,512]{1,0:T(8,128)S(1)} %dynamic-slice_bitcast_fusion.2, pred[512,512]{0,1:T(8,128)(4,1)S(1)} %broadcast_compare_fusion.5, bf16[512,12,64]{0,2,1:T(8,128)(2,1)S(1)} %bitcast.129, ...), kind=kOutput, calls=%fused_computation.17.clone.1 | convolution fusion | flops 418375680 | bytes 27049984 | tf_op jit(solution)/shard_map/while/body/eval_jaxpr/qhd,khd->hqk/dot_general | solution.py:125
  557.1 13.2 %convolution_bitcast_fusion = f32[768,2304]{0,1:T(8,128)} fusion(bf16[2048,2304]{1,0:T(8,128)(2,1)} %bitcast.142, bf16[2048,768]{1,0:T(8,128)(2,1)} %param.19), kind=kOutput, calls=%fused_computation.84 | convolution fusion | flops 7247757312 | bytes 19660800 | tf_op jit(solution)/shard_map/dot_general | solution.py:18
  570.2 8.0 copy.97
  580.1 15.3 %fusion.46 = f32[3072,768]{1,0:T(8,128)} fusion(bf16[2048,3072]{1,0:T(8,128)(2,1)} %get-tuple-element.244, bf16[2048,768]{0,1:T(8,128)(2,1)S(1)} %copy-done.6), kind=kOutput, calls=%fused_computation.110 | convolution fusion | flops 9663676416 | bytes 25165824 | tf_op jit(solution)/shard_map/dot_general | solution.py:18
  596.1 17.7 %fusion.35 = f32[768,3072]{1,0:T(8,128)} fusion(bf16[2048,3072]{1,0:T(8,128)(2,1)} %get-tuple-element.266, f32[2048,768]{0,1:T(8,128)} %copy-done.1, f32[768]{0:T(1024)S(1)} %copy-done.21, f32[768]{0:T(1024)S(1)} %copy-done.15, f32[2048]{0:T(1024)S(1)} %copy-done.12, f32[2048]{0:T(1024)S(1)} %copy-done.9), kind=kOutput, calls=%fused_computation.103 | convolution fusion | flops 9671540736 | bytes 28334080 | tf_op jit(solution)/shard_map/dot_general | solution.py:18
  618.0 42.6 %all-reduce.16 = (f32[1536]{0:T(1024)S(1)}, f32[768]{0:T(1024)S(1)}, f32[768]{0:T(1024)S(1)}, f32[768]{0:T(1024)S(1)}, f32[3072]{0:T(1024)S(1)}, /*index=5*/f32[...) all-reduce(f32[1536]{0:T(1024)S(1)} %pad_maximum_fusion.1, ...), channel_id=3, replica_groups=mesh['dp'=16,'inner'=2] {'dp','inner'}, use_global_device_ids=true, to_apply=%region_18.19.clone | all-reduce | flops 9216 | bytes 73728
  664.1 13.7 %convolution_add_fusion.1 = f32[2048,768]{0,1:T(8,128)} fusion(f32[2048,768]{0,1:T(8,128)} %copy-done.4, bf16[2048,2304]{1,0:T(8,128)(2,1)} %bitcast.144, bf16[768,2304]{1,0:T(8,128)(2,1)} %all-gather.5.cloned.1.call-done), kind=kOutput, calls=%fused_computation.89 | convolution fusion | flops 7249330176 | bytes 25559040 | tf_op jit(solution)/shard_map/dot_general | solution.py:24
  688.5 8.2 reduce-scatter.13.cloned.1.call-done
  696.7 141.3 %reduce-scatter.11.cloned.1.call-done = f32[96,768]{1,0:T(8,128)} async-done(((f32[3072,768]{1,0:T(8,128)}), f32[96,768]{1,0:T(8,128)}) %reduce-scatter.11.cloned.1.call-update) | async-done | bytes 294928 | tf_op jit(solution)/shard_map/reduce_scatter | solution.py:71
  838.0 142.2 %reduce-scatter.9.cloned.1.call-done = f32[24,3072]{1,0:T(8,128)} async-done(((f32[768,3072]{1,0:T(8,128)}), f32[24,3072]{1,0:T(8,128)}) %reduce-scatter.9.cloned.1.call-update) | async-done | bytes 294928 | tf_op jit(solution)/shard_map/reduce_scatter | solution.py:69
  (274 shorter events, 286.4 us)
Async XLA Ops:
  7.2 60.5 %copy-start.5 = (bf16[2048,768]{1,0:T(8,128)(2,1)S(1)}, bf16[2048,768]{1,0:T(8,128)(2,1)}, u32[]{:S(2)}) copy-start(bf16[2048,768]{1,0:T(8,128)(2,1)} %param.33) | copy-start | bytes 9437188
  7.2 66.7 %all-gather.5.cloned.1.call-start = ((), (), s32[]{:S(2)}) async-start(), calls=%async_computation.4 | async-start | bytes 3649536 | tf_op jit(solution)/shard_map/all_gather | solution.py:47
  7.9 148.0 %all-gather.7.cloned.1.call-start = ((), (), s32[]{:S(2)}) async-start(), calls=%async_computation.5 | async-start | bytes 1216512 | tf_op jit(solution)/shard_map/all_gather | solution.py:49
  8.7 186.8 %all-gather.9.cloned.1.call-start = ((), (), s32[]{:S(2)}) async-start(), calls=%async_computation.6 | async-start | bytes 4866048 | tf_op jit(solution)/shard_map/all_gather | solution.py:58
  9.4 256.2 %all-gather.11.cloned.1.call-start = ((), (), s32[]{:S(2)}) async-start(), calls=%async_computation.7 | async-start | bytes 4866048 | tf_op jit(solution)/shard_map/all_gather | solution.py:60
  10.0 678.5 %reduce-scatter.7.cloned.1.call-start = ((), (), s32[]{:S(2)}) async-start(), calls=%async_computation.8 | async-start | bytes 2433024 | tf_op jit(solution)/shard_map/reduce_scatter | solution.py:82
  100.5 55.5 %copy-start.28 = (f32[768]{0:T(1024)S(1)}, f32[768]{0:T(1024)}, u32[]{:S(2)}) copy-start(f32[768]{0:T(1024)} %convert_element_type.110) | copy-start | bytes 9220
  163.3 32.1 %copy-start.25 = (f32[3072]{0:T(1024)S(1)}, f32[3072]{0:T(1024)}, u32[]{:S(2)}) copy-start(f32[3072]{0:T(1024)} %convert_element_type.114) | copy-start | bytes 36868
  195.5 70.2 %copy-start.8 = (f32[2048]{0:T(1024)S(1)}, f32[2048]{0:T(1024)}, u32[]{:S(2)}) copy-start(f32[2048]{0:T(1024)} %copy-done.7) | copy-start | bytes 24580
  195.5 70.2 %copy-start.11 = (f32[2048]{0:T(1024)S(1)}, f32[2048]{0:T(1024)}, u32[]{:S(2)}) copy-start(f32[2048]{0:T(1024)} %copy-done.10) | copy-start | bytes 24580
  195.5 70.2 %copy-start.14 = (f32[768]{0:T(1024)S(1)}, f32[768]{0:T(1024)}, u32[]{:S(2)}) copy-start(f32[768]{0:T(1024)} %convert_element_type.111) | copy-start | bytes 9220
  195.5 70.2 %copy-start.20 = (f32[768]{0:T(1024)S(1)}, f32[768]{0:T(1024)}, u32[]{:S(2)}) copy-start(f32[768]{0:T(1024)} %convert_element_type.112) | copy-start | bytes 9220
  195.5 70.2 %copy-start.27 = (f32[768]{0:T(1024)S(1)}, f32[768]{0:T(1024)}, u32[]{:S(2)}) copy-start(f32[768]{0:T(1024)} %convert_element_type.116) | copy-start | bytes 9220
  265.7 21.6 %copy-start.2 = (bf16[2048,768]{0,1:T(8,128)(2,1)S(1)}, bf16[2048,768]{0,1:T(8,128)(2,1)}, u32[]{:S(2)}) copy-start(bf16[2048,768]{0,1:T(8,128)(2,1)} %copy.79) | copy-start | bytes 9437188
  364.6 332.1 %reduce-scatter.13.cloned.1.call-start = ((), (), s32[]{:S(2)}) async-start(), calls=%async_computation.11 | async-start | bytes 7299072
  386.2 11.1 %slice-start = ((s8[12582912]{0:T(1024)(128)(4,1)}), s8[4194304]{0:T(1024)(128)(4,1)S(1)}, s32[]{:S(2)}) async-start(s8[12582912]{0:T(1024)(128)(4,1)} %bitcast.122), calls=%async_computation.12 | async-start | bytes 8388608 | tf_op jit(solution)/shard_map/while
  386.3 11.1 %slice-start.1 = ((s8[12582912]{0:T(1024)(128)(4,1)}), s8[4194304]{0:T(1024)(128)(4,1)S(1)}, s32[]{:S(2)}) async-start(s8[12582912]{0:T(1024)(128)(4,1)} %bitcast.122), calls=%async_computation.13 | async-start | bytes 8388608 | tf_op jit(solution)/shard_map/while
  386.3 12.9 %slice-start.2 = ((s8[12582912]{0:T(1024)(128)(4,1)}), s8[4194304]{0:T(1024)(128)(4,1)S(1)}, s32[]{:S(2)}) async-start(s8[12582912]{0:T(1024)(128)(4,1)} %bitcast.122), calls=%async_computation.14 | async-start | bytes 8388608 | tf_op jit(solution)/shard_map/while
  432.8 11.0 %slice-start = ((s8[12582912]{0:T(1024)(128)(4,1)}), s8[4194304]{0:T(1024)(128)(4,1)S(1)}, s32[]{:S(2)}) async-start(s8[12582912]{0:T(1024)(128)(4,1)} %bitcast.122), calls=%async_computation.12 | async-start | bytes 8388608 | tf_op jit(solution)/shard_map/while
  432.8 12.7 %slice-start.2 = ((s8[12582912]{0:T(1024)(128)(4,1)}), s8[4194304]{0:T(1024)(128)(4,1)S(1)}, s32[]{:S(2)}) async-start(s8[12582912]{0:T(1024)(128)(4,1)} %bitcast.122), calls=%async_computation.14 | async-start | bytes 8388608 | tf_op jit(solution)/shard_map/while
  479.1 12.6 %slice-start.2 = ((s8[12582912]{0:T(1024)(128)(4,1)}), s8[4194304]{0:T(1024)(128)(4,1)S(1)}, s32[]{:S(2)}) async-start(s8[12582912]{0:T(1024)(128)(4,1)} %bitcast.122), calls=%async_computation.14 | async-start | bytes 8388608 | tf_op jit(solution)/shard_map/while
  525.2 12.6 %slice-start.2 = ((s8[12582912]{0:T(1024)(128)(4,1)}), s8[4194304]{0:T(1024)(128)(4,1)S(1)}, s32[]{:S(2)}) async-start(s8[12582912]{0:T(1024)(128)(4,1)} %bitcast.122), calls=%async_computation.14 | async-start | bytes 8388608 | tf_op jit(solution)/shard_map/while
  578.2 259.8 %reduce-scatter.11.cloned.1.call-start = ((), (), s32[]{:S(2)}) async-start(), calls=%async_computation.10 | async-start | bytes 9732096 | tf_op jit(solution)/shard_map/reduce_scatter | solution.py:71
  595.4 384.8 %reduce-scatter.9.cloned.1.call-start = ((), (), s32[]{:S(2)}) async-start(), calls=%async_computation.9 | async-start | bytes 9732096 | tf_op jit(solution)/shard_map/reduce_scatter | solution.py:69
  (29 other events, 136.8 us)
Sparse Core Ops, SparseCore 0:
  10.9 62.9 all-gather.4
  76.8 53.0 all-gather.6
  132.8 62.6 all-gather.8
  198.2 62.4 all-gather.10
  364.7 97.7 reduce-scatter.6
  578.4 118.2 reduce-scatter.12
  703.1 134.8 reduce-scatter.10
  845.5 134.7 reduce-scatter.8
where the time goes:
time: 999 us; the launch traced here: 988 us
  matrix products  349 us (35%)
  waiting for transfers between devices  326 us (33%)
  local copies, waits for them, and re-layouts  136 us (14%)
  blocking collectives  85.2 us (9%)
  other arithmetic  74.6 us (7%)
  between operations  15 us (2%)
    reduce_scatter x1, waiting for transfers between devices, reduce_feed(): lax.psum_scatter(grads[0], ('dp', 'inner'), scatter_dimension=0, tiled=True)  142 us
    reduce_scatter x1, waiting for transfers between devices, reduce_feed(): lax.psum_scatter(grads[2], ('dp', 'inner'), scatter_dimension=0, tiled=True)  141 us
    dot_general x4, matrix products, product(): return jnp.dot(left, right, preferred_element_type=jnp.float32)  105 us
    unnamed x2, blocking collectives  85.2 us
    dot_general x4, matrix products, product_transposed(): lax.dot_general(left, right, (((1,), (1,)), ((), ())), preferred_element_...  75.7 us
    dot_general x4, matrix products, product_over_rows(): lax.dot_general(left, right, (((0,), (0,)), ((), ())), preferred_element_...  50.3 us
    unnamed x95, local copies, waits for them, and re-layouts  45.2 us
    dot_general x4, matrix products, attend_back(): jnp.einsum('qhd,khd->hqk', grad_heads, split_heads(values), preferred_ele...  44 us
  transfers between devices with their start and end apart: 8, of which 5 were waited for; matrix products, arithmetic and copies ran while one was open for 46% of the time, Pallas kernels for 0%

commit v1 on v0

v1 whole, which is shorter than its diff:
```python
import functools

import jax
import jax.numpy as jnp
from jax import lax
from jax.experimental import pallas as pl
from jax.experimental.pallas import tpu as pltpu
from jax.sharding import PartitionSpec as P

HEAD_DIM = 64
BLOCK = 128
EPSILON = 1e-06
NEG_FILL = -1e30
F32 = jnp.float32
BF16 = jnp.bfloat16
VMEM_LIMIT = 60 << 20


def dot(left, right, dims):
    return lax.dot_general(left, right, ((dims[:1], dims[1:]), ((), ())), preferred_element_type=F32)


def dot_nn(left, right):
    return dot(left, right, (1, 0))


def dot_nt(left, right):
    return dot(left, right, (1, 1))


def dot_tn(left, right):
    return dot(left, right, (0, 0))


def windows(length):
    return [
        (max(0, start - BLOCK), min(length, start + 2 * BLOCK))
        for start in range(0, length, BLOCK)
    ]


def mask_offsets(length):
    offsets, total = [], 0
    for low, high in windows(length):
        offsets.append(total)
        total += high - low
    return offsets, total


def fill_masks(mask_ref, seq, segment_row):
    length = segment_row.shape[1]
    columns = jnp.transpose(jnp.broadcast_to(segment_row, (BLOCK, length)))
    offsets, _ = mask_offsets(length)
    for block, (low, high) in enumerate(windows(length)):
        rows = jnp.broadcast_to(
            segment_row[:, block * BLOCK : (block + 1) * BLOCK], (high - low, BLOCK)
        )
        mask_ref[seq, pl.ds(offsets[block], high - low), :] = jnp.where(
            columns[low:high] == rows, 0.0, NEG_FILL
        )


def stacked(pair):
    lane = lax.broadcasted_iota(jnp.int32, pair.shape, 1)
    zero = jnp.zeros_like(pair)
    return jnp.concatenate(
        [jnp.where(lane < HEAD_DIM, pair, zero), jnp.where(lane < HEAD_DIM, zero, pair)], axis=0
    )


def unstacked_t(joined):
    row = lax.broadcasted_iota(jnp.int32, (2 * HEAD_DIM, BLOCK), 0)
    return jnp.transpose(jnp.where(row < HEAD_DIM, joined[:, :BLOCK], joined[:, BLOCK:]))


def twice(mask):
    return jnp.concatenate([mask, mask], axis=1)


def normalize(summed):
    center = summed - jnp.mean(summed, axis=-1, keepdims=True)
    inverse = lax.rsqrt(jnp.mean(center * center, axis=-1, keepdims=True) + EPSILON)
    return (center * inverse, inverse)


def normalize_back(grad_normed, normed, inverse):
    mean_grad = jnp.mean(grad_normed, axis=-1, keepdims=True)
    mean_cross = jnp.mean(grad_normed * normed, axis=-1, keepdims=True)
    return inverse * (grad_normed - mean_grad - normed * mean_cross)


def column_sum(rows):
    return jnp.sum(rows, axis=0, keepdims=True)


def gelu_parts(pre):
    size = jnp.abs(pre)
    t = 1.0 / (1.0 + 0.3275911 * 0.7071067811865476 * size)
    bell = jnp.exp(-0.5 * pre * pre)
    series = t * (
        0.127414796
        + t * (-0.142248368 + t * (0.7107068705 + t * (-0.7265760135 + t * 0.5307027145)))
    )
    tail = series * bell
    cdf = jnp.where(pre >= 0.0, 1.0 - tail, tail)
    return (pre * cdf, cdf + pre * (bell * 0.3989422804014327))


def attention_kernel(
    tokens_ref, segment_ref, wqkv_ref, wout_ref, bqkv_ref, bout_ref,
    qkv_ref, context_ref, lse_ref, normed_ref, inverse_ref, mask_ref,
):
    length, width = tokens_ref.shape
    fill_masks(mask_ref, 0, segment_ref[0])
    offsets, _ = mask_offsets(length)
    for part in range(3):
        cols = slice(part * width, (part + 1) * width)
        joined = dot_nn(tokens_ref[...], wqkv_ref[:, cols]) + bqkv_ref[:, cols]
        if part == 0:
            joined = joined * HEAD_DIM ** (-0.5)
        qkv_ref[:, cols] = joined.astype(BF16)

    def one_pair(pair, _):
        def cols(part):
            return pl.ds(pl.multiple_of(part * width + pair * BLOCK, BLOCK), BLOCK)

        for block, (low, high) in enumerate(windows(length)):
            here = slice(block * BLOCK, (block + 1) * BLOCK)
            query = stacked(qkv_ref[here, cols(0)])
            scores = dot_nt(qkv_ref[low:high, cols(1)], query)
            scores = scores + twice(mask_ref[0, pl.ds(offsets[block], high - low), :])
            maxima = jnp.max(scores, axis=0, keepdims=True)
            exponent = jnp.exp(scores - maxima)
            totals = jnp.sum(exponent, axis=0, keepdims=True)
            context = dot_tn(qkv_ref[low:high, cols(2)], exponent.astype(BF16)) * (1.0 / totals)
            context_ref[here, cols(0)] = unstacked_t(context).astype(BF16)
            lse_ref[0, pl.ds(pair * (length // BLOCK) + block, 1), :] = maxima + jnp.log(totals)
        return 0

    lax.fori_loop(0, width // BLOCK, one_pair, 0)
    branch = dot_nn(context_ref[...], wout_ref[...]) + bout_ref[...]
    normed, inverse = normalize(tokens_ref[...].astype(F32) + branch)
    normed_ref[...] = normed
    inverse_ref[...] = jnp.broadcast_to(inverse, inverse_ref.shape)


def whole(shape):
    return pl.BlockSpec(shape, lambda *_: (0,) * len(shape), pipeline_mode=pl.Buffered(1))


def attention_forward(tokens, segments, wqkv, wout, bqkv, bout):
    count, length = segments.shape[0], segments.shape[2]
    width = tokens.shape[1]
    rows = pl.BlockSpec((length, width), lambda i: (i, 0))
    lse_rows = (width // BLOCK) * (length // BLOCK)
    return pl.pallas_call(
        attention_kernel,
        grid=(count,),
        in_specs=[
            rows,
            pl.BlockSpec((1, 1, length), lambda i: (i, 0, 0)),
            whole(wqkv.shape),
            whole(wout.shape),
            whole(bqkv.shape),
            whole(bout.shape),
        ],
        out_specs=[
            pl.BlockSpec((length, 3 * width), lambda i: (i, 0)),
            rows,
            pl.BlockSpec((1, lse_rows, 2 * BLOCK), lambda i: (i, 0, 0)),
            rows,
            pl.BlockSpec((length, BLOCK), lambda i: (i, 0)),
        ],
        out_shape=[
            jax.ShapeDtypeStruct((count * length, 3 * width), BF16),
            jax.ShapeDtypeStruct((count * length, width), BF16),
            jax.ShapeDtypeStruct((count, lse_rows, 2 * BLOCK), F32),
            jax.ShapeDtypeStruct((count * length, width), F32),
            jax.ShapeDtypeStruct((count * length, BLOCK), F32),
        ],
        scratch_shapes=[pltpu.VMEM((1, mask_offsets(length)[1], BLOCK), F32)],
        compiler_params=pltpu.CompilerParams(vmem_limit_bytes=VMEM_LIMIT),
        name="attention_forward",
    )(tokens, segments, wqkv, wout, bqkv, bout)


def feed_kernel(
    normed_ref, cot_ref, win_ref, wfin_ref, vec_ref, bin_ref,
    out_ref, act_ref, slope_ref, gsum_ref, gffn_ref, low_ref, gvec_ref,
    hidden_ref,
):
    hidden = normed_ref[...] * vec_ref[0:1] + vec_ref[1:2]
    hidden_ref[...] = hidden
    low_ref[...] = hidden.astype(BF16)
    width = win_ref.shape[0]

    def one_chunk(chunk, _):
        cols = pl.ds(pl.multiple_of(chunk * width, width), width)
        pre = dot_nn(low_ref[...], win_ref[:, cols]) + bin_ref[:, cols]
        active, slope = gelu_parts(pre)
        act_ref[:, cols] = active.astype(BF16)
        slope_ref[:, cols] = slope.astype(BF16)
        return 0

    lax.fori_loop(0, win_ref.shape[1] // width, one_chunk, 0)
    branch = dot_nn(act_ref[...], wfin_ref[...]) + vec_ref[2:3]
    normed, inverse = normalize(hidden_ref[...] + branch)
    gain = vec_ref[3:4]
    out_ref[...] = (normed * gain + vec_ref[4:5]).astype(BF16)
    cot = cot_ref[...].astype(F32)
    gsum = normalize_back(cot * gain, normed, inverse)
    gsum_ref[...] = gsum
    gffn = gsum.astype(BF16)
    gffn_ref[...] = gffn

    @pl.when(pl.program_id(0) == 0)
    def _():
        gvec_ref[...] = jnp.zeros_like(gvec_ref)

    gvec_ref[0:1] += column_sum(cot * normed)
    gvec_ref[1:2] += column_sum(cot)
    gvec_ref[2:3] += column_sum(gffn.astype(F32))


def feed_forward(normed, cotangent, win, wfin, vectors, bin_, tile):
    tokens, width = normed.shape
    hidden = win.shape[1]
    rows = pl.BlockSpec((tile, width), lambda i: (i, 0))
    wide = pl.BlockSpec((tile, hidden), lambda i: (i, 0))
    return pl.pallas_call(
        feed_kernel,
        grid=(tokens // tile,),
        in_specs=[rows, rows, whole(win.shape), whole(wfin.shape), whole(vectors.shape), whole(bin_.shape)],
        out_specs=[rows, wide, wide, rows, rows, rows, pl.BlockSpec((8, width), lambda i: (0, 0))],
        out_shape=[
            jax.ShapeDtypeStruct((tokens, width), BF16),
            jax.ShapeDtypeStruct((tokens, hidden), BF16),
            jax.ShapeDtypeStruct((tokens, hidden), BF16),
            jax.ShapeDtypeStruct((tokens, width), F32),
            jax.ShapeDtypeStruct((tokens, width), BF16),
            jax.ShapeDtypeStruct((tokens, width), BF16),
            jax.ShapeDtypeStruct((8, width), F32),
        ],
        scratch_shapes=[pltpu.VMEM((tile, width), F32)],
        compiler_params=pltpu.CompilerParams(vmem_limit_bytes=VMEM_LIMIT),
        name="feed_forward",
    )(normed, cotangent, win, wfin, vectors, bin_)


def feed_back_kernel(
    gffn_ref, low_ref, gsum_hbm, act_ref, slope_ref, win_ref, wfin_ref,
    dwin_ref, dwfin_ref, gbin_ref, ghid_hbm,
    low_t_ref, acc_ref, gpre_ref, sem,
):
    step = pl.program_id(0)
    tokens = gffn_ref.shape[0]
    tile = 512

    @pl.when(step == 0)
    def _():
        copy = pltpu.make_async_copy(gsum_hbm, acc_ref, sem)
        copy.start()
        low_t_ref[...] = jnp.transpose(low_ref[...])
        copy.wait()

    gbin_ref[...] = jnp.zeros_like(gbin_ref)
    for start in range(0, tokens, tile):
        here = slice(start, start + tile)
        gpre = (dot_nt(gffn_ref[here], wfin_ref[...]) * slope_ref[here].astype(F32)).astype(BF16)
        gpre_ref[here] = gpre
        gbin_ref[0:1] += column_sum(gpre.astype(F32))
        acc_ref[here] += dot_nt(gpre, win_ref[...])
    dwin_ref[...] = dot_nn(low_t_ref[...], gpre_ref[...]).astype(BF16)
    dwfin_ref[...] = dot_tn(act_ref[...], gffn_ref[...]).astype(BF16)

    @pl.when(step == pl.num_programs(0) - 1)
    def _():
        pltpu.sync_copy(acc_ref, ghid_hbm)


def feed_backward(gffn, low, gsum, act, slope, win, wfin, chunk):
    tokens, width = low.shape
    hidden = win.shape[1]
    any_ = pl.BlockSpec(memory_space=pl.ANY)
    return pl.pallas_call(
        feed_back_kernel,
        grid=(hidden // chunk,),
        in_specs=[
            whole(gffn.shape), whole(low.shape), any_,
            pl.BlockSpec((tokens, chunk), lambda i: (0, i)),
            pl.BlockSpec((tokens, chunk), lambda i: (0, i)),
            pl.BlockSpec((width, chunk), lambda i: (0, i)),
            pl.BlockSpec((chunk, width), lambda i: (i, 0)),
        ],
        out_specs=[
            pl.BlockSpec((width, chunk), lambda i: (0, i)),
            pl.BlockSpec((chunk, width), lambda i: (i, 0)),
            pl.BlockSpec((8, chunk), lambda i: (0, i)),
            any_,
        ],
        out_shape=[
            jax.ShapeDtypeStruct((width, hidden), BF16),
            jax.ShapeDtypeStruct((hidden, width), BF16),
            jax.ShapeDtypeStruct((8, hidden), F32),
            jax.ShapeDtypeStruct((tokens, width), F32),
        ],
        scratch_shapes=[
            pltpu.VMEM((width, tokens), BF16),
            pltpu.VMEM((tokens, width), F32),
            pltpu.VMEM((tokens, chunk), BF16),
            pltpu.SemaphoreType.DMA,
        ],
        compiler_params=pltpu.CompilerParams(vmem_limit_bytes=VMEM_LIMIT),
        name="feed_backward",
    )(gffn, low, gsum, act, slope, win, wfin)


def project_back_kernel(
    ghid_ref, normed_ref, inverse_ref, context_ref, wout_ref, gain_ref,
    gsum_ref, gcon_ref, dwout_ref, gvec_ref, acc_ref,
):
    step = pl.program_id(0)

    @pl.when(step == 0)
    def _():
        gvec_ref[...] = jnp.zeros_like(gvec_ref)
        acc_ref[...] = jnp.zeros_like(acc_ref)

    ghid = ghid_ref[...]
    normed = normed_ref[...]
    gvec_ref[0:1] += column_sum(ghid * normed)
    gvec_ref[1:2] += column_sum(ghid)
    gsum = normalize_back(ghid * gain_ref[...], normed, inverse_ref[:, 0:1])
    gsum_ref[...] = gsum
    gattn = gsum.astype(BF16)
    gvec_ref[2:3] += column_sum(gattn.astype(F32))
    gcon_ref[...] = dot_nt(gattn, wout_ref[...]).astype(BF16)
    acc_ref[...] += dot_tn(context_ref[...], gattn)

    @pl.when(step == pl.num_programs(0) - 1)
    def _():
        dwout_ref[...] = acc_ref[...].astype(BF16)


def project_backward(ghid, normed, inverse, context, wout, gain, tile):
    tokens, width = ghid.shape
    rows = pl.BlockSpec((tile, width), lambda i: (i, 0))
    return pl.pallas_call(
        project_back_kernel,
        grid=(tokens // tile,),
        in_specs=[
            rows, rows, pl.BlockSpec((tile, BLOCK), lambda i: (i, 0)), rows,
            whole(wout.shape), whole(gain.shape),
        ],
        out_specs=[rows, rows, whole((width, width)), pl.BlockSpec((8, width), lambda i: (0, 0))],
        out_shape=[
            jax.ShapeDtypeStruct((tokens, width), F32),
            jax.ShapeDtypeStruct((tokens, width), BF16),
            jax.ShapeDtypeStruct((width, width), BF16),
            jax.ShapeDtypeStruct((8, width), F32),
        ],
        scratch_shapes=[pltpu.VMEM((width, width), F32)],
        compiler_params=pltpu.CompilerParams(vmem_limit_bytes=VMEM_LIMIT),
        name="project_backward",
    )(ghid, normed, inverse, context, wout, gain)


def attention_back_kernel(
    q_ref, k_ref, v_ref, gcon_ref, lse_ref, segment_ref, tokens_ref, wq_ref, wk_ref, wv_ref, gsum_hbm,
    dw_ref, gvec_ref, gtok_hbm,
    tokens_t_ref, acc_ref, mask_ref, grad_ref, dk_ref, dv_ref, sem,
):
    pair = pl.program_id(0)
    count, length = segment_ref.shape[0], segment_ref.shape[2]
    blocks = length // BLOCK
    offsets, _ = mask_offsets(length)
    tile = 512

    @pl.when(pair == 0)
    def _():
        copy = pltpu.make_async_copy(gsum_hbm, acc_ref, sem)
        copy.start()
        tokens_t_ref[...] = jnp.transpose(tokens_ref[...])
        for seq in range(count):
            fill_masks(mask_ref, seq, segment_ref[seq])
        copy.wait()

    def one_seq(seq, _):
        base = pl.multiple_of(seq * length, length)
        dk_ref[...] = jnp.zeros_like(dk_ref)
        dv_ref[...] = jnp.zeros_like(dv_ref)
        for block, (low, high) in enumerate(windows(length)):
            here = pl.ds(base + block * BLOCK, BLOCK)
            reach = pl.ds(base + low, high - low)
            query = stacked(q_ref[here])
            grad = stacked(gcon_ref[here])
            keys = k_ref[reach]
            scores = dot_nt(keys, query) + twice(mask_ref[seq, pl.ds(offsets[block], high - low), :])
            probs = jnp.exp(scores - lse_ref[seq, pl.ds(pair * blocks + block, 1), :])
            gprobs = dot_nt(v_ref[reach], grad)
            dots = jnp.sum(probs * gprobs, axis=0, keepdims=True)
            gscores = (probs * (gprobs - dots)).astype(BF16)
            dv_ref[low:high] += dot_nn(probs.astype(BF16), grad)
            dk_ref[low:high] += dot_nn(gscores, query)
            gquery = unstacked_t(dot_tn(keys, gscores)) * HEAD_DIM ** (-0.5)
            grad_ref[here, 0:BLOCK] = gquery.astype(BF16)
        rows = pl.ds(base, length)
        grad_ref[rows, BLOCK : 2 * BLOCK] = dk_ref[...].astype(BF16)
        grad_ref[rows, 2 * BLOCK :] = dv_ref[...].astype(BF16)
        return 0

    lax.fori_loop(0, count, one_seq, 0)
    gvec_ref[...] = jnp.zeros_like(gvec_ref)
    gvec_ref[0:1] = column_sum(grad_ref[:, :BLOCK].astype(F32))
    gvec_ref[1:2] = column_sum(grad_ref[:, 2 * BLOCK :].astype(F32))
    weights = jnp.concatenate([wq_ref[...], wk_ref[...], wv_ref[...]], axis=1)
    for start in range(0, acc_ref.shape[0], tile):
        here = slice(start, start + tile)
        acc_ref[here] += dot_nt(grad_ref[here], weights)
    dw = dot_nn(tokens_t_ref[...], grad_ref[...]).astype(BF16)
    for part in range(3):
        dw_ref[part] = dw[:, part * BLOCK : (part + 1) * BLOCK]

    @pl.when(pair == pl.num_programs(0) - 1)
    def _():
        pltpu.sync_copy(acc_ref, gtok_hbm)


def attention_backward(qkv, gcon, lse, segments, tokens, wqkv, gsum):
    count, length = segments.shape[0], segments.shape[2]
    total, width = tokens.shape
    pairs = width // BLOCK
    any_ = pl.BlockSpec(memory_space=pl.ANY)

    def part(rows, index):
        return pl.BlockSpec((rows, BLOCK), lambda i: (0, index * pairs + i))

    return pl.pallas_call(
        attention_back_kernel,
        grid=(pairs,),
        in_specs=[
            part(total, 0), part(total, 1), part(total, 2), part(total, 0),
            whole(lse.shape), whole(segments.shape), whole(tokens.shape),
            part(width, 0), part(width, 1), part(width, 2), any_,
        ],
        out_specs=[
            pl.BlockSpec((3, width, BLOCK), lambda i: (0, 0, i)),
            pl.BlockSpec((8, BLOCK), lambda i: (0, i)),
            any_,
        ],
        out_shape=[
            jax.ShapeDtypeStruct((3, width, width), BF16),
            jax.ShapeDtypeStruct((8, width), F32),
            jax.ShapeDtypeStruct((total, width), F32),
        ],
        scratch_shapes=[
            pltpu.VMEM((width, total), BF16),
            pltpu.VMEM((total, width), F32),
            pltpu.VMEM((count, mask_offsets(length)[1], BLOCK), F32),
            pltpu.VMEM((total, 3 * BLOCK), BF16),
            pltpu.VMEM((length, BLOCK), F32),
            pltpu.VMEM((length, BLOCK), F32),
            pltpu.SemaphoreType.DMA,
        ],
        compiler_params=pltpu.CompilerParams(vmem_limit_bytes=VMEM_LIMIT),
        name="attention_backward",
    )(qkv, qkv, qkv, gcon, lse, segments, tokens, wqkv, wqkv, wqkv, gsum)


def layer(
    tokens, wqkv, bqv, wout, bout, gain_one, shift_one,
    win, bin_, wfin, bfin, gain_two, shift_two, segments, cotangent,
):
    width = tokens.shape[1]
    length = segments.shape[1]
    segments = segments.reshape(segments.shape[0], 1, length)
    bqkv = jnp.concatenate([bqv[:, :width], jnp.zeros_like(bout), bqv[:, width:]], axis=1)
    qkv, context, lse, normed, inverse = attention_forward(tokens, segments, wqkv, wout, bqkv, bout)
    zero = jnp.zeros_like(bfin)
    vectors = jnp.concatenate([gain_one, shift_one, bfin, gain_two, shift_two, zero, zero, zero], axis=0)
    output, act, slope, gsum_two, gffn, low, gvec_two = feed_forward(
        normed, cotangent, win, wfin, vectors, bin_, min(512, tokens.shape[0])
    )
    dwin, dwfin, gbin, ghid = feed_backward(gffn, low, gsum_two, act, slope, win, wfin, 512)
    gsum_one, gcon, dwout, gvec_one = project_backward(
        ghid, normed, inverse, context, wout, gain_one, min(512, tokens.shape[0])
    )
    dwqkv, gvec_qv, gtok = attention_backward(qkv, gcon, lse, segments, tokens, wqkv, gsum_one)
    return (
        output, gtok, dwqkv, gvec_qv[0:2].reshape(1, -1), dwout, gvec_one[2:3], gvec_one[0:1], gvec_one[1:2],
        dwin, gbin[0:1], dwfin, gvec_two[2:3], gvec_two[0:1], gvec_two[1:2],
    )


AXES = ("dp", "inner")


def shards(
    tokens, weight_qkv, bias_qv, weight_out, bias_out, gain_one, shift_one,
    weight_in, bias_in, weight_fin, bias_fin, gain_two, shift_two, segments, cotangent,
):
    vectors = (bias_qv, bias_out, gain_one, shift_one, bias_in, bias_fin, gain_two, shift_two)
    sizes = [v.shape[0] for v in vectors]
    joined = jnp.concatenate(vectors).reshape(1, -1)
    joined = lax.all_gather(joined, AXES, axis=0, tiled=True).astype(F32)
    rows, start = [], 0
    for size in sizes:
        rows.append(joined[:, start : start + size].reshape(1, -1))
        start += size
    full = [lax.all_gather(w, AXES, axis=0, tiled=True) for w in (weight_qkv, weight_out, weight_in, weight_fin)]
    out = layer(
        tokens, full[0], rows[0], full[1], rows[1], rows[2], rows[3],
        full[2], rows[4], full[3], rows[5], rows[6], rows[7], segments, cotangent,
    )
    def scatter(grad, axis=0):
        return lax.psum_scatter(grad, AXES, scatter_dimension=axis, tiled=True).astype(F32)

    count = joined.shape[0]
    order = (3, 5, 6, 7, 9, 11, 12, 13)
    small = jnp.concatenate([out[i].reshape(count, -1) for i in order], axis=1)
    small = lax.psum_scatter(small, AXES, scatter_dimension=0, tiled=True).reshape(-1)
    parts, start = {}, 0
    for index, size in zip(order, sizes):
        parts[index] = small[start : start + size]
        start += size
    dwqkv = scatter(out[2], 1)
    dwqkv = jnp.concatenate([dwqkv[0], dwqkv[1], dwqkv[2]], axis=1)
    return (
        out[0], out[1], dwqkv, parts[3], scatter(out[4]), parts[5], parts[6], parts[7],
        scatter(out[8]), parts[9], scatter(out[10]), parts[11], parts[12], parts[13],
    )


def solution(mesh):
    row, vec = P(AXES, None), P(AXES)
    in_specs = (row, row, vec, row, vec, vec, vec, row, vec, row, vec, vec, vec, row, row)
    out_specs = (row, row, row, vec, row, vec, vec, vec, row, vec, row, vec, vec, vec)
    return jax.shard_map(shards, mesh=mesh, in_specs=in_specs, out_specs=out_specs, check_vma=False)
```

time: 999 us -> 821 us (0.82); the launches traced: 988 us -> 820 us
  matrix products: 349 us -> 0 us
  Pallas kernels: 0 us -> 249 us
  waiting for transfers between devices: 326 us -> 444 us
  local copies, waits for them, and re-layouts: 136 us -> 24.2 us
  other arithmetic: 74.6 us -> 6.02 us
    dot_general x40 -> x0, matrix products: 349 us -> none  [the longest x4 105 us: product(): return jnp.dot(left, right, preferred_element_type=jnp.float32)]
    pallas_call x0 -> x5, Pallas kernels: none -> 249 us  [the longest x1 70.6 us: attention_backward(): pl.pallas_call(attention_back_kernel, grid=(pairs,), in_specs=[part(total...]
    all_gather x4, waiting for transfers between devices: 31.4 us -> 144 us  [shards(): lax.all_gather(w, AXES, axis=0, tiled=True)]
    unnamed x9, waiting for transfers between devices: 10.8 us -> 79.5 us
    reduce_scatter x3, waiting for transfers between devices: 284 us -> 221 us  [scatter(): lax.psum_scatter(grad, AXES, scatter_dimension=axis, tiled=True).astype(F32)]
    dynamic_slice x32 -> x0, local copies, waits for them, and re-layouts: 40.9 us -> none  [shards(): lax.map(attend, (query_seqs, key_seqs, value_seqs, segments))]
    unnamed x95 -> x7, local copies, waits for them, and re-layouts: 45.2 us -> 8.77 us
    reduce_sum x10 -> x0, other arithmetic: 33.1 us -> none  [the longest x4 10.2 us: attend(): totals = jnp.sum(exponent, axis=-1, keepdims=True)]
  transfers between devices with their start and end apart: 8 -> 8, of which waited for: 5 -> 7; matrix products, arithmetic and copies ran while one was open for 46% -> 3% of each run, Pallas kernels for 0% -> 15%
where the time goes in v1:
time: 821 us; the launch traced here: 820 us
  waiting for transfers between devices  444 us (54%)
  Pallas kernels  249 us (30%)
  blocking collectives  82.3 us (10%)
  local copies, waits for them, and re-layouts  24.2 us (3%)
  between operations  14.3 us (2%)
    reduce_scatter x3, waiting for transfers between devices, scatter(): lax.psum_scatter(grad, AXES, scatter_dimension=axis, tiled=True).astype(F32)  221 us
    all_gather x4, waiting for transfers between devices, shards(): lax.all_gather(w, AXES, axis=0, tiled=True)  144 us
    unnamed x2, blocking collectives  82.3 us
    unnamed x9, waiting for transfers between devices  79.5 us
    pallas_call x1, Pallas kernels, attention_backward(): pl.pallas_call(attention_back_kernel, grid=(pairs,), in_specs=[part(total...  70.6 us
    pallas_call x1, Pallas kernels, feed_forward(): pl.pallas_call(feed_kernel, grid=(tokens // tile,), in_specs=[rows, rows,...  55.8 us
    pallas_call x1, Pallas kernels, attention_forward(): pl.pallas_call(attention_kernel, grid=(count,), in_specs=[rows, pl.BlockS...  54.1 us
    pallas_call x1, Pallas kernels, feed_backward(): pl.pallas_call(feed_back_kernel, grid=(hidden // chunk,), in_specs=[whole...  53.6 us
  transfers between devices with their start and end apart: 8, of which 7 were waited for; matrix products, arithmetic and copies ran while one was open for 3% of the time, Pallas kernels for 15%

profile of v1, /device:TPU:0, one launch (start us, length us, event | category | flops | bytes accessed | tf_op | source)
XLA Modules:
  0.0 820.1 jit_solution(1800958588300390241)
XLA Ops:
  10.0 5.4 concatenate.18
  15.7 42.2 %all-reduce = bf16[9216]{0:T(1024)(128)(2,1)S(1)} all-reduce(bf16[9216]{0:T(1024)(128)(2,1)S(1)} %dynamic-update-slice), channel_id=2, replica_groups=mesh['dp'=16,'inner'=2] {'dp','inner'}, use_global_device_ids=true, to_apply=%add | all-reduce | flops 9216 | bytes 36864
  59.5 1.3 reshape.88.segment_ref
  62.7 5.1 all-gather.8.cloned.1.call-done.wout_ref
  67.9 62.3 %all-gather.6.cloned.1.call-done.wqkv_ref.wq_ref.wk_ref.wv_ref = bf16[768,2304]{1,0:T(8,128)(2,1)} async-done(((bf16[24,2304]{1,0:T(8,128)(2,1)}), bf16[768,2304]{1,0:T(8,128)(2,1)}) %all-gather.6.cloned.1.call-update) | async-done | bytes 3538960 | tf_op jit(solution)/shard_map/all_gather | solution.py:510
  130.1 54.1 %attention_forward.1 = (bf16[2048,2304]{1,0:T(8,128)(2,1)}, bf16[2048,768]{1,0:T(8,128)(2,1)}, f32[4,24,256]{2,1,0:T(8,128)}, f32[2048,768]{1,0:T(8,128)}, f32[2048,128]{1,0:T(8,128)}) custom-call(bf16[2048,768]{1,0:T(8,128)(2,1)} %tokens_ref.3, s32[4,1,512]{2,1,0:T(1,128)} %reshape.88.segment_ref, ...), custom_call_target="tpu_custom_call" | custom-call | tf_op jit(solution)/shard_map/attention_forward/pallas_call | solution.py:156
  184.2 11.5 %all-gather.10.cloned.1.call-done.win_ref = bf16[768,3072]{1,0:T(8,128)(2,1)} async-done(((bf16[24,3072]{1,0:T(8,128)(2,1)}), bf16[768,3072]{1,0:T(8,128)(2,1)}) %all-gather.10.cloned.1.call-update) | async-done | bytes 4718608 | tf_op jit(solution)/shard_map/all_gather | solution.py:510
  195.7 65.3 %all-gather.12.cloned.1.call-done.wfin_ref = bf16[3072,768]{1,0:T(8,128)(2,1)} async-done(((bf16[96,768]{1,0:T(8,128)(2,1)}), bf16[3072,768]{1,0:T(8,128)(2,1)}) %all-gather.12.cloned.1.call-update) | async-done | bytes 4718608 | tf_op jit(solution)/shard_map/all_gather | solution.py:510
  261.0 55.8 %feed_forward.1 = (bf16[2048,768]{1,0:T(8,128)(2,1)}, bf16[2048,3072]{1,0:T(8,128)(2,1)}, bf16[2048,3072]{1,0:T(8,128)(2,1)}, f32[2048,768]{1,0:T(8,128)}, bf16[...) custom-call(f32[2048,768]{1,0:T(8,128)} %get-tuple-element.37.normed_ref, ...), custom_call_target="tpu_custom_call" | custom-call | tf_op jit(solution)/shard_map/feed_forward/pallas_call | solution.py:230
  316.8 53.6 %feed_backward.1 = (bf16[768,3072]{1,0:T(8,128)(2,1)}, bf16[3072,768]{1,0:T(8,128)(2,1)}, f32[8,3072]{1,0:T(8,128)}, f32[2048,768]{1,0:T(8,128)}) custom-call(bf16[2048,768]{1,0:T(8,128)(2,1)} %get-tuple-element.40.gffn_ref, bf16[2048,768]{1,0:T(8,128)(2,1)} %get-tuple-element.41.low_ref, f32[2048,768]{1,0:T(8,128)} %get-tuple-element.42.gsum_hbm, ...), custom_call_target="tpu_custom_call" | custom-call | tf_op jit(solution)/shard_map/feed_backward/pallas_call | solution.py:285
  370.4 14.6 %project_backward.1 = (f32[2048,768]{1,0:T(8,128)}, bf16[2048,768]{1,0:T(8,128)(2,1)}, bf16[768,768]{1,0:T(8,128)(2,1)}, f32[8,768]{1,0:T(8,128)}) custom-call(f32[2048,768]{1,0:T(8,128)} %get-tuple-element.45.ghid_ref, f32[2048,768]{1,0:T(8,128)} %get-tuple-element.37.normed_ref, f32[2048,128]{1,0:T(8,128)} %get-tuple-element.46.inverse_ref, ...), custom_call_target="tpu_custom_call" | custom-call | tf_op jit(solution)/shard_map/project_backward/pallas_call | solution.py:348
  385.1 70.6 %attention_backward.1 = (bf16[3,768,768]{2,1,0:T(8,128)(2,1)}, f32[8,768]{1,0:T(8,128)}, f32[2048,768]{1,0:T(8,128)}) custom-call(bf16[2048,2304]{1,0:T(8,128)(2,1)} %get-tuple-element.39.q_ref.k_ref.v_ref, bf16[2048,2304]{1,0:T(8,128)(2,1)} %get-tuple-element.39.q_ref.k_ref.v_ref, bf16[2048,2304]{1,0:T(8,128)(2,1)} %get-tuple-element.39.q_ref.k_ref.v_ref, ...), custom_call_target="tpu_custom_call" | custom-call | tf_op jit(solution)/shard_map/attention_backward/pallas_call | solution.py:438
  455.7 5.0 copy.29
  460.7 2.5 copy.31
  466.7 0.9 slice_reduce_fusion
  467.7 0.9 slice_reduce_fusion.1
  469.0 40.0 %all-reduce.1 = f32[32,288]{1,0:T(8,128)S(1)} all-reduce(f32[32,288]{1,0:T(8,128)S(1)} %concatenate.23), channel_id=4, replica_groups=mesh['dp'=16,'inner'=2] {'dp','inner'}, use_global_device_ids=true, to_apply=%region_1.0.clone | all-reduce | flops 9216 | bytes 73728
  510.7 1.4 convert_element_type.17
  512.1 75.5 %reduce-scatter.13.cloned.1.call-done = bf16[24,2304]{1,0:T(8,128)(2,1)} async-done(((bf16[768,2304]{1,0:T(8,128)(2,1)}), bf16[24,2304]{1,0:T(8,128)(2,1)}) %reduce-scatter.13.cloned.1.call-update) | async-done | bytes 110608
  587.6 0.9 reshape.110
  589.3 109.8 %reduce-scatter.9.cloned.1.call-done = bf16[24,3072]{1,0:T(8,128)(2,1)} async-done(((bf16[768,3072]{1,0:T(8,128)(2,1)}), bf16[24,3072]{1,0:T(8,128)(2,1)}) %reduce-scatter.9.cloned.1.call-update) | async-done | bytes 147472 | tf_op jit(solution)/shard_map/reduce_scatter | solution.py:516
  699.1 1.6 convert_element_type.18
  700.8 110.8 %reduce-scatter.11.cloned.1.call-done = bf16[96,768]{1,0:T(8,128)(2,1)} async-done(((bf16[3072,768]{1,0:T(8,128)(2,1)}), bf16[96,768]{1,0:T(8,128)(2,1)}) %reduce-scatter.11.cloned.1.call-update) | async-done | bytes 147472 | tf_op jit(solution)/shard_map/reduce_scatter | solution.py:516
  811.6 1.6 convert_element_type.19
  (56 shorter events, 12.8 us)
Async XLA Ops:
  7.2 60.7 %all-gather.8.cloned.1.call-start = ((), (), s32[]{:S(2)}) async-start(), calls=%async_computation.5 | async-start | bytes 1216512 | tf_op jit(solution)/shard_map/all_gather | solution.py:510
  7.9 122.2 %all-gather.6.cloned.1.call-start = ((), (), s32[]{:S(2)}) async-start(), calls=%async_computation.4 | async-start | bytes 3649536 | tf_op jit(solution)/shard_map/all_gather | solution.py:510
  8.7 187.0 %all-gather.10.cloned.1.call-start = ((), (), s32[]{:S(2)}) async-start(), calls=%async_computation.6 | async-start | bytes 4866048 | tf_op jit(solution)/shard_map/all_gather | solution.py:510
  9.4 251.6 %all-gather.12.cloned.1.call-start = ((), (), s32[]{:S(2)}) async-start(), calls=%async_computation.7 | async-start | bytes 4866048 | tf_op jit(solution)/shard_map/all_gather | solution.py:510
  10.0 500.8 %reduce-scatter.7.cloned.1.call-start = ((), (), s32[]{:S(2)}) async-start(), calls=%async_computation.8 | async-start | bytes 1216512 | tf_op jit(solution)/shard_map/reduce_scatter | solution.py:516
  58.3 258.5 %copy-start = (f32[1,768]{1,0:T(1,128)}, f32[1,768]{1,0:T(1,128)S(1)}, u32[]{:S(2)}) copy-start(f32[1,768]{1,0:T(1,128)S(1)} %reshape.92.gain_ref) | copy-start | bytes 9220
  385.0 202.6 %reduce-scatter.13.cloned.1.call-start = ((), (), s32[]{:S(2)}) async-start(), calls=%async_computation.11 | async-start | bytes 3649536
  463.3 235.9 %reduce-scatter.9.cloned.1.call-start = ((), (), s32[]{:S(2)}) async-start(), calls=%async_computation.9 | async-start | bytes 4866048 | tf_op jit(solution)/shard_map/reduce_scatter | solution.py:516
  464.0 347.6 %reduce-scatter.11.cloned.1.call-start = ((), (), s32[]{:S(2)}) async-start(), calls=%async_computation.10 | async-start | bytes 4866048 | tf_op jit(solution)/shard_map/reduce_scatter | solution.py:516
Sparse Core Ops, SparseCore 0:
  10.9 56.8 all-gather.7
  70.8 59.2 all-gather.5
  133.0 62.6 all-gather.9
  198.5 62.4 all-gather.11
  385.2 95.0 reduce-scatter.6
  485.5 102.0 reduce-scatter.12
  593.1 105.9 reduce-scatter.8
  705.5 106.0 reduce-scatter.10

commit v2 on v1

--- a/solution.py
+++ b/solution.py
@@ -417,9 +417,7 @@
     for start in range(0, acc_ref.shape[0], tile):
         here = slice(start, start + tile)
         acc_ref[here] += dot_nt(grad_ref[here], weights)
-    dw = dot_nn(tokens_t_ref[...], grad_ref[...]).astype(BF16)
-    for part in range(3):
-        dw_ref[part] = dw[:, part * BLOCK : (part + 1) * BLOCK]
+    dw_ref[...] = dot_nn(tokens_t_ref[...], grad_ref[...]).astype(BF16)
 
     @pl.when(pair == pl.num_programs(0) - 1)
     def _():
@@ -444,12 +442,12 @@
             part(width, 0), part(width, 1), part(width, 2), any_,
         ],
         out_specs=[
-            pl.BlockSpec((3, width, BLOCK), lambda i: (0, 0, i)),
+            pl.BlockSpec((width, 3 * BLOCK), lambda i: (0, i)),
             pl.BlockSpec((8, BLOCK), lambda i: (0, i)),
             any_,
         ],
         out_shape=[
-            jax.ShapeDtypeStruct((3, width, width), BF16),
+            jax.ShapeDtypeStruct((width, 3 * width), BF16),
             jax.ShapeDtypeStruct((8, width), F32),
             jax.ShapeDtypeStruct((total, width), F32),
         ],
@@ -492,42 +490,1911 @@
     )
 
 
+MESH = pl.DeviceIdType.MESH
+
+
+def when(condition, body):
+    if condition is True:
+        body()
+    else:
+        pl.when(condition)(body)
+
+
+class Place:
+    def __init__(self, planes):
+        along = lax.axis_index("dp")
+        self.planes = planes
+        self.y = lax.axis_index("inner")
+        self.c = lax.rem(along, 2)
+        self.x = lax.rem(lax.div(along, 2), 2)
+        self.z = lax.div(along, 4)
+
+    def device(self, z=None, x=None, c=None, y=None):
+        z = self.z if z is None else z
+        x = self.x if x is None else x
+        c = self.c if c is None else c
+        return ((z * 2 + x) * 2 + c, self.y if y is None else y)
+
+    @property
+    def above(self):
+        return self.device(z=lax.rem(self.z + 1, self.planes))
+
+    @property
+    def below(self):
+        return self.device(z=lax.rem(self.z + self.planes - 1, self.planes))
+
+    @property
+    def across(self):
+        return self.device(x=1 - self.x)
+
+    @property
+    def beside(self):
+        return self.device(y=1 - self.y)
+
+    @property
+    def partner(self):
+        return self.device(c=1 - self.c)
+
+    @property
+    def has_above(self):
+        return self.z < self.planes - 1
+
+    @property
+    def has_below(self):
+        return self.z > 0
+
+    def enter(self):
+        barrier = pltpu.get_barrier_semaphore()
+
+        def greet(device):
+            pl.semaphore_signal(barrier, inc=1, device_id=device, device_id_type=MESH)
+
+        for device in (self.across, self.beside, self.partner):
+            greet(device)
+        when(self.has_above, lambda: greet(self.above))
+        when(self.has_below, lambda: greet(self.below))
+        pl.semaphore_wait(
+            barrier, 3 + self.has_above.astype(jnp.int32) + self.has_below.astype(jnp.int32)
+        )
+
+
+def half_of(ref, half):
+    if half == 2:
+        return ref
+    width = ref.shape[-1] // 2
+    lead = (slice(None),) * (len(ref.shape) - 1)
+    return ref.at[lead + (slice(half * width, (half + 1) * width),)]
+
+
+SENDS = 48
+
+
+class Gather:
+    def __init__(self, place, index, shard, full, send, recv, local):
+        self.place, self.index, self.shard, self.full = place, index, shard, full
+        self.send, self.recv, self.local = send, recv, local
+        self.halves = (0, 1) if full.shape[-1] % (2 * BLOCK) == 0 else (2, None)
+        self.slot = 0
+        self.ends = []
+
+    def push(self, condition, item, half, device, source=None):
+        slot = self.slot
+        self.slot += 1
+
+        def make():
+            return pltpu.make_async_remote_copy(
+                src_ref=half_of(self.full.at[item] if source is None else source, half),
+                dst_ref=half_of(self.full.at[item], half),
+                send_sem=self.send.at[self.index, slot],
+                recv_sem=self.recv.at[(self.index,) + item + (min(half, 1),)],
+                device_id=device,
+                device_id_type=MESH,
+            )
+
+        when(condition, lambda: make().start())
+        self.ends.append((condition, make))
+
+    def await_item(self, item, half):
+        ref = half_of(self.full.at[item], half)
+        pltpu.make_async_remote_copy(
+            src_ref=ref, dst_ref=ref, send_sem=self.send.at[self.index, 0],
+            recv_sem=self.recv.at[(self.index,) + item + (min(half, 1),)],
+            device_id=self.place.partner, device_id_type=MESH,
+        ).wait_recv()
+
+    def own_copy(self):
+        p = self.place
+        return pltpu.make_async_copy(
+            self.shard, self.full.at[p.z, p.x, p.c, p.y], self.local.at[self.index]
+        )
+
+    def first(self):
+        p = self.place
+        item = (p.z, p.x, p.c, p.y)
+        self.push(p.has_above, item, 2, p.above, self.shard)
+        self.push(p.has_below, item, 2, p.below, self.shard)
+        self.push(True, item, 2, p.across, self.shard)
+        self.push(True, item, 2, p.beside, self.shard)
+        self.push(True, item, 2, p.partner, self.shard)
+        self.own_copy().start()
+
+    def planes_at(self, distance):
+        p = self.place
+        if distance == 0:
+            return [(True, p.z, None, None)]
+        return [
+            (p.z >= distance, p.z - distance, p.has_above, p.above),
+            (p.z + distance < p.planes, p.z + distance, p.has_below, p.below),
+        ]
+
+    def along_z(self, distance):
+        p = self.place
+        for there, z, more, onward in self.planes_at(distance):
+            item = (jnp.clip(z, 0, p.planes - 1), p.x, p.c, p.y)
+            when(there, lambda: self.await_item(item, 2))
+            self.push(jnp.logical_and(there, more), item, 2, onward)
+            for device in (p.across, p.beside, p.partner):
+                self.push(there, item, 2, device)
+
+    def across_xy(self, distance):
+        p = self.place
+        for there, z, _, _ in self.planes_at(distance):
+            z = jnp.clip(z, 0, p.planes - 1)
+            for half, item, onward in (
+                (self.halves[0], (z, 1 - p.x, p.c, p.y), p.beside),
+                (self.halves[1], (z, p.x, p.c, 1 - p.y), p.across),
+            ):
+                when(there, lambda: self.await_item(item, 2))
+                if half is not None:
+                    self.push(there, item, half, onward)
+                self.push(there, item, 2, p.partner)
+
+    def diagonal(self, distance):
+        p = self.place
+        for there, z, _, _ in self.planes_at(distance):
+            item = (jnp.clip(z, 0, p.planes - 1), 1 - p.x, p.c, 1 - p.y)
+
+            def arrive():
+                for half in self.halves:
+                    if half is not None:
+                        self.await_item(item, half)
+
+            when(there, arrive)
+            self.push(there, item, 2, p.partner)
+
+    def finish(self):
+        p = self.place
+        for z in range(p.planes):
+            for x in range(2):
+                for y in range(2):
+                    self.await_item((z, x, 1 - p.c, y), 2)
+        for condition, make in self.ends:
+            when(condition, lambda: make().wait_send())
+        self.own_copy().wait()
+
+
+def gather_kernel(planes, count, *refs):
+    shards, fulls = refs[:count], refs[count : 2 * count]
+    send, recv, local = refs[2 * count :]
+    place = Place(planes)
+    place.enter()
+    gathers = [
+        Gather(place, i, shards[i], fulls[i], send, recv, local) for i in range(count)
+    ]
+    for gather in gathers:
+        gather.first()
+    for distance in range(1, planes + 2):
+        for gather in gathers:
+            if distance < planes:
+                gather.along_z(distance)
+            if distance - 1 < planes:
+                gather.across_xy(distance - 1)
+            if distance >= 2:
+                gather.diagonal(distance - 2)
+    for gather in gathers:
+        gather.finish()
+
+
+def gather_all(planes, shards):
+    count = len(shards)
+    any_ = pl.BlockSpec(memory_space=pl.ANY)
+    fulls = pl.pallas_call(
+        functools.partial(gather_kernel, planes, count),
+        in_specs=[any_] * count,
+        out_specs=[any_] * count,
+        out_shape=[jax.ShapeDtypeStruct((planes, 2, 2, 2) + s.shape, s.dtype) for s in shards],
+        scratch_shapes=[
+            pltpu.SemaphoreType.DMA((count, SENDS)),
+            pltpu.SemaphoreType.DMA((count, planes, 2, 2, 2, 2)),
+            pltpu.SemaphoreType.DMA((count,)),
+        ],
+        compiler_params=pltpu.CompilerParams(collective_id=0, has_side_effects=True, vmem_limit_bytes=VMEM_LIMIT),
+        name="gather_weights",
+    )(*shards)
+    return [f.reshape((-1,) + f.shape[5:]) for f in fulls]
+
+
+class Scatter:
+    def __init__(self, place, index, source, out, bufs, send, recv, local):
+        self.place, self.index, self.source, self.out = place, index, source, out
+        self.held, self.from_partner, self.from_diag, self.from_side, self.from_z, self.spare = bufs
+        self.send, self.recv, self.local = send, recv, local
+        self.split = source.shape[-1] % (2 * BLOCK) == 0
+
+    def copy(self, slot, src, dst, device):
+        return pltpu.make_async_remote_copy(
+            src_ref=src, dst_ref=dst, send_sem=self.send.at[self.index, slot],
+            recv_sem=self.recv.at[self.index, slot], device_id=device, device_id_type=MESH,
+        )
+
+    def own_copy(self):
+        p = self.place
+        return pltpu.make_async_copy(self.source.at[:, :, p.c], self.held, self.local.at[self.index])
+
+    def partner_copy(self):
+        p = self.place
+        return self.copy(0, self.source.at[:, :, 1 - p.c], self.from_partner, p.partner)
+
+    def diag_copies(self):
+        p = self.place
+        ref = self.held.at[:, 1 - p.x, 1 - p.y]
+        if not self.split:
+            return [self.copy(1, ref, self.from_diag.at[0], p.across)]
+        return [
+            self.copy(1, half_of(ref, 0), self.from_diag.at[0], p.across),
+            self.copy(2, half_of(ref, 1), self.from_diag.at[1], p.beside),
+        ]
+
+    def side_copies(self):
+        p = self.place
+        return [
+            self.copy(3, self.held.at[:, 1 - p.x, p.y], self.from_side.at[0], p.across),
+            self.copy(4, self.held.at[:, p.x, 1 - p.y], self.from_side.at[1], p.beside),
+        ]
+
+    def z_copy(self, up, z):
+        p = self.place
+        return self.copy(
+            5 + up * p.planes + z, self.spare.at[z], self.from_z.at[up, z], p.above if up else p.below
+        )
+
+    def start(self):
+        self.own_copy().start()
+        self.partner_copy().start()
+
+    def add(self, x, y, *others):
+        def one(z, _):
+            total = self.held[z, x, y].astype(F32)
+            for other in others:
+                total = total + other(z).astype(F32)
+            self.held[z, x, y] = total.astype(self.held.dtype)
+            return 0
+
+        lax.fori_loop(0, self.place.planes, one, 0)
+
+    def after_partner(self):
+        p = self.place
+        self.own_copy().wait()
+        self.partner_copy().wait_recv()
+        for x, y in ((1 - p.x, 1 - p.y), (1 - p.x, p.y), (p.x, 1 - p.y), (p.x, p.y)):
+            self.add(x, y, lambda z: self.from_partner[z, x, y])
+            if x is not p.x and y is not p.y:
+                for copy in self.diag_copies():
+                    copy.start()
+
+    def after_diag(self):
+        p = self.place
+        width = self.held.shape[-1]
+        for copy in self.diag_copies():
+            copy.wait_recv()
+        parts = ((0, p.x, 1 - p.y, 0, width // 2), (1, 1 - p.x, p.y, width // 2, width))
+        if not self.split:
+            parts = ((0, p.x, 1 - p.y, 0, width),)
+
+        def one(z, _):
+            for index, x, y, low, high in parts:
+                total = self.held[z, x, y, :, low:high].astype(F32) + self.from_diag[index, z].astype(F32)
+                self.held[z, x, y, :, low:high] = total.astype(self.held.dtype)
+            return 0
+
+        lax.fori_loop(0, p.planes, one, 0)
+        for copy in self.side_copies():
+            copy.start()
+
+    def after_side(self):
+        p = self.place
+        for copy in self.side_copies():
+            copy.wait_recv()
+
+        def one(z, _):
+            total = self.held[z, p.x, p.y].astype(F32)
+            total = total + self.from_side[0, z].astype(F32) + self.from_side[1, z].astype(F32)
+            self.spare[z] = total.astype(self.spare.dtype)
+            return 0
+
+        lax.fori_loop(0, p.planes, one, 0)
+        for z in range(p.planes):
+            when(jnp.logical_and(jnp.logical_not(p.has_below), z > p.z), lambda: self.z_copy(1, z).start())
+            when(jnp.logical_and(jnp.logical_not(p.has_above), z < p.z), lambda: self.z_copy(0, z).start())
+
+    def along_z(self):
+        p = self.place
+        for z in range(p.planes):
+            def onward(up, z=z):
+                self.z_copy(up, z).wait_recv()
+                total = self.spare[z].astype(F32) + self.from_z[up, z].astype(F32)
+                self.spare[z] = total.astype(self.spare.dtype)
+                self.z_copy(up, z).start()
+
+            when(jnp.logical_and(jnp.logical_and(p.has_below, p.has_above), z > p.z), lambda: onward(1))
+            when(jnp.logical_and(jnp.logical_and(p.has_below, p.has_above), z < p.z), lambda: onward(0))
+
+    def finish(self, store):
+        p = self.place
+        store(self.spare[p.z].astype(F32), False)
+        for up, there in ((1, p.has_below), (0, p.has_above)):
+            def arrive(up=up):
+                self.z_copy(up, p.z).wait_recv()
+                store(self.from_z[up, p.z].astype(F32), True)
+
+            when(there, arrive)
+        self.partner_copy().wait_send()
+        for copy in self.diag_copies() + self.side_copies():
+            copy.wait_send()
+        for z in range(p.planes):
+            when(jnp.logical_and(z > p.z, p.has_above), lambda: self.z_copy(1, z).wait_send())
+            when(jnp.logical_and(z < p.z, p.has_below), lambda: self.z_copy(0, z).wait_send())
+
+
+def scatter_scratch(planes, rows, width, dtype):
+    split = width % (2 * BLOCK) == 0
+    return [
+        pltpu.VMEM((planes, 2, 2, rows, width), dtype),
+        pltpu.VMEM((planes, 2, 2, rows, width), dtype),
+        pltpu.VMEM((2 if split else 1, planes, rows, width // 2 if split else width), dtype),
+        pltpu.VMEM((2, planes, rows, width), dtype),
+        pltpu.VMEM((2, planes, rows, width), dtype),
+        pltpu.VMEM((planes, rows, width), dtype),
+    ]
+
+
+def scatter_kernel(planes, count, *refs):
+    sources, outs, rest = refs[:count], refs[count : 2 * count], refs[2 * count :]
+    send, recv, local = rest[:3]
+    place = Place(planes)
+    place.enter()
+    scatters = [
+        Scatter(place, i, sources[i], outs[i], rest[3 + 6 * i : 9 + 6 * i], send, recv, local)
+        for i in range(count)
+    ]
+    for s in scatters:
+        s.start()
+    for stage in ("after_partner", "after_diag", "after_side", "along_z"):
+        for s in scatters:
+            getattr(s, stage)()
+    for s in scatters:
+        def store(value, more, out=s.out):
+            if more:
+                out[...] += value
+            else:
+                out[...] = value
+
+        s.finish(store)
+
+
+def scatter_all(planes, sources):
+    count = len(sources)
+    sources = [s.reshape((planes, 2, 2, 2, -1) + s.shape[1:]) for s in sources]
+    shapes = [s.shape[4:] for s in sources]
+    scratch = []
+    for s in sources:
+        scratch += scatter_scratch(planes, *s.shape[4:], s.dtype)
+    any_ = pl.BlockSpec(memory_space=pl.ANY)
+    vmem = pl.BlockSpec(memory_space=pltpu.VMEM)
+    return pl.pallas_call(
+        functools.partial(scatter_kernel, planes, count),
+        in_specs=[any_] * count,
+        out_specs=[vmem] * count,
+        out_shape=[jax.ShapeDtypeStruct(s, F32) for s in shapes],
+        scratch_shapes=[
+            pltpu.SemaphoreType.DMA((count, 5 + 2 * planes)),
+            pltpu.SemaphoreType.DMA((count, 5 + 2 * planes)),
+            pltpu.SemaphoreType.DMA((count,)),
+        ] + scratch,
+        compiler_params=pltpu.CompilerParams(collective_id=1, has_side_effects=True, vmem_limit_bytes=VMEM_LIMIT),
+        name="scatter_gradients",
+    )(*sources)
+
+
+def spread_masks(devices, piece):
+    size = devices * piece
+    column = lax.broadcasted_iota(jnp.int32, (devices, size), 1)
+    start = lax.broadcasted_iota(jnp.int32, (devices, size), 0) * piece
+    owner = jnp.logical_and(column >= start, column < start + piece)
+    column = lax.broadcasted_iota(jnp.int32, (BLOCK, size), 1)
+    number = jnp.floor((column.astype(F32) + 0.5) * (1.0 / piece)).astype(jnp.int32)
+    place = column - number * piece == lax.broadcasted_iota(jnp.int32, (BLOCK, size), 0)
+    return owner, place.astype(F32)
+
+
+def spread_kernel(pieces, gathered_ref, *outs):
+    devices = gathered_ref.shape[0]
+    masks = {piece: spread_masks(devices, piece) for piece in set(pieces)}
+    for index, piece in enumerate(pieces):
+        owner, place = masks[piece]
+        wide = dot_nn(gathered_ref[:, index, :].astype(F32), place)
+        outs[index][...] = jnp.sum(jnp.where(owner, wide, 0.0), axis=0, keepdims=True)
+
+
+def spread_vectors(gathered, pieces):
+    devices = gathered.shape[0]
+    return pl.pallas_call(
+        functools.partial(spread_kernel, pieces),
+        out_shape=[jax.ShapeDtypeStruct((1, devices * piece), F32) for piece in pieces],
+        compiler_params=pltpu.CompilerParams(vmem_limit_bytes=VMEM_LIMIT),
+        name="spread_vectors",
+    )(gathered)
+
+
+def collect_kernel(pieces, devices, *refs):
+    out_ref = refs[-1]
+    masks = {piece: spread_masks(devices, piece) for piece in set(pieces)}
+    for index, piece in enumerate(pieces):
+        owner, place = masks[piece]
+        wide = jnp.where(owner, refs[index][...], 0.0)
+        out_ref[:, index, :] = lax.dot_general(
+            wide, place, (((1,), (1,)), ((), ())),
+            precision=lax.Precision.HIGHEST, preferred_element_type=F32,
+        )
+
+
+def collect_vectors(vectors, pieces, devices):
+    return pl.pallas_call(
+        functools.partial(collect_kernel, pieces, devices),
+        out_shape=jax.ShapeDtypeStruct((devices, 8, BLOCK), F32),
+        compiler_params=pltpu.CompilerParams(vmem_limit_bytes=VMEM_LIMIT),
+        name="collect_vectors",
+    )(*vectors)
+
+
+MESH = pl.DeviceIdType.MESH
+
+
+def when(condition, body):
+    if condition is True:
+        body()
+    else:
+        pl.when(condition)(body)
+
+
+class Place:
+    def __init__(self, planes):
+        along = lax.axis_index("dp")
+        self.planes = planes
+        self.y = lax.axis_index("inner")
+        self.c = lax.rem(along, 2)
+        self.x = lax.rem(lax.div(along, 2), 2)
+        self.z = lax.div(along, 4)
+
+    def device(self, z=None, x=None, c=None, y=None):
+        z = self.z if z is None else z
+        x = self.x if x is None else x
+        c = self.c if c is None else c
+        return ((z * 2 + x) * 2 + c, self.y if y is None else y)
+
+    @property
+    def above(self):
+        return self.device(z=lax.rem(self.z + 1, self.planes))
+
+    @property
+    def below(self):
+        return self.device(z=lax.rem(self.z + self.planes - 1, self.planes))
+
+    @property
+    def across(self):
+        return self.device(x=1 - self.x)
+
+    @property
+    def beside(self):
+        return self.device(y=1 - self.y)
+
+    @property
+    def partner(self):
+        return self.device(c=1 - self.c)
+
+    @property
+    def has_above(self):
+        return self.z < self.planes - 1
+
+    @property
+    def has_below(self):
+        return self.z > 0
+
+    def enter(self):
+        barrier = pltpu.get_barrier_semaphore()
+
+        def greet(device):
+            pl.semaphore_signal(barrier, inc=1, device_id=device, device_id_type=MESH)
+
+        for device in (self.across, self.beside, self.partner):
+            greet(device)
+        when(self.has_above, lambda: greet(self.above))
+        when(self.has_below, lambda: greet(self.below))
+        pl.semaphore_wait(
+            barrier, 3 + self.has_above.astype(jnp.int32) + self.has_below.astype(jnp.int32)
+        )
+
+
+def half_of(ref, half):
+    if half == 2:
+        return ref
+    width = ref.shape[-1] // 2
+    lead = (slice(None),) * (len(ref.shape) - 1)
+    return ref.at[lead + (slice(half * width, (half + 1) * width),)]
+
+
+SENDS = 48
+
+
+class Gather:
+    def __init__(self, place, index, shard, full, send, recv, local):
+        self.place, self.index, self.shard, self.full = place, index, shard, full
+        self.send, self.recv, self.local = send, recv, local
+        self.halves = (0, 1) if full.shape[-1] % (2 * BLOCK) == 0 else (2, None)
+        self.slot = 0
+        self.ends = []
+
+    def push(self, condition, item, half, device, source=None):
+        slot = self.slot
+        self.slot += 1
+
+        def make():
+            return pltpu.make_async_remote_copy(
+                src_ref=half_of(self.full.at[item] if source is None else source, half),
+                dst_ref=half_of(self.full.at[item], half),
+                send_sem=self.send.at[self.index, slot],
+                recv_sem=self.recv.at[(self.index,) + item + (min(half, 1),)],
+                device_id=device,
+                device_id_type=MESH,
+            )
+
+        when(condition, lambda: make().start())
+        self.ends.append((condition, make))
+
+    def await_item(self, item, half):
+        ref = half_of(self.full.at[item], half)
+        pltpu.make_async_remote_copy(
+            src_ref=ref, dst_ref=ref, send_sem=self.send.at[self.index, 0],
+            recv_sem=self.recv.at[(self.index,) + item + (min(half, 1),)],
+            device_id=self.place.partner, device_id_type=MESH,
+        ).wait_recv()
+
+    def own_copy(self):
+        p = self.place
+        return pltpu.make_async_copy(
+            self.shard, self.full.at[p.z, p.x, p.c, p.y], self.local.at[self.index]
+        )
+
+    def first(self):
+        p = self.place
+        item = (p.z, p.x, p.c, p.y)
+        self.push(p.has_above, item, 2, p.above, self.shard)
+        self.push(p.has_below, item, 2, p.below, self.shard)
+        self.push(True, item, 2, p.across, self.shard)
+        self.push(True, item, 2, p.beside, self.shard)
+        self.push(True, item, 2, p.partner, self.shard)
+        self.own_copy().start()
+
+    def planes_at(self, distance):
+        p = self.place
+        if distance == 0:
+            return [(True, p.z, None, None)]
+        return [
+            (p.z >= distance, p.z - distance, p.has_above, p.above),
+            (p.z + distance < p.planes, p.z + distance, p.has_below, p.below),
+        ]
+
+    def along_z(self, distance):
+        p = self.place
+        for there, z, more, onward in self.planes_at(distance):
+            item = (jnp.clip(z, 0, p.planes - 1), p.x, p.c, p.y)
+            when(there, lambda: self.await_item(item, 2))
+            self.push(jnp.logical_and(there, more), item, 2, onward)
+            for device in (p.across, p.beside, p.partner):
+                self.push(there, item, 2, device)
+
+    def across_xy(self, distance):
+        p = self.place
+        for there, z, _, _ in self.planes_at(distance):
+            z = jnp.clip(z, 0, p.planes - 1)
+            for half, item, onward in (
+                (self.halves[0], (z, 1 - p.x, p.c, p.y), p.beside),
+                (self.halves[1], (z, p.x, p.c, 1 - p.y), p.across),
+            ):
+                when(there, lambda: self.await_item(item, 2))
+                if half is not None:
+                    self.push(there, item, half, onward)
+                self.push(there, item, 2, p.partner)
+
+    def diagonal(self, distance):
+        p = self.place
+        for there, z, _, _ in self.planes_at(distance):
+            item = (jnp.clip(z, 0, p.planes - 1), 1 - p.x, p.c, 1 - p.y)
+
+            def arrive():
+                for half in self.halves:
+                    if half is not None:
+                        self.await_item(item, half)
+
+            when(there, arrive)
+            self.push(there, item, 2, p.partner)
+
+    def finish(self):
+        p = self.place
+        for z in range(p.planes):
+            for x in range(2):
+                for y in range(2):
+                    self.await_item((z, x, 1 - p.c, y), 2)
+        for condition, make in self.ends:
+            when(condition, lambda: make().wait_send())
+        self.own_copy().wait()
+
+
+def gather_kernel(planes, count, *refs):
+    shards, fulls = refs[:count], refs[count : 2 * count]
+    send, recv, local = refs[2 * count :]
+    place = Place(planes)
+    place.enter()
+    gathers = [
+        Gather(place, i, shards[i], fulls[i], send, recv, local) for i in range(count)
+    ]
+    for gather in gathers:
+        gather.first()
+    for distance in range(1, planes + 2):
+        for gather in gathers:
+            if distance < planes:
+                gather.along_z(distance)
+            if distance - 1 < planes:
+                gather.across_xy(distance - 1)
+            if distance >= 2:
+                gather.diagonal(distance - 2)
+    for gather in gathers:
+        gather.finish()
+
+
+def gather_all(planes, shards):
+    count = len(shards)
+    any_ = pl.BlockSpec(memory_space=pl.ANY)
+    fulls = pl.pallas_call(
+        functools.partial(gather_kernel, planes, count),
+        in_specs=[any_] * count,
+        out_specs=[any_] * count,
+        out_shape=[jax.ShapeDtypeStruct((planes, 2, 2, 2) + s.shape, s.dtype) for s in shards],
+        scratch_shapes=[
+            pltpu.SemaphoreType.DMA((count, SENDS)),
+            pltpu.SemaphoreType.DMA((count, planes, 2, 2, 2, 2)),
+            pltpu.SemaphoreType.DMA((count,)),
+        ],
+        compiler_params=pltpu.CompilerParams(collective_id=0, has_side_effects=True, vmem_limit_bytes=VMEM_LIMIT),
+        name="gather_weights",
+    )(*shards)
+    return [f.reshape((-1,) + f.shape[4:]) for f in fulls]
+
+
+class Scatter:
+    def __init__(self, place, index, source, out, bufs, send, recv, local):
+        self.place, self.index, self.source, self.out = place, index, source, out
+        self.held, self.from_partner, self.from_diag, self.from_side, self.from_z, self.spare = bufs
+        self.send, self.recv, self.local = send, recv, local
+        self.split = source.shape[-1] % (2 * BLOCK) == 0
+
+    def copy(self, slot, src, dst, device):
+        return pltpu.make_async_remote_copy(
+            src_ref=src, dst_ref=dst, send_sem=self.send.at[self.index, slot],
+            recv_sem=self.recv.at[self.index, slot], device_id=device, device_id_type=MESH,
+        )
+
+    def own_copy(self):
+        p = self.place
+        return pltpu.make_async_copy(self.source.at[:, :, p.c], self.held, self.local.at[self.index])
+
+    def partner_copy(self):
+        p = self.place
+        return self.copy(0, self.source.at[:, :, 1 - p.c], self.from_partner, p.partner)
+
+    def diag_copies(self):
+        p = self.place
+        ref = self.held.at[:, 1 - p.x, 1 - p.y]
+        if not self.split:
+            return [self.copy(1, ref, self.from_diag.at[0], p.across)]
+        return [
+            self.copy(1, half_of(ref, 0), self.from_diag.at[0], p.across),
+            self.copy(2, half_of(ref, 1), self.from_diag.at[1], p.beside),
+        ]
+
+    def side_copies(self):
+        p = self.place
+        return [
+            self.copy(3, self.held.at[:, 1 - p.x, p.y], self.from_side.at[0], p.across),
+            self.copy(4, self.held.at[:, p.x, 1 - p.y], self.from_side.at[1], p.beside),
+        ]
+
+    def z_copy(self, up, z):
+        p = self.place
+        return self.copy(
+            5 + up * p.planes + z, self.spare.at[z], self.from_z.at[up, z], p.above if up else p.below
+        )
+
+    def start(self):
+        self.own_copy().start()
+        self.partner_copy().start()
+
+    def add(self, x, y, *others):
+        def one(z, _):
+            total = self.held[z, x, y].astype(F32)
+            for other in others:
+                total = total + other(z).astype(F32)
+            self.held[z, x, y] = total.astype(self.held.dtype)
+            return 0
+
+        lax.fori_loop(0, self.place.planes, one, 0)
+
+    def after_partner(self):
+        p = self.place
+        self.own_copy().wait()
+        self.partner_copy().wait_recv()
+        for x, y in ((1 - p.x, 1 - p.y), (1 - p.x, p.y), (p.x, 1 - p.y), (p.x, p.y)):
+            self.add(x, y, lambda z: self.from_partner[z, x, y])
+            if x is not p.x and y is not p.y:
+                for copy in self.diag_copies():
+                    copy.start()
+
+    def after_diag(self):
+        p = self.place
+        width = self.held.shape[-1]
+        for copy in self.diag_copies():
+            copy.wait_recv()
+        parts = ((0, p.x, 1 - p.y, 0, width // 2), (1, 1 - p.x, p.y, width // 2, width))
+        if not self.split:
+            parts = ((0, p.x, 1 - p.y, 0, width),)
+
+        def one(z, _):
+            for index, x, y, low, high in parts:
+                total = self.held[z, x, y, :, low:high].astype(F32) + self.from_diag[index, z].astype(F32)
+                self.held[z, x, y, :, low:high] = total.astype(self.held.dtype)
+            return 0
+
+        lax.fori_loop(0, p.planes, one, 0)
+        for copy in self.side_copies():
+            copy.start()
+
+    def after_side(self):
+        p = self.place
+        for copy in self.side_copies():
+            copy.wait_recv()
+
+        def one(z, _):
+            total = self.held[z, p.x, p.y].astype(F32)
+            total = total + self.from_side[0, z].astype(F32) + self.from_side[1, z].astype(F32)
+            self.spare[z] = total.astype(self.spare.dtype)
+            return 0
+
+        lax.fori_loop(0, p.planes, one, 0)
+        for z in range(p.planes):
+            when(jnp.logical_and(jnp.logical_not(p.has_below), z > p.z), lambda: self.z_copy(1, z).start())
+            when(jnp.logical_and(jnp.logical_not(p.has_above), z < p.z), lambda: self.z_copy(0, z).start())
+
+    def along_z(self):
+        p = self.place
+        for z in range(p.planes):
+            def onward(up, z=z):
+                self.z_copy(up, z).wait_recv()
+                total = self.spare[z].astype(F32) + self.from_z[up, z].astype(F32)
+                self.spare[z] = total.astype(self.spare.dtype)
+                self.z_copy(up, z).start()
+
+            when(jnp.logical_and(jnp.logical_and(p.has_below, p.has_above), z > p.z), lambda: onward(1))
+            when(jnp.logical_and(jnp.logical_and(p.has_below, p.has_above), z < p.z), lambda: onward(0))
+
+    def finish(self, store):
+        p = self.place
+        store(self.spare[p.z].astype(F32), False)
+        for up, there in ((1, p.has_below), (0, p.has_above)):
+            def arrive(up=up):
+                self.z_copy(up, p.z).wait_recv()
+                store(self.from_z[up, p.z].astype(F32), True)
+
+            when(there, arrive)
+        self.partner_copy().wait_send()
+        for copy in self.diag_copies() + self.side_copies():
+            copy.wait_send()
+        for z in range(p.planes):
+            when(jnp.logical_and(z > p.z, p.has_above), lambda: self.z_copy(1, z).wait_send())
+            when(jnp.logical_and(z < p.z, p.has_below), lambda: self.z_copy(0, z).wait_send())
+
+
+def scatter_scratch(planes, rows, width, dtype):
+    split = width % (2 * BLOCK) == 0
+    return [
+        pltpu.VMEM((planes, 2, 2, rows, width), dtype),
+        pltpu.VMEM((planes, 2, 2, rows, width), dtype),
+        pltpu.VMEM((2 if split else 1, planes, rows, width // 2 if split else width), dtype),
+        pltpu.VMEM((2, planes, rows, width), dtype),
+        pltpu.VMEM((2, planes, rows, width), dtype),
+        pltpu.VMEM((planes, rows, width), dtype),
+    ]
+
+
+def scatter_kernel(planes, count, *refs):
+    sources, outs, rest = refs[:count], refs[count : 2 * count], refs[2 * count :]
+    send, recv, local = rest[:3]
+    place = Place(planes)
+    place.enter()
+    scatters = [
+        Scatter(place, i, sources[i], outs[i], rest[3 + 6 * i : 9 + 6 * i], send, recv, local)
+        for i in range(count)
+    ]
+    for s in scatters:
+        s.start()
+    for stage in ("after_partner", "after_diag", "after_side", "along_z"):
+        for s in scatters:
+            getattr(s, stage)()
+    for s in scatters:
+        def store(value, more, out=s.out):
+            if more:
+                out[...] += value
+            else:
+                out[...] = value
+
+        s.finish(store)
+
+
+def scatter_all(planes, sources):
+    count = len(sources)
+    sources = [s.reshape((planes, 2, 2, 2, -1) + s.shape[1:]) for s in sources]
+    shapes = [s.shape[4:] for s in sources]
+    scratch = []
+    for s in sources:
+        scratch += scatter_scratch(planes, *s.shape[4:], s.dtype)
+    any_ = pl.BlockSpec(memory_space=pl.ANY)
+    vmem = pl.BlockSpec(memory_space=pltpu.VMEM)
+    return pl.pallas_call(
+        functools.partial(scatter_kernel, planes, count),
+        in_specs=[any_] * count,
+        out_specs=[vmem] * count,
+        out_shape=[jax.ShapeDtypeStruct(s, F32) for s in shapes],
+        scratch_shapes=[
+            pltpu.SemaphoreType.DMA((count, 5 + 2 * planes)),
+            pltpu.SemaphoreType.DMA((count, 5 + 2 * planes)),
+            pltpu.SemaphoreType.DMA((count,)),
+        ] + scratch,
+        compiler_params=pltpu.CompilerParams(collective_id=1, has_side_effects=True, vmem_limit_bytes=VMEM_LIMIT),
+        name="scatter_gradients",
+    )(*sources)
+
+
+def spread_masks(devices, piece):
+    size = devices * piece
+    column = lax.broadcasted_iota(jnp.int32, (devices, size), 1)
+    start = lax.broadcasted_iota(jnp.int32, (devices, size), 0) * piece
+    owner = jnp.logical_and(column >= start, column < start + piece)
+    column = lax.broadcasted_iota(jnp.int32, (BLOCK, size), 1)
+    number = jnp.floor((column.astype(F32) + 0.5) * (1.0 / piece)).astype(jnp.int32)
+    place = column - number * piece == lax.broadcasted_iota(jnp.int32, (BLOCK, size), 0)
+    return owner, place.astype(F32)
+
+
+def spread_kernel(pieces, gathered_ref, *outs):
+    devices = gathered_ref.shape[0]
+    masks = {piece: spread_masks(devices, piece) for piece in set(pieces)}
+    for index, piece in enumerate(pieces):
+        owner, place = masks[piece]
+        wide = dot_nn(gathered_ref[:, index, :].astype(F32), place)
+        outs[index][...] = jnp.sum(jnp.where(owner, wide, 0.0), axis=0, keepdims=True)
+
+
+def spread_vectors(gathered, pieces):
+    devices = gathered.shape[0]
+    return pl.pallas_call(
+        functools.partial(spread_kernel, pieces),
+        out_shape=[jax.ShapeDtypeStruct((1, devices * piece), F32) for piece in pieces],
+        compiler_params=pltpu.CompilerParams(vmem_limit_bytes=VMEM_LIMIT),
+        name="spread_vectors",
+    )(gathered)
+
+
+def collect_kernel(pieces, devices, *refs):
+    out_ref = refs[-1]
+    masks = {piece: spread_masks(devices, piece) for piece in set(pieces)}
+    for index, piece in enumerate(pieces):
+        owner, place = masks[piece]
+        wide = jnp.where(owner, refs[index][...], 0.0)
+        out_ref[:, index, :] = lax.dot_general(
+            wide, place, (((1,), (1,)), ((), ())),
+            precision=lax.Precision.HIGHEST, preferred_element_type=F32,
+        )
+
+
+def collect_vectors(vectors, pieces, devices):
+    return pl.pallas_call(
+        functools.partial(collect_kernel, pieces, devices),
+        out_shape=jax.ShapeDtypeStruct((devices, 8, BLOCK), F32),
+        compiler_params=pltpu.CompilerParams(vmem_limit_bytes=VMEM_LIMIT),
+        name="collect_vectors",
+    )(*vectors)
+
+
+MESH = pl.DeviceIdType.MESH
+
+
+def when(condition, body):
+    if condition is True:
+        body()
+    else:
+        pl.when(condition)(body)
+
+
+class Place:
+    def __init__(self, planes):
+        along = lax.axis_index("dp")
+        self.planes = planes
+        self.y = lax.axis_index("inner")
+        self.c = lax.rem(along, 2)
+        self.x = lax.rem(lax.div(along, 2), 2)
+        self.z = lax.div(along, 4)
+
+    def device(self, z=None, x=None, c=None, y=None):
+        z = self.z if z is None else z
+        x = self.x if x is None else x
+        c = self.c if c is None else c
+        return ((z * 2 + x) * 2 + c, self.y if y is None else y)
+
+    @property
+    def above(self):
+        return self.device(z=lax.rem(self.z + 1, self.planes))
+
+    @property
+    def below(self):
+        return self.device(z=lax.rem(self.z + self.planes - 1, self.planes))
+
+    @property
+    def across(self):
+        return self.device(x=1 - self.x)
+
+    @property
+    def beside(self):
+        return self.device(y=1 - self.y)
+
+    @property
+    def partner(self):
+        return self.device(c=1 - self.c)
+
+    @property
+    def has_above(self):
+        return self.z < self.planes - 1
+
+    @property
+    def has_below(self):
+        return self.z > 0
+
+    def enter(self):
+        barrier = pltpu.get_barrier_semaphore()
+
+        def greet(device):
+            pl.semaphore_signal(barrier, inc=1, device_id=device, device_id_type=MESH)
+
+        for device in (self.across, self.beside, self.partner):
+            greet(device)
+        when(self.has_above, lambda: greet(self.above))
+        when(self.has_below, lambda: greet(self.below))
+        pl.semaphore_wait(
+            barrier, 3 + self.has_above.astype(jnp.int32) + self.has_below.astype(jnp.int32)
+        )
+
+
+def half_of(ref, half):
+    if half == 2:
+        return ref
+    width = ref.shape[-1] // 2
+    lead = (slice(None),) * (len(ref.shape) - 1)
+    return ref.at[lead + (slice(half * width, (half + 1) * width),)]
+
+
+SENDS = 48
+
+
+class Gather:
+    def __init__(self, place, index, shard, full, send, recv, local):
+        self.place, self.index, self.shard, self.full = place, index, shard, full
+        self.send, self.recv, self.local = send, recv, local
+        self.halves = (0, 1) if full.shape[-1] % (2 * BLOCK) == 0 else (2, None)
+        self.slot = 0
+        self.ends = []
+
+    def push(self, condition, item, half, device, source=None):
+        slot = self.slot
+        self.slot += 1
+
+        def make():
+            return pltpu.make_async_remote_copy(
+                src_ref=half_of(self.full.at[item] if source is None else source, half),
+                dst_ref=half_of(self.full.at[item], half),
+                send_sem=self.send.at[self.index, slot],
+                recv_sem=self.recv.at[(self.index,) + item + (min(half, 1),)],
+                device_id=device,
+                device_id_type=MESH,
+            )
+
+        when(condition, lambda: make().start())
+        self.ends.append((condition, make))
+
+    def await_item(self, item, half):
+        ref = half_of(self.full.at[item], half)
+        pltpu.make_async_remote_copy(
+            src_ref=ref, dst_ref=ref, send_sem=self.send.at[self.index, 0],
+            recv_sem=self.recv.at[(self.index,) + item + (min(half, 1),)],
+            device_id=self.place.partner, device_id_type=MESH,
+        ).wait_recv()
+
+    def own_copy(self):
+        p = self.place
+        return pltpu.make_async_copy(
+            self.shard, self.full.at[p.z, p.x, p.c, p.y], self.local.at[self.index]
+        )
+
+    def first(self):
+        p = self.place
+        item = (p.z, p.x, p.c, p.y)
+        self.push(p.has_above, item, 2, p.above, self.shard)
+        self.push(p.has_below, item, 2, p.below, self.shard)
+        self.push(True, item, 2, p.across, self.shard)
+        self.push(True, item, 2, p.beside, self.shard)
+        self.push(True, item, 2, p.partner, self.shard)
+        self.own_copy().start()
+
+    def planes_at(self, distance):
+        p = self.place
+        if distance == 0:
+            return [(True, p.z, None, None)]
+        return [
+            (p.z >= distance, p.z - distance, p.has_above, p.above),
+            (p.z + distance < p.planes, p.z + distance, p.has_below, p.below),
+        ]
+
+    def along_z(self, distance):
+        p = self.place
+        for there, z, more, onward in self.planes_at(distance):
+            item = (jnp.clip(z, 0, p.planes - 1), p.x, p.c, p.y)
+            when(there, lambda: self.await_item(item, 2))
+            self.push(jnp.logical_and(there, more), item, 2, onward)
+            for device in (p.across, p.beside, p.partner):
+                self.push(there, item, 2, device)
+
+    def across_xy(self, distance):
+        p = self.place
+        for there, z, _, _ in self.planes_at(distance):
+            z = jnp.clip(z, 0, p.planes - 1)
+            for half, item, onward in (
+                (self.halves[0], (z, 1 - p.x, p.c, p.y), p.beside),
+                (self.halves[1], (z, p.x, p.c, 1 - p.y), p.across),
+            ):
+                when(there, lambda: self.await_item(item, 2))
+                if half is not None:
+                    self.push(there, item, half, onward)
+                self.push(there, item, 2, p.partner)
+
+    def diagonal(self, distance):
+        p = self.place
+        for there, z, _, _ in self.planes_at(distance):
+            item = (jnp.clip(z, 0, p.planes - 1), 1 - p.x, p.c, 1 - p.y)
+
+            def arrive():
+                for half in self.halves:
+                    if half is not None:
+                        self.await_item(item, half)
+
+            when(there, arrive)
+            self.push(there, item, 2, p.partner)
+
+    def finish(self):
+        p = self.place
+        for z in range(p.planes):
+            for x in range(2):
+                for y in range(2):
+                    self.await_item((z, x, 1 - p.c, y), 2)
+        for condition, make in self.ends:
+            when(condition, lambda: make().wait_send())
+        self.own_copy().wait()
+
+
+def gather_kernel(planes, count, *refs):
+    shards, fulls = refs[:count], refs[count : 2 * count]
+    send, recv, local = refs[2 * count :]
+    place = Place(planes)
+    place.enter()
+    gathers = [
+        Gather(place, i, shards[i], fulls[i], send, recv, local) for i in range(count)
+    ]
+    for gather in gathers:
+        gather.first()
+    for distance in range(1, planes + 2):
+        for gather in gathers:
+            if distance < planes:
+                gather.along_z(distance)
+            if distance - 1 < planes:
+                gather.across_xy(distance - 1)
+            if distance >= 2:
+                gather.diagonal(distance - 2)
+    for gather in gathers:
+        gather.finish()
+
+
+def gather_all(planes, shards):
+    count = len(shards)
+    any_ = pl.BlockSpec(memory_space=pl.ANY)
+    fulls = pl.pallas_call(
+        functools.partial(gather_kernel, planes, count),
+        in_specs=[any_] * count,
+        out_specs=[any_] * count,
+        out_shape=[jax.ShapeDtypeStruct((planes, 2, 2, 2) + s.shape, s.dtype) for s in shards],
+        scratch_shapes=[
+            pltpu.SemaphoreType.DMA((count, SENDS)),
+            pltpu.SemaphoreType.DMA((count, planes, 2, 2, 2, 2)),
+            pltpu.SemaphoreType.DMA((count,)),
+        ],
+        compiler_params=pltpu.CompilerParams(collective_id=0, has_side_effects=True, vmem_limit_bytes=VMEM_LIMIT),
+        name="gather_weights",
+    )(*shards)
+    return [f.reshape((-1,) + f.shape[4:]) for f in fulls]
+
+
+class Scatter:
+    def __init__(self, place, index, source, out, bufs, send, recv, local):
+        self.place, self.index, self.source, self.out = place, index, source, out
+        self.held, self.from_partner, self.from_diag, self.from_side, self.from_z, self.spare = bufs
+        self.send, self.recv, self.local = send, recv, local
+        self.split = source.shape[-1] % (2 * BLOCK) == 0
+
+    def copy(self, slot, src, dst, device):
+        return pltpu.make_async_remote_copy(
+            src_ref=src, dst_ref=dst, send_sem=self.send.at[self.index, slot],
+            recv_sem=self.recv.at[self.index, slot], device_id=device, device_id_type=MESH,
+        )
+
+    def own_copy(self):
+        p = self.place
+        return pltpu.make_async_copy(self.source.at[:, :, p.c], self.held, self.local.at[self.index])
+
+    def partner_copy(self):
+        p = self.place
+        return self.copy(0, self.source.at[:, :, 1 - p.c], self.from_partner, p.partner)
+
+    def diag_copies(self):
+        p = self.place
+        ref = self.held.at[:, 1 - p.x, 1 - p.y]
+        if not self.split:
+            return [self.copy(1, ref, self.from_diag.at[0], p.across)]
+        return [
+            self.copy(1, half_of(ref, 0), self.from_diag.at[0], p.across),
+            self.copy(2, half_of(ref, 1), self.from_diag.at[1], p.beside),
+        ]
+
+    def side_copies(self):
+        p = self.place
+        return [
+            self.copy(3, self.held.at[:, 1 - p.x, p.y], self.from_side.at[0], p.across),
+            self.copy(4, self.held.at[:, p.x, 1 - p.y], self.from_side.at[1], p.beside),
+        ]
+
+    def z_copy(self, up, z):
+        p = self.place
+        return self.copy(
+            5 + up * p.planes + z, self.spare.at[z], self.from_z.at[up, z], p.above if up else p.below
+        )
+
+    def start(self):
+        self.own_copy().start()
+        self.partner_copy().start()
+
+    def add(self, x, y, *others):
+        def one(z, _):
+            total = self.held[z, x, y].astype(F32)
+            for other in others:
+                total = total + other(z).astype(F32)
+            self.held[z, x, y] = total.astype(self.held.dtype)
+            return 0
+
+        lax.fori_loop(0, self.place.planes, one, 0)
+
+    def after_partner(self):
+        p = self.place
+        self.own_copy().wait()
+        self.partner_copy().wait_recv()
+        for x, y in ((1 - p.x, 1 - p.y), (1 - p.x, p.y), (p.x, 1 - p.y), (p.x, p.y)):
+            self.add(x, y, lambda z: self.from_partner[z, x, y])
+            if x is not p.x and y is not p.y:
+                for copy in self.diag_copies():
+                    copy.start()
+
+    def after_diag(self):
+        p = self.place
+        width = self.held.shape[-1]
+        for copy in self.diag_copies():
+            copy.wait_recv()
+        parts = ((0, p.x, 1 - p.y, 0, width // 2), (1, 1 - p.x, p.y, width // 2, width))
+        if not self.split:
+            parts = ((0, p.x, 1 - p.y, 0, width),)
+
+        def one(z, _):
+            for index, x, y, low, high in parts:
+                total = self.held[z, x, y, :, low:high].astype(F32) + self.from_diag[index, z].astype(F32)
+                self.held[z, x, y, :, low:high] = total.astype(self.held.dtype)
+            return 0
+
+        lax.fori_loop(0, p.planes, one, 0)
+        for copy in self.side_copies():
+            copy.start()
+
+    def after_side(self):
+        p = self.place
+        for copy in self.side_copies():
+            copy.wait_recv()
+
+        def one(z, _):
+            total = self.held[z, p.x, p.y].astype(F32)
+            total = total + self.from_side[0, z].astype(F32) + self.from_side[1, z].astype(F32)
+            self.spare[z] = total.astype(self.spare.dtype)
+            return 0
+
+        lax.fori_loop(0, p.planes, one, 0)
+        for z in range(p.planes):
+            when(jnp.logical_and(jnp.logical_not(p.has_below), z > p.z), lambda: self.z_copy(1, z).start())
+            when(jnp.logical_and(jnp.logical_not(p.has_above), z < p.z), lambda: self.z_copy(0, z).start())
+
+    def along_z(self):
+        p = self.place
+        for z in range(p.planes):
+            def onward(up, z=z):
+                self.z_copy(up, z).wait_recv()
+                total = self.spare[z].astype(F32) + self.from_z[up, z].astype(F32)
+                self.spare[z] = total.astype(self.spare.dtype)
+                self.z_copy(up, z).start()
+
+            when(jnp.logical_and(jnp.logical_and(p.has_below, p.has_above), z > p.z), lambda: onward(1))
+            when(jnp.logical_and(jnp.logical_and(p.has_below, p.has_above), z < p.z), lambda: onward(0))
+
+    def finish(self, store):
+        p = self.place
+        store(self.spare[p.z].astype(F32), False)
+        for up, there in ((1, p.has_below), (0, p.has_above)):
+            def arrive(up=up):
+                self.z_copy(up, p.z).wait_recv()
+                store(self.from_z[up, p.z].astype(F32), True)
+
+            when(there, arrive)
+        self.partner_copy().wait_send()
+        for copy in self.diag_copies() + self.side_copies():
+            copy.wait_send()
+        for z in range(p.planes):
+            when(jnp.logical_and(z > p.z, p.has_above), lambda: self.z_copy(1, z).wait_send())
+            when(jnp.logical_and(z < p.z, p.has_below), lambda: self.z_copy(0, z).wait_send())
+
+
+def scatter_scratch(planes, rows, width, dtype):
+    split = width % (2 * BLOCK) == 0
+    return [
+        pltpu.VMEM((planes, 2, 2, rows, width), dtype),
+        pltpu.VMEM((planes, 2, 2, rows, width), dtype),
+        pltpu.VMEM((2 if split else 1, planes, rows, width // 2 if split else width), dtype),
+        pltpu.VMEM((2, planes, rows, width), dtype),
+        pltpu.VMEM((2, planes, rows, width), dtype),
+        pltpu.VMEM((planes, rows, width), dtype),
+    ]
+
+
+def scatter_kernel(planes, count, *refs):
+    sources, outs, rest = refs[:count], refs[count : 2 * count], refs[2 * count :]
+    send, recv, local = rest[:3]
+    place = Place(planes)
+    place.enter()
+    scatters = [
+        Scatter(place, i, sources[i], outs[i], rest[3 + 6 * i : 9 + 6 * i], send, recv, local)
+        for i in range(count)
+    ]
+    for s in scatters:
+        s.start()
+    for stage in ("after_partner", "after_diag", "after_side", "along_z"):
+        for s in scatters:
+            getattr(s, stage)()
+    for s in scatters:
+        def store(value, more, out=s.out):
+            if more:
+                out[...] += value
+            else:
+                out[...] = value
+
+        s.finish(store)
+
+
+def scatter_all(planes, sources):
+    count = len(sources)
+    sources = [s.reshape((planes, 2, 2, 2) + s.shape[1:]) for s in sources]
+    shapes = [s.shape[4:] for s in sources]
+    scratch = []
+    for s in sources:
+        scratch += scatter_scratch(planes, *s.shape[4:], s.dtype)
+    any_ = pl.BlockSpec(memory_space=pl.ANY)
+    vmem = pl.BlockSpec(memory_space=pltpu.VMEM)
+    return pl.pallas_call(
+        functools.partial(scatter_kernel, planes, count),
+        in_specs=[any_] * count,
+        out_specs=[vmem] * count,
+        out_shape=[jax.ShapeDtypeStruct(s, F32) for s in shapes],
+        scratch_shapes=[
+            pltpu.SemaphoreType.DMA((count, 5 + 2 * planes)),
+            pltpu.SemaphoreType.DMA((count, 5 + 2 * planes)),
+            pltpu.SemaphoreType.DMA((count,)),
+        ] + scratch,
+        compiler_params=pltpu.CompilerParams(collective_id=1, has_side_effects=True, vmem_limit_bytes=VMEM_LIMIT),
+        name="scatter_gradients",
+    )(*sources)
+
+
+def spread_masks(devices, piece):
+    size = devices * piece
+    column = lax.broadcasted_iota(jnp.int32, (devices, size), 1)
+    start = lax.broadcasted_iota(jnp.int32, (devices, size), 0) * piece
+    owner = jnp.logical_and(column >= start, column < start + piece)
+    column = lax.broadcasted_iota(jnp.int32, (BLOCK, size), 1)
+    number = jnp.floor((column.astype(F32) + 0.5) * (1.0 / piece)).astype(jnp.int32)
+    place = column - number * piece == lax.broadcasted_iota(jnp.int32, (BLOCK, size), 0)
+    return owner, place.astype(F32)
+
+
+def spread_kernel(pieces, gathered_ref, *outs):
+    devices = gathered_ref.shape[0]
+    masks = {piece: spread_masks(devices, piece) for piece in set(pieces)}
+    for index, piece in enumerate(pieces):
+        owner, place = masks[piece]
+        wide = dot_nn(gathered_ref[:, index, :].astype(F32), place)
+        outs[index][...] = jnp.sum(jnp.where(owner, wide, 0.0), axis=0, keepdims=True)
+
+
+def spread_vectors(gathered, pieces):
+    devices = gathered.shape[0]
+    return pl.pallas_call(
+        functools.partial(spread_kernel, pieces),
+        out_shape=[jax.ShapeDtypeStruct((1, devices * piece), F32) for piece in pieces],
+        compiler_params=pltpu.CompilerParams(vmem_limit_bytes=VMEM_LIMIT),
+        name="spread_vectors",
+    )(gathered)
+
+
+def collect_kernel(pieces, devices, *refs):
+    out_ref = refs[-1]
+    masks = {piece: spread_masks(devices, piece) for piece in set(pieces)}
+    for index, piece in enumerate(pieces):
+        owner, place = masks[piece]
+        wide = jnp.where(owner, refs[index][...], 0.0)
+        out_ref[:, index, :] = lax.dot_general(
+            wide, place, (((1,), (1,)), ((), ())),
+            precision=lax.Precision.HIGHEST, preferred_element_type=F32,
+        )
+
+
+def collect_vectors(vectors, pieces, devices):
+    return pl.pallas_call(
+        functools.partial(collect_kernel, pieces, devices),
+        out_shape=jax.ShapeDtypeStruct((devices, 8, BLOCK), F32),
+        compiler_params=pltpu.CompilerParams(vmem_limit_bytes=VMEM_LIMIT),
+        name="collect_vectors",
+    )(*vectors)
+
+
+MESH = pl.DeviceIdType.MESH
+
+
+def when(condition, body):
+    if condition is True:
+        body()
+    else:
+        pl.when(condition)(body)
+
+
+class Place:
+    def __init__(self, planes):
+        along = lax.axis_index("dp")
+        self.planes = planes
+        self.y = lax.axis_index("inner")
+        self.c = lax.rem(along, 2)
+        self.x = lax.rem(lax.div(along, 2), 2)
+        self.z = lax.div(along, 4)
+
+    def device(self, z=None, x=None, c=None, y=None):
+        z = self.z if z is None else z
+        x = self.x if x is None else x
+        c = self.c if c is None else c
+        return ((z * 2 + x) * 2 + c, self.y if y is None else y)
+
+    @property
+    def above(self):
+        return self.device(z=lax.rem(self.z + 1, self.planes))
+
+    @property
+    def below(self):
+        return self.device(z=lax.rem(self.z + self.planes - 1, self.planes))
+
+    @property
+    def across(self):
+        return self.device(x=1 - self.x)
+
+    @property
+    def beside(self):
+        return self.device(y=1 - self.y)
+
+    @property
+    def partner(self):
+        return self.device(c=1 - self.c)
+
+    @property
+    def has_above(self):
+        return self.z < self.planes - 1
+
+    @property
+    def has_below(self):
+        return self.z > 0
+
+    def enter(self):
+        barrier = pltpu.get_barrier_semaphore()
+
+        def greet(device):
+            pl.semaphore_signal(barrier, inc=1, device_id=device, device_id_type=MESH)
+
+        for device in (self.across, self.beside, self.partner):
+            greet(device)
+        when(self.has_above, lambda: greet(self.above))
+        when(self.has_below, lambda: greet(self.below))
+        pl.semaphore_wait(
+            barrier, 3 + self.has_above.astype(jnp.int32) + self.has_below.astype(jnp.int32)
+        )
+
+
+def half_of(ref, half):
+    if half == 2:
+        return ref
+    width = ref.shape[-1] // 2
+    lead = (slice(None),) * (len(ref.shape) - 1)
+    return ref.at[lead + (slice(half * width, (half + 1) * width),)]
+
+
+SENDS = 64
+
+
+class Gather:
+    def __init__(self, place, index, shard, full, send, recv, local):
+        self.place, self.index, self.shard, self.full = place, index, shard, full
+        self.send, self.recv, self.local = send, recv, local
+        self.halves = (0, 1) if full.shape[-1] % (2 * BLOCK) == 0 else (2, None)
+        self.slot = 0
+        self.ends = []
+
+    def push(self, condition, item, half, device, source=None):
+        slot = self.slot
+        self.slot += 1
+        assert slot < SENDS
+
+        def make():
+            return pltpu.make_async_remote_copy(
+                src_ref=half_of(self.full.at[item] if source is None else source, half),
+                dst_ref=half_of(self.full.at[item], half),
+                send_sem=self.send.at[self.index, slot],
+                recv_sem=self.recv.at[(self.index,) + item + (min(half, 1),)],
+                device_id=device,
+                device_id_type=MESH,
+            )
+
+        when(condition, lambda: make().start())
+        self.ends.append((condition, make))
+
+    def await_item(self, item, half):
+        ref = half_of(self.full.at[item], half)
+        pltpu.make_async_remote_copy(
+            src_ref=ref, dst_ref=ref, send_sem=self.send.at[self.index, 0],
+            recv_sem=self.recv.at[(self.index,) + item + (min(half, 1),)],
+            device_id=self.place.partner, device_id_type=MESH,
+        ).wait_recv()
+
+    def own_copy(self):
+        p = self.place
+        return pltpu.make_async_copy(
+            self.shard, self.full.at[p.z, p.x, p.c, p.y], self.local.at[self.index]
+        )
+
+    def first(self):
+        p = self.place
+        item = (p.z, p.x, p.c, p.y)
+        self.push(p.has_above, item, 2, p.above, self.shard)
+        self.push(p.has_below, item, 2, p.below, self.shard)
+        self.push(True, item, 2, p.across, self.shard)
+        self.push(True, item, 2, p.beside, self.shard)
+        self.push(True, item, 2, p.partner, self.shard)
+        self.own_copy().start()
+
+    def planes_at(self, distance):
+        p = self.place
+        if distance == 0:
+            return [(True, p.z, None, None)]
+        return [
+            (p.z >= distance, p.z - distance, p.has_above, p.above),
+            (p.z + distance < p.planes, p.z + distance, p.has_below, p.below),
+        ]
+
+    def along_z(self, distance):
+        p = self.place
+        for there, z, more, onward in self.planes_at(distance):
+            item = (jnp.clip(z, 0, p.planes - 1), p.x, p.c, p.y)
+            when(there, lambda: self.await_item(item, 2))
+            self.push(jnp.logical_and(there, more), item, 2, onward)
+            for device in (p.across, p.beside, p.partner):
+                self.push(there, item, 2, device)
+
+    def across_xy(self, distance):
+        p = self.place
+        for there, z, _, _ in self.planes_at(distance):
+            z = jnp.clip(z, 0, p.planes - 1)
+            for half, item, onward in (
+                (self.halves[0], (z, 1 - p.x, p.c, p.y), p.beside),
+                (self.halves[1], (z, p.x, p.c, 1 - p.y), p.across),
+            ):
+                when(there, lambda: self.await_item(item, 2))
+                if half is not None:
+                    self.push(there, item, half, onward)
+                self.push(there, item, 2, p.partner)
+
+    def diagonal(self, distance):
+        p = self.place
+        for there, z, _, _ in self.planes_at(distance):
+            item = (jnp.clip(z, 0, p.planes - 1), 1 - p.x, p.c, 1 - p.y)
+
+            def arrive():
+                for half in self.halves:
+                    if half is not None:
+                        self.await_item(item, half)
+
+            when(there, arrive)
+            self.push(there, item, 2, p.partner)
+
+    def finish(self):
+        p = self.place
+        for z in range(p.planes):
+            for x in range(2):
+                for y in range(2):
+                    self.await_item((z, x, 1 - p.c, y), 2)
+        for condition, make in self.ends:
+            when(condition, lambda: make().wait_send())
+        self.own_copy().wait()
+
+
+def gather_kernel(planes, count, *refs):
+    shards, fulls = refs[:count], refs[count : 2 * count]
+    send, recv, local = refs[2 * count :]
+    place = Place(planes)
+    place.enter()
+    gathers = [
+        Gather(place, i, shards[i], fulls[i], send, recv, local) for i in range(count)
+    ]
+    for gather in gathers:
+        gather.first()
+    for distance in range(1, planes + 2):
+        for gather in gathers:
+            if distance < planes:
+                gather.along_z(distance)
+            if distance - 1 < planes:
+                gather.across_xy(distance - 1)
+            if distance >= 2:
+                gather.diagonal(distance - 2)
+    for gather in gathers:
+        gather.finish()
+
+
+def gather_all(planes, shards):
+    count = len(shards)
+    any_ = pl.BlockSpec(memory_space=pl.ANY)
+    fulls = pl.pallas_call(
+        functools.partial(gather_kernel, planes, count),
+        in_specs=[any_] * count,
+        out_specs=[any_] * count,
+        out_shape=[jax.ShapeDtypeStruct((planes, 2, 2, 2) + s.shape, s.dtype) for s in shards],
+        scratch_shapes=[
+            pltpu.SemaphoreType.DMA((count, SENDS)),
+            pltpu.SemaphoreType.DMA((count, planes, 2, 2, 2, 2)),
+            pltpu.SemaphoreType.DMA((count,)),
+        ],
+        compiler_params=pltpu.CompilerParams(collective_id=0, has_side_effects=True, vmem_limit_bytes=VMEM_LIMIT),
+        name="gather_weights",
+    )(*shards)
+    return [f.reshape((-1,) + f.shape[4:]) for f in fulls]
+
+
+class Scatter:
+    def __init__(self, place, index, source, out, bufs, send, recv, local):
+        self.place, self.index, self.source, self.out = place, index, source, out
+        self.held, self.from_partner, self.from_diag, self.from_side, self.from_z, self.spare = bufs
+        self.send, self.recv, self.local = send, recv, local
+        self.split = source.shape[-1] % (2 * BLOCK) == 0
+
+    def copy(self, slot, src, dst, device):
+        return pltpu.make_async_remote_copy(
+            src_ref=src, dst_ref=dst, send_sem=self.send.at[self.index, slot],
+            recv_sem=self.recv.at[self.index, slot], device_id=device, device_id_type=MESH,
+        )
+
+    def own_copy(self):
+        p = self.place
+        return pltpu.make_async_copy(self.source.at[:, :, p.c], self.held, self.local.at[self.index])
+
+    def partner_copy(self):
+        p = self.place
+        return self.copy(0, self.source.at[:, :, 1 - p.c], self.from_partner, p.partner)
+
+    def diag_copies(self):
+        p = self.place
+        ref = self.held.at[:, 1 - p.x, 1 - p.y]
+        if not self.split:
+            return [self.copy(1, ref, self.from_diag.at[0], p.across)]
+        return [
+            self.copy(1, half_of(ref, 0), self.from_diag.at[0], p.across),
+            self.copy(2, half_of(ref, 1), self.from_diag.at[1], p.beside),
+        ]
+
+    def side_copies(self):
+        p = self.place
+        return [
+            self.copy(3, self.held.at[:, 1 - p.x, p.y], self.from_side.at[0], p.across),
+            self.copy(4, self.held.at[:, p.x, 1 - p.y], self.from_side.at[1], p.beside),
+        ]
+
+    def z_copy(self, up, z):
+        p = self.place
+        return self.copy(
+            5 + up * p.planes + z, self.spare.at[z], self.from_z.at[up, z], p.above if up else p.below
+        )
+
+    def start(self):
+        self.own_copy().start()
+        self.partner_copy().start()
+
+    def add(self, x, y, *others):
+        def one(z, _):
+            total = self.held[z, x, y].astype(F32)
+            for other in others:
+                total = total + other(z).astype(F32)
+            self.held[z, x, y] = total.astype(self.held.dtype)
+            return 0
+
+        lax.fori_loop(0, self.place.planes, one, 0)
+
+    def after_partner(self):
+        p = self.place
+        self.own_copy().wait()
+        self.partner_copy().wait_recv()
+        for x, y in ((1 - p.x, 1 - p.y), (1 - p.x, p.y), (p.x, 1 - p.y), (p.x, p.y)):
+            self.add(x, y, lambda z: self.from_partner[z, x, y])
+            if x is not p.x and y is not p.y:
+                for copy in self.diag_copies():
+                    copy.start()
+
+    def after_diag(self):
+        p = self.place
+        width = self.held.shape[-1]
+        for copy in self.diag_copies():
+            copy.wait_recv()
+        parts = ((0, p.x, 1 - p.y, 0, width // 2), (1, 1 - p.x, p.y, width // 2, width))
+        if not self.split:
+            parts = ((0, p.x, 1 - p.y, 0, width),)
+
+        def one(z, _):
+            for index, x, y, low, high in parts:
+                total = self.held[z, x, y, :, low:high].astype(F32) + self.from_diag[index, z].astype(F32)
+                self.held[z, x, y, :, low:high] = total.astype(self.held.dtype)
+            return 0
+
+        lax.fori_loop(0, p.planes, one, 0)
+        for copy in self.side_copies():
+            copy.start()
+
+    def after_side(self):
+        p = self.place
+        for copy in self.side_copies():
+            copy.wait_recv()
+
+        def one(z, _):
+            total = self.held[z, p.x, p.y].astype(F32)
+            total = total + self.from_side[0, z].astype(F32) + self.from_side[1, z].astype(F32)
+            self.spare[z] = total.astype(self.spare.dtype)
+            return 0
+
+        lax.fori_loop(0, p.planes, one, 0)
+        for z in range(p.planes):
+            when(jnp.logical_and(jnp.logical_not(p.has_below), z > p.z), lambda: self.z_copy(1, z).start())
+            when(jnp.logical_and(jnp.logical_not(p.has_above), z < p.z), lambda: self.z_copy(0, z).start())
+
+    def along_z(self):
+        p = self.place
+        for z in range(p.planes):
+            def onward(up, z=z):
+                self.z_copy(up, z).wait_recv()
+                total = self.spare[z].astype(F32) + self.from_z[up, z].astype(F32)
+                self.spare[z] = total.astype(self.spare.dtype)
+                self.z_copy(up, z).start()
+
+            when(jnp.logical_and(jnp.logical_and(p.has_below, p.has_above), z > p.z), lambda: onward(1))
+            when(jnp.logical_and(jnp.logical_and(p.has_below, p.has_above), z < p.z), lambda: onward(0))
+
+    def finish(self, store):
+        p = self.place
+        store(self.spare[p.z].astype(F32), False)
+        for up, there in ((1, p.has_below), (0, p.has_above)):
+            def arrive(up=up):
+                self.z_copy(up, p.z).wait_recv()
+                store(self.from_z[up, p.z].astype(F32), True)
+
+            when(there, arrive)
+        self.partner_copy().wait_send()
+        for copy in self.diag_copies() + self.side_copies():
+            copy.wait_send()
+        for z in range(p.planes):
+            when(jnp.logical_and(z > p.z, p.has_above), lambda: self.z_copy(1, z).wait_send())
+            when(jnp.logical_and(z < p.z, p.has_below), lambda: self.z_copy(0, z).wait_send())
+
+
+def scatter_scratch(planes, rows, width, dtype):
+    split = width % (2 * BLOCK) == 0
+    return [
+        pltpu.VMEM((planes, 2, 2, rows, width), dtype),
+        pltpu.VMEM((planes, 2, 2, rows, width), dtype),
+        pltpu.VMEM((2 if split else 1, planes, rows, width // 2 if split else width), dtype),
+        pltpu.VMEM((2, planes, rows, width), dtype),
+        pltpu.VMEM((2, planes, rows, width), dtype),
+        pltpu.VMEM((planes, rows, width), dtype),
+    ]
+
+
+def scatter_kernel(planes, count, *refs):
+    sources, outs, rest = refs[:count], refs[count : 2 * count], refs[2 * count :]
+    send, recv, local = rest[:3]
+    place = Place(planes)
+    place.enter()
+    scatters = [
+        Scatter(place, i, sources[i], outs[i], rest[3 + 6 * i : 9 + 6 * i], send, recv, local)
+        for i in range(count)
+    ]
+    for s in scatters:
+        s.start()
+    for stage in ("after_partner", "after_diag", "after_side", "along_z"):
+        for s in scatters:
+            getattr(s, stage)()
+    for s in scatters:
+        def store(value, more, out=s.out):
+            if more:
+                out[...] += value
+            else:
+                out[...] = value
+
+        s.finish(store)
+
+
+def scatter_all(planes, sources):
+    count = len(sources)
+    sources = [s.reshape((planes, 2, 2, 2) + s.shape[1:]) for s in sources]
+    shapes = [s.shape[4:] for s in sources]
+    scratch = []
+    for s in sources:
+        scratch += scatter_scratch(planes, *s.shape[4:], s.dtype)
+    any_ = pl.BlockSpec(memory_space=pl.ANY)
+    vmem = pl.BlockSpec(memory_space=pltpu.VMEM)
+    return pl.pallas_call(
+        functools.partial(scatter_kernel, planes, count),
+        in_specs=[any_] * count,
+        out_specs=[vmem] * count,
+        out_shape=[jax.ShapeDtypeStruct(s, F32) for s in shapes],
+        scratch_shapes=[
+            pltpu.SemaphoreType.DMA((count, 5 + 2 * planes)),
+            pltpu.SemaphoreType.DMA((count, 5 + 2 * planes)),
+            pltpu.SemaphoreType.DMA((count,)),
+        ] + scratch,
+        compiler_params=pltpu.CompilerParams(collective_id=1, has_side_effects=True, vmem_limit_bytes=VMEM_LIMIT),
+        name="scatter_gradients",
+    )(*sources)
+
+
+def spread_masks(devices, piece):
+    size = devices * piece
+    column = lax.broadcasted_iota(jnp.int32, (devices, size), 1)
+    start = lax.broadcasted_iota(jnp.int32, (devices, size), 0) * piece
+    owner = jnp.logical_and(column >= start, column < start + piece)
+    column = lax.broadcasted_iota(jnp.int32, (BLOCK, size), 1)
+    number = jnp.floor((column.astype(F32) + 0.5) * (1.0 / piece)).astype(jnp.int32)
+    place = column - number * piece == lax.broadcasted_iota(jnp.int32, (BLOCK, size), 0)
+    return owner, place.astype(F32)
+
+
+def spread_kernel(pieces, gathered_ref, *outs):
+    devices = gathered_ref.shape[0]
+    masks = {piece: spread_masks(devices, piece) for piece in set(pieces)}
+    for index, piece in enumerate(pieces):
+        owner, place = masks[piece]
+        wide = dot_nn(gathered_ref[:, index, :].astype(F32), place)
+        outs[index][...] = jnp.sum(jnp.where(owner, wide, 0.0), axis=0, keepdims=True)
+
+
+def spread_vectors(gathered, pieces):
+    devices = gathered.shape[0]
+    return pl.pallas_call(
+        functools.partial(spread_kernel, pieces),
+        out_shape=[jax.ShapeDtypeStruct((1, devices * piece), F32) for piece in pieces],
+        compiler_params=pltpu.CompilerParams(vmem_limit_bytes=VMEM_LIMIT),
+        name="spread_vectors",
+    )(gathered)
+
+
+def collect_kernel(pieces, devices, *refs):
+    out_ref = refs[-1]
+    masks = {piece: spread_masks(devices, piece) for piece in set(pieces)}
+    for index, piece in enumerate(pieces):
+        owner, place = masks[piece]
+        wide = jnp.where(owner, refs[index][...], 0.0)
+        out_ref[:, index, :] = lax.dot_general(
+            wide, place, (((1,), (1,)), ((), ())),
+            precision=lax.Precision.HIGHEST, preferred_element_type=F32,
+        )
+
+
+def collect_vectors(vectors, pieces, devices):
+    return pl.pallas_call(
+        functools.partial(collect_kernel, pieces, devices),
+        out_shape=jax.ShapeDtypeStruct((devices, 8, BLOCK), F32),
+        compiler_params=pltpu.CompilerParams(vmem_limit_bytes=VMEM_LIMIT),
+        name="collect_vectors",
+    )(*vectors)
+
+
 AXES = ("dp", "inner")
 
 
 def shards(
+    planes,
     tokens, weight_qkv, bias_qv, weight_out, bias_out, gain_one, shift_one,
     weight_in, bias_in, weight_fin, bias_fin, gain_two, shift_two, segments, cotangent,
 ):
     vectors = (bias_qv, bias_out, gain_one, shift_one, bias_in, bias_fin, gain_two, shift_two)
-    sizes = [v.shape[0] for v in vectors]
-    joined = jnp.concatenate(vectors).reshape(1, -1)
-    joined = lax.all_gather(joined, AXES, axis=0, tiled=True).astype(F32)
-    rows, start = [], 0
-    for size in sizes:
-        rows.append(joined[:, start : start + size].reshape(1, -1))
-        start += size
-    full = [lax.all_gather(w, AXES, axis=0, tiled=True) for w in (weight_qkv, weight_out, weight_in, weight_fin)]
+    pieces = tuple(v.shape[0] for v in vectors)
+    joined = jnp.stack([jnp.pad(v, (0, BLOCK - v.shape[0])) for v in vectors])
+    local = [weight_qkv, weight_out, weight_in, weight_fin, joined]
+    if planes:
+        full = gather_all(planes, local)
+    else:
+        full = [lax.all_gather(w, AXES, axis=0) for w in local]
+    devices = full[0].shape[0]
+    rows = spread_vectors(full[4], pieces)
+    full = [f.reshape(-1, f.shape[2]) for f in full[:4]]
     out = layer(
         tokens, full[0], rows[0], full[1], rows[1], rows[2], rows[3],
         full[2], rows[4], full[3], rows[5], rows[6], rows[7], segments, cotangent,
     )
-    def scatter(grad, axis=0):
-        return lax.psum_scatter(grad, AXES, scatter_dimension=axis, tiled=True).astype(F32)
-
-    count = joined.shape[0]
-    order = (3, 5, 6, 7, 9, 11, 12, 13)
-    small = jnp.concatenate([out[i].reshape(count, -1) for i in order], axis=1)
-    small = lax.psum_scatter(small, AXES, scatter_dimension=0, tiled=True).reshape(-1)
-    parts, start = {}, 0
-    for index, size in zip(order, sizes):
-        parts[index] = small[start : start + size]
-        start += size
-    dwqkv = scatter(out[2], 1)
-    dwqkv = jnp.concatenate([dwqkv[0], dwqkv[1], dwqkv[2]], axis=1)
+    small = collect_vectors([out[i] for i in (3, 5, 6, 7, 9, 11, 12, 13)], pieces, devices)
+    large = [g.reshape(devices, -1, g.shape[1]) for g in (out[2], out[4], out[8], out[10])]
+    if planes:
+        sums = scatter_all(planes, large + [small])
+    else:
+        sums = [
+            lax.psum_scatter(g, AXES, scatter_dimension=0).astype(F32) for g in large + [small]
+        ]
+    parts = [sums[4][i, :piece] for i, piece in enumerate(pieces)]
+    dwqkv = sums[0].reshape(sums[0].shape[0], -1, 3, BLOCK).swapaxes(1, 2).reshape(sums[0].shape)
     return (
-        out[0], out[1], dwqkv, parts[3], scatter(out[4]), parts[5], parts[6], parts[7],
-        scatter(out[8]), parts[9], scatter(out[10]), parts[11], parts[12], parts[13],
+        out[0], out[1], dwqkv, parts[0], sums[1], parts[1], parts[2], parts[3],
+        sums[2], parts[4], sums[3], parts[5], parts[6], parts[7],
     )
 
 
@@ -535,4 +2402,8 @@
     row, vec = P(AXES, None), P(AXES)
     in_specs = (row, row, vec, row, vec, vec, vec, row, vec, row, vec, vec, vec, row, row)
     out_specs = (row, row, row, vec, row, vec, vec, vec, row, vec, row, vec, vec, vec)
-    return jax.shard_map(shards, mesh=mesh, in_specs=in_specs, out_specs=out_specs, check_vma=False)
+    planes = mesh.shape["dp"] // 4 if mesh.shape["inner"] == 2 and mesh.shape["dp"] == 16 else 0
+    return jax.shard_map(
+        functools.partial(shards, planes),
+        mesh=mesh, in_specs=in_specs, out_specs=out_specs, check_vma=False,
+    )

time: 821 us -> 468 us (0.57)
  waiting for transfers between devices: 444 us -> 0 us
  Pallas kernels: 249 us -> 437 us
  blocking collectives: 82.3 us -> 0 us
  between operations: 14.3 us -> 1.15 us
    reduce_scatter x3 -> x0, waiting for transfers between devices: 221 us -> none  [scatter(): lax.psum_scatter(grad, AXES, scatter_dimension=axis, tiled=True).astype(F32)]
    pallas_call x0 -> x4, Pallas kernels: none -> 188 us  [the longest x1 110 us: scatter_all(): pl.pallas_call(functools.partial(scatter_kernel, planes, count), in_specs...]
    all_gather x4 -> x0, waiting for transfers between devices: 144 us -> none  [shards(): lax.all_gather(w, AXES, axis=0, tiled=True)]
    unnamed x2 -> x0, blocking collectives: 82.3 us -> none
    unnamed x9 -> x0, waiting for transfers between devices: 79.5 us -> none
  transfers between devices with their start and end apart: 8 -> 0, of which waited for: 7 -> 0; matrix products, arithmetic and copies ran while one was open for 3% -> 0% of each run, Pallas kernels for 15% -> 0%
where the time goes in v2:
time: 468 us; the launch traced here: 462 us
  Pallas kernels  437 us (93%)
  local copies, waits for them, and re-layouts  22.9 us (5%)
    pallas_call x1, Pallas kernels, scatter_all(): pl.pallas_call(functools.partial(scatter_kernel, planes, count), in_specs...  110 us
    pallas_call x1, Pallas kernels, attention_backward(): pl.pallas_call(attention_back_kernel, grid=(pairs,), in_specs=[part(total...  70.5 us
    pallas_call x1, Pallas kernels, gather_all(): pl.pallas_call(functools.partial(gather_kernel, planes, count), in_specs=...  69.8 us
    pallas_call x1, Pallas kernels, feed_forward(): pl.pallas_call(feed_kernel, grid=(tokens // tile,), in_specs=[rows, rows,...  55.8 us
    pallas_call x1, Pallas kernels, attention_forward(): pl.pallas_call(attention_kernel, grid=(count,), in_specs=[rows, pl.BlockS...  54.2 us
    pallas_call x1, Pallas kernels, feed_backward(): pl.pallas_call(feed_back_kernel, grid=(hidden // chunk,), in_specs=[whole...  53.6 us
    pallas_call x1, Pallas kernels, project_backward(): pl.pallas_call(project_back_kernel, grid=(tokens // tile,), in_specs=[row...  14.7 us

profile of v2, /device:TPU:0, one launch (start us, length us, event | category | flops | bytes accessed | tf_op | source)
XLA Modules:
  0.0 462.0 jit_solution(4730212913448471943)
XLA Ops:
  4.0 1.3 reshape.46.segment_ref
  5.3 69.8 %gather_weights.1 = (bf16[4,2,2,2,24,2304]{5,4,3,2,1,0:T(8,128)(2,1)}, bf16[4,2,2,2,24,768]{5,4,3,2,1,0:T(8,128)(2,1)}, bf16[4,2,2,2,24,3072]{5,4,3,2,1,0:T(8,12...) custom-call(bf16[24,2304]{1,0:T(8,128)(2,1)} %refs_0_.1, bf16[24,768]{1,0:T(8,128)(2,1)} %refs_1_.1, ...), custom_call_target="tpu_custom_call" | custom-call | tf_op jit(solution)/shard_map/gather_weights/pallas_call | solution.py:2103
  75.1 2.3 spread_vectors.1
  77.4 0.7 fusion.3
  78.7 1.4 concatenate.11.vec_ref
  80.1 54.2 %attention_forward.1 = (bf16[2048,2304]{1,0:T(8,128)(2,1)}, bf16[2048,768]{1,0:T(8,128)(2,1)}, f32[4,24,256]{2,1,0:T(8,128)}, f32[2048,768]{1,0:T(8,128)}, f32[2048,128]{1,0:T(8,128)}) custom-call(bf16[2048,768]{1,0:T(8,128)(2,1)} %tokens_ref.3, s32[4,1,512]{2,1,0:T(1,128)} %reshape.46.segment_ref, bf16[768,2304]{1,0:T(8,128)(2,1)} %bitcast.47, ...), custom_call_target="tpu_custom_call" | custom-call | tf_op jit(solution)/shard_map/attention_forward/pallas_call | solution.py:156
  134.3 55.8 %feed_forward.1 = (bf16[2048,768]{1,0:T(8,128)(2,1)}, bf16[2048,3072]{1,0:T(8,128)(2,1)}, bf16[2048,3072]{1,0:T(8,128)(2,1)}, f32[2048,768]{1,0:T(8,128)}, bf16[...) custom-call(f32[2048,768]{1,0:T(8,128)} %get-tuple-element.60.normed_ref, ...), custom_call_target="tpu_custom_call" | custom-call | tf_op jit(solution)/shard_map/feed_forward/pallas_call | solution.py:230
  190.1 1.4 fusion.1
  191.6 53.6 %feed_backward.1 = (bf16[768,3072]{1,0:T(8,128)(2,1)}, bf16[3072,768]{1,0:T(8,128)(2,1)}, f32[8,3072]{1,0:T(8,128)}, f32[2048,768]{1,0:T(8,128)}) custom-call(bf16[2048,768]{1,0:T(8,128)(2,1)} %get-tuple-element.71.gffn_ref, bf16[2048,768]{1,0:T(8,128)(2,1)} %get-tuple-element.72.low_ref, f32[2048,768]{1,0:T(8,128)} %get-tuple-element.73.gsum_hbm, ...), custom_call_target="tpu_custom_call" | custom-call | tf_op jit(solution)/shard_map/feed_backward/pallas_call | solution.py:285
  245.2 14.7 %project_backward.1 = (f32[2048,768]{1,0:T(8,128)}, bf16[2048,768]{1,0:T(8,128)(2,1)}, bf16[768,768]{1,0:T(8,128)(2,1)}, f32[8,768]{1,0:T(8,128)}) custom-call(f32[2048,768]{1,0:T(8,128)} %get-tuple-element.76.ghid_ref, f32[2048,768]{1,0:T(8,128)} %get-tuple-element.60.normed_ref, f32[2048,128]{1,0:T(8,128)} %get-tuple-element.77.inverse_ref, ...), custom_call_target="tpu_custom_call" | custom-call | tf_op jit(solution)/shard_map/project_backward/pallas_call | solution.py:348
  259.9 70.5 %attention_backward.1 = (bf16[768,2304]{1,0:T(8,128)(2,1)}, f32[8,768]{1,0:T(8,128)}, f32[2048,768]{1,0:T(8,128)}) custom-call(bf16[2048,2304]{1,0:T(8,128)(2,1)} %get-tuple-element.70.q_ref.k_ref.v_ref, bf16[2048,2304]{1,0:T(8,128)(2,1)} %get-tuple-element.70.q_ref.k_ref.v_ref, bf16[2048,2304]{1,0:T(8,128)(2,1)} %get-tuple-element.70.q_ref.k_ref.v_ref, ...), custom_call_target="tpu_custom_call" | custom-call | tf_op jit(solution)/shard_map/attention_backward/pallas_call | solution.py:436
  330.5 0.7 slice_bitcast_fusion
  331.8 1.5 fusion.2
  333.3 1.5 slice.60.refs_4_
  334.8 6.1 %collect_vectors.1 = f32[32,8,128]{2,1,0:T(8,128)} custom-call(f32[1,1536]{1,0:T(1,128)} %bitcast.64, f32[1,768]{1,0:T(1,128)} %get-tuple-element.101.refs_1_, f32[1,768]{1,0:T(1,128)} %get-tuple-element.100.refs_2_, f32[1,768]{1,0:T(1,128)} %get-tuple-element.99.refs_3_, f32[1,3072]{1,0:T(1,128)} %slice.60.refs_4_, f32[1,768]{1,0:T(1,128)} %get-tuple-element.98.refs_5_, ...), custom_call_target="tpu_custom_call" | custom-call | tf_op jit(solution)/shard_map/collect_vectors/pallas_call | solution.py:2354
  340.9 110.1 %scatter_gradients.1 = (f32[24,2304]{1,0:T(8,128)}, f32[24,768]{1,0:T(8,128)}, f32[24,3072]{1,0:T(8,128)}, f32[96,768]{1,0:T(8,128)}, f32[8,128]{1,0:T(8,128)}) custom-call(bf16[4,2,2,2,24,2304]{5,4,3,2,1,0:T(8,128)(2,1)} %bitcast.59, bf16[4,2,2,2,24,768]{5,4,3,2,1,0:T(8,128)(2,1)} %bitcast.60, bf16[4,2,2,2,24,3072]{5,4,3,2,1,0:T(8,128)(2,1)} %bitcast.57, ...), custom_call_target="tpu_custom_call" | custom-call | tf_op jit(solution)/shard_map/scatter_gradients/pallas_call | solution.py:2296
  451.0 1.2 slice_bitcast_fusion.4
  452.2 1.2 slice_bitcast_fusion.8
  453.4 1.4 slice_bitcast_fusion.1
  454.8 1.0 reshape.50
  455.9 0.7 reshape.51
  456.7 1.5 copy.35
  458.2 1.7 copy.36
  459.9 1.7 copy.37
  (11 shorter events, 4.6 us)

commit v3 on v1

--- a/solution.py
+++ b/solution.py
@@ -106,21 +106,496 @@
     return (pre * cdf, cdf + pre * (bell * 0.3989422804014327))
 
 
-def attention_kernel(
-    tokens_ref, segment_ref, wqkv_ref, wout_ref, bqkv_ref, bout_ref,
-    qkv_ref, context_ref, lse_ref, normed_ref, inverse_ref, mask_ref,
-):
+MESH = pl.DeviceIdType.MESH
+
+
+def when(condition, body):
+    if condition is True:
+        body()
+    else:
+        pl.when(condition)(body)
+
+
+class Place:
+    def __init__(self, planes):
+        along = lax.axis_index("dp")
+        self.planes = planes
+        self.y = lax.axis_index("inner")
+        self.c = lax.rem(along, 2)
+        self.x = lax.rem(lax.div(along, 2), 2)
+        self.z = lax.div(along, 4)
+
+    def device(self, z=None, x=None, c=None, y=None):
+        z = self.z if z is None else z
+        x = self.x if x is None else x
+        c = self.c if c is None else c
+        return ((z * 2 + x) * 2 + c, self.y if y is None else y)
+
+    @property
+    def above(self):
+        return self.device(z=jnp.minimum(self.z + 1, self.planes - 1))
+
+    @property
+    def below(self):
+        return self.device(z=jnp.maximum(self.z - 1, 0))
+
+    @property
+    def across(self):
+        return self.device(x=1 - self.x)
+
+    @property
+    def beside(self):
+        return self.device(y=1 - self.y)
+
+    @property
+    def partner(self):
+        return self.device(c=1 - self.c)
+
+    @property
+    def has_above(self):
+        return self.z < self.planes - 1
+
+    @property
+    def has_below(self):
+        return self.z > 0
+
+    def enter(self):
+        barrier = pltpu.get_barrier_semaphore()
+
+        def greet(device):
+            pl.semaphore_signal(barrier, inc=1, device_id=device, device_id_type=MESH)
+
+        for device in (self.across, self.beside, self.partner):
+            greet(device)
+        when(self.has_above, lambda: greet(self.above))
+        when(self.has_below, lambda: greet(self.below))
+        pl.semaphore_wait(
+            barrier, 3 + self.has_above.astype(jnp.int32) + self.has_below.astype(jnp.int32)
+        )
+
+
+def half_of(ref, half):
+    if half == 2:
+        return ref
+    width = ref.shape[-1] // 2
+    lead = (slice(None),) * (len(ref.shape) - 1)
+    return ref.at[lead + (slice(half * width, (half + 1) * width),)]
+
+
+SENDS = 64
+
+
+class Gather:
+    def __init__(self, place, index, shard, full, send, recv, local):
+        self.place, self.index, self.shard, self.full = place, index, shard, full
+        self.send, self.recv, self.local = send, recv, local
+        self.rows = shard.shape[0]
+        self.halves = (0, 1) if full.shape[-1] % (2 * BLOCK) == 0 else (2, None)
+        self.slot = 0
+        self.draining = False
+        self.log = []
+
+    def entry(self, z, x, c, y):
+        device = ((z * 2 + x) * 2 + c) * 2 + y
+        return self.full.at[pl.ds(pl.multiple_of(device * self.rows, 8), self.rows)]
+
+    def run(self, name, *args):
+        self.log.append((name, args))
+        getattr(self, name)(*args)
+
+    def push(self, condition, item, half, device, source=None):
+        slot = self.slot
+        self.slot += 1
+        assert slot < SENDS
+
+        def make():
+            return pltpu.make_async_remote_copy(
+                src_ref=half_of(self.entry(*item) if source is None else source, half),
+                dst_ref=half_of(self.entry(*item), half),
+                send_sem=self.send.at[self.index, slot],
+                recv_sem=self.recv.at[(self.index,) + item + (min(half, 1),)],
+                device_id=device,
+                device_id_type=MESH,
+            )
+
+        if self.draining:
+            when(condition, lambda: make().wait_send())
+        else:
+            when(condition, lambda: make().start())
+
+    def await_item(self, item, half):
+        if self.draining:
+            return
+        ref = half_of(self.entry(*item), half)
+        pltpu.make_async_remote_copy(
+            src_ref=ref, dst_ref=ref, send_sem=self.send.at[self.index, 0],
+            recv_sem=self.recv.at[(self.index,) + item + (min(half, 1),)],
+            device_id=self.place.partner, device_id_type=MESH,
+        ).wait_recv()
+
+    def own_copy(self):
+        p = self.place
+        return pltpu.make_async_copy(
+            self.shard, self.entry(p.z, p.x, p.c, p.y), self.local.at[self.index]
+        )
+
+    def first_z(self):
+        p = self.place
+        item = (p.z, p.x, p.c, p.y)
+        self.push(p.has_above, item, 2, p.above, self.shard)
+        self.push(p.has_below, item, 2, p.below, self.shard)
+        if not self.draining:
+            self.own_copy().start()
+
+    def first_xy(self):
+        p = self.place
+        item = (p.z, p.x, p.c, p.y)
+        for device in (p.across, p.beside, p.partner):
+            self.push(True, item, 2, device, self.shard)
+
+    def planes_at(self, distance):
+        p = self.place
+        if distance == 0:
+            return [(True, p.z, None, None)]
+        return [
+            (p.z >= distance, p.z - distance, p.has_above, p.above),
+            (p.z + distance < p.planes, p.z + distance, p.has_below, p.below),
+        ]
+
+    def along_z(self, distance):
+        p = self.place
+        for there, z, more, onward in self.planes_at(distance):
+            item = (jnp.clip(z, 0, p.planes - 1), p.x, p.c, p.y)
+            if not self.draining:
+                when(there, lambda: self.await_item(item, 2))
+            self.push(jnp.logical_and(there, more), item, 2, onward)
+            for device in (p.across, p.beside, p.partner):
+                self.push(there, item, 2, device)
+
+    def across_xy(self, distance):
+        p = self.place
+        for there, z, _, _ in self.planes_at(distance):
+            z = jnp.clip(z, 0, p.planes - 1)
+            for half, item, onward in (
+                (self.halves[0], (z, 1 - p.x, p.c, p.y), p.beside),
+                (self.halves[1], (z, p.x, p.c, 1 - p.y), p.across),
+            ):
+                if not self.draining:
+                    when(there, lambda: self.await_item(item, 2))
+                if half is not None:
+                    self.push(there, item, half, onward)
+                self.push(there, item, 2, p.partner)
+
+    def diagonal(self, distance):
+        p = self.place
+        for there, z, _, _ in self.planes_at(distance):
+            item = (jnp.clip(z, 0, p.planes - 1), 1 - p.x, p.c, 1 - p.y)
+
+            def arrive():
+                for half in self.halves:
+                    if half is not None:
+                        self.await_item(item, half)
+
+            if not self.draining:
+                when(there, arrive)
+            self.push(there, item, 2, p.partner)
+
+    def finish(self):
+        p = self.place
+        for z in range(p.planes):
+            for x in range(2):
+                for y in range(2):
+                    self.await_item((z, x, 1 - p.c, y), 2)
+        self.own_copy().wait()
+        self.draining, self.slot = True, 0
+        for name, args in self.log:
+            getattr(self, name)(*args)
+
+
+class Scatter:
+    def __init__(self, place, index, source, held, bufs, sems, store, via=None):
+        self.place, self.index, self.source, self.via, self.store = place, index, source, via, store
+        self.held = source.at[:, :, place.c] if held is None else held
+        self.loads = held is not None
+        self.from_partner, self.from_diag, self.from_side, self.from_z, self.spare = bufs
+        self.send, self.recv, self.local = sems
+        self.dtype = source.dtype
+
+    def copy(self, slot, src, dst, device):
+        return pltpu.make_async_remote_copy(
+            src_ref=src, dst_ref=dst, send_sem=self.send.at[self.index, slot],
+            recv_sem=self.recv.at[self.index, slot], device_id=device, device_id_type=MESH,
+        )
+
+    def own_copy(self):
+        return pltpu.make_async_copy(
+            self.source.at[:, :, self.place.c], self.held, self.local.at[self.index]
+        )
+
+    def partner_copy(self):
+        p = self.place
+        return self.copy(0, self.source.at[:, :, 1 - p.c], self.from_partner, p.partner)
+
+    def diag_copies(self):
+        p = self.place
+        ref = self.held.at[:, 1 - p.x, 1 - p.y]
+        if self.via is not None:
+            return [self.copy(1, ref, self.from_diag.at[0], p.beside if self.via else p.across)]
+        return [
+            self.copy(1, half_of(ref, 0), self.from_diag.at[0], p.across),
+            self.copy(2, half_of(ref, 1), self.from_diag.at[1], p.beside),
+        ]
+
+    def side_copies(self):
+        p = self.place
+        return [
+            self.copy(3, self.held.at[:, 1 - p.x, p.y], self.from_side.at[0], p.across),
+            self.copy(4, self.held.at[:, p.x, 1 - p.y], self.from_side.at[1], p.beside),
+        ]
+
+    def z_copy(self, up, z):
+        p = self.place
+        return self.copy(
+            5 + up * p.planes + z, self.spare.at[z], self.from_z.at[up, z], p.above if up else p.below
+        )
+
+    def start(self):
+        if self.loads:
+            self.own_copy().start()
+        self.partner_copy().start()
+
+    def after_partner(self):
+        p = self.place
+        if self.loads:
+            self.own_copy().wait()
+        self.partner_copy().wait_recv()
+
+        def add(x, y):
+            def one(z, _):
+                total = self.held[z, x, y].astype(F32) + self.from_partner[z, x, y].astype(F32)
+                self.held[z, x, y] = total.astype(self.dtype)
+                return 0
+
+            lax.fori_loop(0, p.planes, one, 0)
+
+        add(1 - p.x, 1 - p.y)
+        for copy in self.diag_copies():
+            copy.start()
+        add(1 - p.x, p.y)
+        add(p.x, 1 - p.y)
+        add(p.x, p.y)
+
+    def after_diag(self):
+        p = self.place
+        width = self.source.shape[-1]
+        for copy in self.diag_copies():
+            copy.wait_recv()
+        if self.via is None:
+            parts = ((0, p.x, 1 - p.y, 0, width // 2), (1, 1 - p.x, p.y, width // 2, width))
+        elif self.via:
+            parts = ((0, 1 - p.x, p.y, 0, width),)
+        else:
+            parts = ((0, p.x, 1 - p.y, 0, width),)
+
+        def one(z, _):
+            for index, x, y, low, high in parts:
+                total = self.held[z, x, y, :, low:high].astype(F32) + self.from_diag[index, z].astype(F32)
+                self.held[z, x, y, :, low:high] = total.astype(self.dtype)
+            return 0
+
+        lax.fori_loop(0, p.planes, one, 0)
+        for copy in self.side_copies():
+            copy.start()
+
+    def after_side(self):
+        p = self.place
+        for copy in self.side_copies():
+            copy.wait_recv()
+
+        def one(z, _):
+            total = self.held[z, p.x, p.y].astype(F32)
+            total = total + self.from_side[0, z].astype(F32) + self.from_side[1, z].astype(F32)
+            self.spare[z] = total.astype(self.dtype)
+            return 0
+
+        lax.fori_loop(0, p.planes, one, 0)
+        for z in range(p.planes):
+            when(jnp.logical_and(jnp.logical_not(p.has_below), z > p.z), lambda: self.z_copy(1, z).start())
+            when(jnp.logical_and(jnp.logical_not(p.has_above), z < p.z), lambda: self.z_copy(0, z).start())
+
+    def along_z(self):
+        p = self.place
+        inside = jnp.logical_and(p.has_below, p.has_above)
+        for z in range(p.planes):
+            def onward(up, z=z):
+                self.z_copy(up, z).wait_recv()
+                total = self.spare[z].astype(F32) + self.from_z[up, z].astype(F32)
+                self.spare[z] = total.astype(self.dtype)
+                self.z_copy(up, z).start()
+
+            when(jnp.logical_and(inside, z > p.z), lambda: onward(1))
+            when(jnp.logical_and(inside, z < p.z), lambda: onward(0))
+
+    def finish(self):
+        p = self.place
+        self.store(self.spare[p.z].astype(F32), False)
+        for up, there in ((1, p.has_below), (0, p.has_above)):
+            def arrive(up=up):
+                self.z_copy(up, p.z).wait_recv()
+                self.store(self.from_z[up, p.z].astype(F32), True)
+
+            when(there, arrive)
+        self.partner_copy().wait_send()
+        for copy in self.diag_copies() + self.side_copies():
+            copy.wait_send()
+        for z in range(p.planes):
+            when(jnp.logical_and(z > p.z, p.has_above), lambda: self.z_copy(1, z).wait_send())
+            when(jnp.logical_and(z < p.z, p.has_below), lambda: self.z_copy(0, z).wait_send())
+
+
+STAGES = ("start", "after_partner", "after_diag", "after_side", "along_z", "finish")
+
+
+def scatter_scratch(planes, rows, width, dtype, held, via):
+    return ([pltpu.VMEM((planes, 2, 2, rows, width), dtype)] if held else []) + [
+        pltpu.VMEM((planes, 2, 2, rows, width), dtype),
+        pltpu.VMEM((2, planes, rows, width // 2) if via is None else (1, planes, rows, width), dtype),
+        pltpu.VMEM((2, planes, rows, width), dtype),
+        pltpu.VMEM((2, planes, rows, width), dtype),
+        pltpu.VMEM((planes, rows, width), dtype),
+    ]
+
+
+def store_to(out, cols=None, rows=None):
+    def store(value, more):
+        index = (slice(None) if rows is None else rows, slice(None) if cols is None else cols)
+        out[index] = out[index] + value if more else value
+
+    return store
+
+
+def spread_masks(devices, piece):
+    size = devices * piece
+    column = lax.broadcasted_iota(jnp.int32, (devices, size), 1)
+    start = lax.broadcasted_iota(jnp.int32, (devices, size), 0) * piece
+    owner = jnp.logical_and(column >= start, column < start + piece)
+    column = lax.broadcasted_iota(jnp.int32, (BLOCK, size), 1)
+    number = jnp.floor((column.astype(F32) + 0.5) * (1.0 / piece)).astype(jnp.int32)
+    place = column - number * piece == lax.broadcasted_iota(jnp.int32, (BLOCK, size), 0)
+    return owner, place.astype(F32)
+
+
+def spread_vectors(gathered, pieces):
+    masks = {piece: spread_masks(gathered.shape[0], piece) for piece in set(pieces)}
+    rows = []
+    for index, piece in enumerate(pieces):
+        owner, place = masks[piece]
+        wide = dot_nn(gathered[:, index, :], place.astype(BF16))
+        rows.append(jnp.sum(jnp.where(owner, wide, 0.0), axis=0, keepdims=True))
+    return rows
+
+
+def collect_vector(row, piece, devices):
+    owner, place = spread_masks(devices, piece)
+    wide = jnp.where(owner, row, 0.0)
+    high = wide.astype(BF16)
+    low = (wide - high.astype(F32)).astype(BF16)
+    place = place.astype(BF16)
+    return dot_nt(high, place) + dot_nt(low, place)
+
+
+OUT_TICKS = (
+    (0, "along_z", 1), (0, "across_xy", 0), (0, "along_z", 2), (1, "across_xy", 1), (1, "diagonal", 0),
+    (1, "along_z", 3), (2, "across_xy", 2), (2, "diagonal", 1), (3, "across_xy", 3), (3, "diagonal", 2),
+    (4, "diagonal", 3),
+)
+FEED_TICKS = (
+    (0, "first_xy"), (0, "along_z", 1), (2, "along_z", 2), (4, "across_xy", 0), (5, "along_z", 3),
+    (8, "diagonal", 0), (9, "across_xy", 1), (13, "diagonal", 1), (14, "across_xy", 2),
+    (18, "diagonal", 2), (18, "across_xy", 3), (22, "diagonal", 3),
+)
+
+
+def attention_kernel(planes, pieces, tokens_ref, segment_ref, *refs):
+    shards, refs = refs[:5], refs[5:]
+    if planes:
+        fulls, refs = refs[:5], refs[5:]
+    else:
+        fulls = shards
+    (
+        qkv_ref, context_ref, lse_ref, normed_ref, inverse_ref, vectors_ref, bin_ref,
+        wqkv_ref, wout_ref, small_ref, bias_ref, mask_ref, load_sem, *sems,
+    ) = refs
     length, width = tokens_ref.shape
-    fill_masks(mask_ref, 0, segment_ref[0])
+    count = pl.num_programs(0)
+    step = pl.program_id(0)
+    pairs = width // BLOCK
     offsets, _ = mask_offsets(length)
+    gathers = []
+    if planes:
+        place = Place(planes)
+        gathers = [Gather(place, i, shards[i], fulls[i], *sems) for i in range(5)]
+    attn, out, feed = gathers[:2], gathers[2:3], gathers[3:]
+
+    def load(index, ref):
+        return pltpu.make_async_copy(fulls[index], ref, load_sem.at[index])
+
+    @pl.when(step == 0)
+    def _():
+        if planes:
+            place.enter()
+            for gather in attn + out:
+                gather.run("first_z")
+                gather.run("first_xy")
+            for gather in feed:
+                gather.run("first_z")
+        for seq in range(segment_ref.shape[0]):
+            fill_masks(mask_ref, seq, segment_ref[seq])
+        for distance in range(1, planes + 2 if planes else 0):
+            for gather in attn:
+                if distance < planes:
+                    gather.run("along_z", distance)
+                if distance - 1 < planes:
+                    gather.run("across_xy", distance - 1)
+                if distance >= 2:
+                    gather.run("diagonal", distance - 2)
+        for gather in attn:
+            gather.finish()
+        load(0, wqkv_ref).start()
+        load(1, small_ref).start()
+        load(1, small_ref).wait()
+        small = small_ref[...].astype(F32).reshape(-1, 8, BLOCK)
+        bqv, bout, gain_one, shift_one, bin_, bfin, gain_two, shift_two = spread_vectors(small, pieces)
+        bias_ref[:, :width] = bqv[:, :width]
+        bias_ref[:, width : 2 * width] = jnp.zeros_like(bout)
+        bias_ref[:, 2 * width : 3 * width] = bqv[:, width:]
+        bias_ref[:, 3 * width :] = bout
+        bin_ref[...] = bin_
+        for row, vector in enumerate((gain_one, shift_one, bfin, gain_two, shift_two)):
+            vectors_ref[row : row + 1] = vector
+        vectors_ref[5:8] = jnp.zeros((3, width), F32)
+        load(0, wqkv_ref).wait()
+
+    due = {}
+    for group, ticks in ((out, OUT_TICKS), (feed, FEED_TICKS)):
+        for number, name, *args in ticks:
+            for gather in group:
+                due.setdefault(number, []).append(functools.partial(gather.run, name, *args))
+
     for part in range(3):
         cols = slice(part * width, (part + 1) * width)
-        joined = dot_nn(tokens_ref[...], wqkv_ref[:, cols]) + bqkv_ref[:, cols]
+        joined = dot_nn(tokens_ref[...], wqkv_ref[:, cols]) + bias_ref[:, cols]
         if part == 0:
             joined = joined * HEAD_DIM ** (-0.5)
         qkv_ref[:, cols] = joined.astype(BF16)
 
     def one_pair(pair, _):
+        for number, acts in due.items():
+            @pl.when(step * pairs + pair == number)
+            def _():
+                for act in acts:
+                    act()
+
         def cols(part):
             return pl.ds(pl.multiple_of(part * width + pair * BLOCK, BLOCK), BLOCK)
 
@@ -128,7 +603,7 @@
             here = slice(block * BLOCK, (block + 1) * BLOCK)
             query = stacked(qkv_ref[here, cols(0)])
             scores = dot_nt(qkv_ref[low:high, cols(1)], query)
-            scores = scores + twice(mask_ref[0, pl.ds(offsets[block], high - low), :])
+            scores = scores + twice(mask_ref[step, pl.ds(offsets[block], high - low), :])
             maxima = jnp.max(scores, axis=0, keepdims=True)
             exponent = jnp.exp(scores - maxima)
             totals = jnp.sum(exponent, axis=0, keepdims=True)
@@ -137,51 +612,84 @@
             lse_ref[0, pl.ds(pair * (length // BLOCK) + block, 1), :] = maxima + jnp.log(totals)
         return 0
 
-    lax.fori_loop(0, width // BLOCK, one_pair, 0)
-    branch = dot_nn(context_ref[...], wout_ref[...]) + bout_ref[...]
+    lax.fori_loop(0, pairs, one_pair, 0)
+
+    @pl.when(step == 0)
+    def _():
+        for gather in out:
+            gather.finish()
+        load(2, wout_ref).start()
+        load(2, wout_ref).wait()
+
+    branch = dot_nn(context_ref[...], wout_ref[...]) + bias_ref[:, 3 * width :]
     normed, inverse = normalize(tokens_ref[...].astype(F32) + branch)
     normed_ref[...] = normed
     inverse_ref[...] = jnp.broadcast_to(inverse, inverse_ref.shape)
 
+    @pl.when(step == count - 1)
+    def _():
+        for gather in feed:
+            gather.finish()
+
 
 def whole(shape):
     return pl.BlockSpec(shape, lambda *_: (0,) * len(shape), pipeline_mode=pl.Buffered(1))
 
 
-def attention_forward(tokens, segments, wqkv, wout, bqkv, bout):
+def attention_forward(planes, tokens, segments, weights, pieces):
     count, length = segments.shape[0], segments.shape[2]
     width = tokens.shape[1]
     rows = pl.BlockSpec((length, width), lambda i: (i, 0))
+    any_ = pl.BlockSpec(memory_space=pl.ANY)
     lse_rows = (width // BLOCK) * (length // BLOCK)
-    return pl.pallas_call(
-        attention_kernel,
+    hidden = weights[3].shape[-1]
+    devices = planes * 8 if planes else weights[1].shape[0] // 8
+    gathered = [(devices * w.shape[0], w.shape[1]) for w in weights] if planes else []
+    sems = []
+    if planes:
+        sems = [
+            pltpu.SemaphoreType.DMA((5, SENDS)),
+            pltpu.SemaphoreType.DMA((5, planes, 2, 2, 2, 2)),
+            pltpu.SemaphoreType.DMA((5,)),
+        ]
+    out = pl.pallas_call(
+        functools.partial(attention_kernel, planes, pieces),
         grid=(count,),
-        in_specs=[
-            rows,
-            pl.BlockSpec((1, 1, length), lambda i: (i, 0, 0)),
-            whole(wqkv.shape),
-            whole(wout.shape),
-            whole(bqkv.shape),
-            whole(bout.shape),
-        ],
-        out_specs=[
+        in_specs=[rows, whole(segments.shape)] + [whole(w.shape) if planes else any_ for w in weights],
+        out_specs=[any_] * len(gathered) + [
             pl.BlockSpec((length, 3 * width), lambda i: (i, 0)),
             rows,
             pl.BlockSpec((1, lse_rows, 2 * BLOCK), lambda i: (i, 0, 0)),
             rows,
             pl.BlockSpec((length, BLOCK), lambda i: (i, 0)),
+            whole((8, width)),
+            whole((1, hidden)),
         ],
-        out_shape=[
+        out_shape=[jax.ShapeDtypeStruct(s, w.dtype) for s, w in zip(gathered, weights)] + [
             jax.ShapeDtypeStruct((count * length, 3 * width), BF16),
             jax.ShapeDtypeStruct((count * length, width), BF16),
             jax.ShapeDtypeStruct((count, lse_rows, 2 * BLOCK), F32),
             jax.ShapeDtypeStruct((count * length, width), F32),
             jax.ShapeDtypeStruct((count * length, BLOCK), F32),
+            jax.ShapeDtypeStruct((8, width), F32),
+            jax.ShapeDtypeStruct((1, hidden), F32),
         ],
-        scratch_shapes=[pltpu.VMEM((1, mask_offsets(length)[1], BLOCK), F32)],
-        compiler_params=pltpu.CompilerParams(vmem_limit_bytes=VMEM_LIMIT),
+        scratch_shapes=[
+            pltpu.VMEM((width, 3 * width), BF16),
+            pltpu.VMEM((width, width), BF16),
+            pltpu.VMEM((devices * 8, BLOCK), BF16),
+            pltpu.VMEM((1, 4 * width), F32),
+            pltpu.VMEM((count, mask_offsets(length)[1], BLOCK), F32),
+            pltpu.SemaphoreType.DMA((3,)),
+        ] + sems,
+        compiler_params=pltpu.CompilerParams(
+            vmem_limit_bytes=VMEM_LIMIT,
+            **(dict(collective_id=0, has_side_effects=True) if planes else {}),
+        ),
         name="attention_forward",
-    )(tokens, segments, wqkv, wout, bqkv, bout)
+    )(tokens, segments, *weights)
+    fulls = out[: len(gathered)] if planes else weights
+    return fulls, out[len(gathered) :]
 
 
 def feed_kernel(
@@ -330,7 +838,7 @@
     normed = normed_ref[...]
     gvec_ref[0:1] += column_sum(ghid * normed)
     gvec_ref[1:2] += column_sum(ghid)
-    gsum = normalize_back(ghid * gain_ref[...], normed, inverse_ref[:, 0:1])
+    gsum = normalize_back(ghid * gain_ref[0:1], normed, inverse_ref[:, 0:1])
     gsum_ref[...] = gsum
     gattn = gsum.astype(BF16)
     gvec_ref[2:3] += column_sum(gattn.astype(F32))
@@ -365,27 +873,99 @@
     )(ghid, normed, inverse, context, wout, gain)
 
 
+FEED_STEPS = ((0, 2, 4, 7, 8, 11), (0, 5, 8, 11, 12, 15), (1, 9, 12, 15, 16, 19), (5, 13, 16, 19, 20, 23))
+OUT_STEPS = (0, 1, 3, 6, 7, 10)
+PAIR_STEPS = (0, 1, 2, 3, 5, 7)
+
+
 def attention_back_kernel(
+    planes, pieces, devices,
     q_ref, k_ref, v_ref, gcon_ref, lse_ref, segment_ref, tokens_ref, wq_ref, wk_ref, wv_ref, gsum_hbm,
-    dw_ref, gvec_ref, gtok_hbm,
-    tokens_t_ref, acc_ref, mask_ref, grad_ref, dk_ref, dv_ref, sem,
+    gtwo_ref, gbin_ref, gone_ref, *refs,
 ):
+    sources, refs = refs[: 3 if planes else 0], refs[3 if planes else 0 :]
+    gtok_hbm, refs = refs[0], refs[1:]
+    if planes:
+        outs, refs = refs[:5], refs[5:]
+    else:
+        dw_ref, small_ref, refs = refs[0], refs[1], refs[2:]
+    tokens_t_ref, acc_ref, mask_ref, grad_ref, dk_ref, dv_ref, gbqv_ref, sem, *refs = refs
     pair = pl.program_id(0)
+    last = pl.num_programs(0) - 1
     count, length = segment_ref.shape[0], segment_ref.shape[2]
+    total, width = tokens_ref.shape
+    pairs = width // BLOCK
     blocks = length // BLOCK
     offsets, _ = mask_offsets(length)
     tile = 512
+    due, late = {}, []
+
+    if planes:
+        place = Place(planes)
+        sems, (pair_dw_ref, small_ref), refs = refs[:3], refs[3:5], refs[5:]
+        scatters = []
+
+        def scatter(source, load, store, steps, via=None):
+            nonlocal refs
+            size = 6 if load else 5
+            bufs, refs = refs[:size], refs[size:]
+            held, bufs = (bufs[0], bufs[1:]) if load else (None, bufs)
+            one = Scatter(place, len(scatters), source, held, bufs, sems, store, via)
+            scatters.append(one)
+            for stage, number in zip(STAGES, steps):
+                if number < count * pairs:
+                    due.setdefault(number, []).append(getattr(one, stage))
+                else:
+                    late.append((number, len(scatters), getattr(one, stage)))
+
+        dwin, dwfin, dwout = sources
+        half, wide = dwfin.shape[4] // 2, dwin.shape[5] // 2
+        lead = (slice(None),) * 4
+        for i in range(2):
+            rows = slice(i * half, (i + 1) * half)
+            scatter(dwfin.at[lead + (rows,)], True, store_to(outs[3], rows=rows), FEED_STEPS[i])
+        for i in range(2):
+            cols = slice(i * wide, (i + 1) * wide)
+            scatter(dwin.at[lead + (slice(None), cols)], True, store_to(outs[2], cols=cols), FEED_STEPS[2 + i])
+        scatter(dwout, True, store_to(outs[1]), OUT_STEPS)
+        for i in range(pairs):
+            def store(value, more, i=i):
+                for part in range(3):
+                    cols = slice(part * BLOCK, (part + 1) * BLOCK)
+                    here = slice(part * width + i * BLOCK, part * width + (i + 1) * BLOCK)
+                    store_to(outs[0], cols=here)(value[:, cols], more)
+
+            scatter(
+                pair_dw_ref.at[i], False, store, [count * (i + 1) + n for n in PAIR_STEPS], via=i % 2
+            )
+        scatter(
+            small_ref.reshape(planes, 2, 2, 2, 8, BLOCK), False, store_to(outs[4]),
+            [count * pairs + n for n in PAIR_STEPS], via=0,
+        )
 
     @pl.when(pair == 0)
     def _():
         copy = pltpu.make_async_copy(gsum_hbm, acc_ref, sem)
         copy.start()
+        if planes:
+            place.enter()
         tokens_t_ref[...] = jnp.transpose(tokens_ref[...])
         for seq in range(count):
             fill_masks(mask_ref, seq, segment_ref[seq])
+        for index, row in (
+            (1, gone_ref[2:3]), (2, gone_ref[0:1]), (3, gone_ref[1:2]), (4, gbin_ref[0:1]),
+            (5, gtwo_ref[2:3]), (6, gtwo_ref[0:1]), (7, gtwo_ref[1:2]),
+        ):
+            small_ref[:, index, :] = collect_vector(row, pieces[index], devices)
         copy.wait()
 
     def one_seq(seq, _):
+        for number, acts in due.items():
+            @pl.when(pair * count + seq == number)
+            def _():
+                for act in acts:
+                    act()
+
         base = pl.multiple_of(seq * length, length)
         dk_ref[...] = jnp.zeros_like(dk_ref)
         dv_ref[...] = jnp.zeros_like(dv_ref)
@@ -410,23 +990,32 @@
         return 0
 
     lax.fori_loop(0, count, one_seq, 0)
-    gvec_ref[...] = jnp.zeros_like(gvec_ref)
-    gvec_ref[0:1] = column_sum(grad_ref[:, :BLOCK].astype(F32))
-    gvec_ref[1:2] = column_sum(grad_ref[:, 2 * BLOCK :].astype(F32))
+    cols = pl.multiple_of(pair * BLOCK, BLOCK)
+    gbqv_ref[:, pl.ds(cols, BLOCK)] = column_sum(grad_ref[:, :BLOCK].astype(F32))
+    gbqv_ref[:, pl.ds(width + cols, BLOCK)] = column_sum(grad_ref[:, 2 * BLOCK :].astype(F32))
+    dw = dot_nn(tokens_t_ref[...], grad_ref[...])
+    if planes:
+        for part in range(3):
+            here = slice(part * BLOCK, (part + 1) * BLOCK)
+            pair_dw_ref[pair, ..., here] = dw[:, here].reshape(planes, 2, 2, 2, -1, BLOCK).astype(BF16)
+    else:
+        dw_ref[...] = dw.astype(BF16)
     weights = jnp.concatenate([wq_ref[...], wk_ref[...], wv_ref[...]], axis=1)
-    for start in range(0, acc_ref.shape[0], tile):
+    for start in range(0, total, tile):
         here = slice(start, start + tile)
         acc_ref[here] += dot_nt(grad_ref[here], weights)
-    dw = dot_nn(tokens_t_ref[...], grad_ref[...]).astype(BF16)
-    for part in range(3):
-        dw_ref[part] = dw[:, part * BLOCK : (part + 1) * BLOCK]
-
-    @pl.when(pair == pl.num_programs(0) - 1)
+
+    @pl.when(pair == last)
     def _():
-        pltpu.sync_copy(acc_ref, gtok_hbm)
-
-
-def attention_backward(qkv, gcon, lse, segments, tokens, wqkv, gsum):
+        copy = pltpu.make_async_copy(acc_ref, gtok_hbm, sem)
+        copy.start()
+        small_ref[:, 0, :] = collect_vector(gbqv_ref[...], pieces[0], devices)
+        for _, _, act in sorted(late, key=lambda entry: entry[:2]):
+            act()
+        copy.wait()
+
+
+def attention_backward(planes, pieces, devices, qkv, gcon, lse, segments, tokens, wqkv, gsum, vectors, grads):
     count, length = segments.shape[0], segments.shape[2]
     total, width = tokens.shape
     pairs = width // BLOCK
@@ -435,104 +1024,107 @@
     def part(rows, index):
         return pl.BlockSpec((rows, BLOCK), lambda i: (0, index * pairs + i))
 
+    scratch = [
+        pltpu.VMEM((width, total), BF16),
+        pltpu.VMEM((total, width), F32),
+        pltpu.VMEM((count, mask_offsets(length)[1], BLOCK), F32),
+        pltpu.VMEM((total, 3 * BLOCK), BF16),
+        pltpu.VMEM((length, BLOCK), F32),
+        pltpu.VMEM((length, BLOCK), F32),
+        pltpu.VMEM((1, 2 * width), F32),
+        pltpu.SemaphoreType.DMA,
+    ]
+    small = (devices, 8, BLOCK)
+    if planes:
+        grads = [g.reshape((planes, 2, 2, 2, -1) + g.shape[1:]) for g in grads]
+        rows = width // devices
+        shards = [(rows, 3 * width)] + [grads[i].shape[4:] for i in (2, 0, 1)] + [(8, BLOCK)]
+        outs = [whole(shape) for shape in shards]
+        out_shape = [jax.ShapeDtypeStruct(shape, F32) for shape in shards]
+        number = 6 + pairs
+        scratch += [
+            pltpu.SemaphoreType.DMA((number, 5 + 2 * planes)),
+            pltpu.SemaphoreType.DMA((number, 5 + 2 * planes)),
+            pltpu.SemaphoreType.DMA((number,)),
+            pltpu.VMEM((pairs, planes, 2, 2, 2, rows, 3 * BLOCK), BF16),
+            pltpu.VMEM(small, F32),
+        ]
+        for shape in [(grads[1].shape[4] // 2, width)] * 2 + [(rows, grads[0].shape[5] // 2)] * 2 + [(rows, width)]:
+            scratch += scatter_scratch(planes, *shape, BF16, True, None)
+        for _ in range(pairs):
+            scratch += scatter_scratch(planes, rows, 3 * BLOCK, BF16, False, 0)
+        scratch += scatter_scratch(planes, 8, BLOCK, F32, False, 0)
+    else:
+        grads = []
+        outs = [pl.BlockSpec((width, 3 * BLOCK), lambda i: (0, i)), whole(small)]
+        out_shape = [jax.ShapeDtypeStruct((width, 3 * width), BF16), jax.ShapeDtypeStruct(small, F32)]
     return pl.pallas_call(
-        attention_back_kernel,
+        functools.partial(attention_back_kernel, planes, pieces, devices),
         grid=(pairs,),
         in_specs=[
             part(total, 0), part(total, 1), part(total, 2), part(total, 0),
             whole(lse.shape), whole(segments.shape), whole(tokens.shape),
             part(width, 0), part(width, 1), part(width, 2), any_,
-        ],
-        out_specs=[
-            pl.BlockSpec((3, width, BLOCK), lambda i: (0, 0, i)),
-            pl.BlockSpec((8, BLOCK), lambda i: (0, i)),
-            any_,
-        ],
-        out_shape=[
-            jax.ShapeDtypeStruct((3, width, width), BF16),
-            jax.ShapeDtypeStruct((8, width), F32),
-            jax.ShapeDtypeStruct((total, width), F32),
-        ],
-        scratch_shapes=[
-            pltpu.VMEM((width, total), BF16),
-            pltpu.VMEM((total, width), F32),
-            pltpu.VMEM((count, mask_offsets(length)[1], BLOCK), F32),
-            pltpu.VMEM((total, 3 * BLOCK), BF16),
-            pltpu.VMEM((length, BLOCK), F32),
-            pltpu.VMEM((length, BLOCK), F32),
-            pltpu.SemaphoreType.DMA,
-        ],
-        compiler_params=pltpu.CompilerParams(vmem_limit_bytes=VMEM_LIMIT),
+        ] + [whole(v.shape) for v in vectors] + [any_] * len(grads),
+        out_specs=[any_] + outs,
+        out_shape=[jax.ShapeDtypeStruct((total, width), F32)] + out_shape,
+        scratch_shapes=scratch,
+        compiler_params=pltpu.CompilerParams(
+            vmem_limit_bytes=VMEM_LIMIT,
+            **(dict(collective_id=1, has_side_effects=True) if planes else {}),
+        ),
         name="attention_backward",
-    )(qkv, qkv, qkv, gcon, lse, segments, tokens, wqkv, wqkv, wqkv, gsum)
-
-
-def layer(
-    tokens, wqkv, bqv, wout, bout, gain_one, shift_one,
-    win, bin_, wfin, bfin, gain_two, shift_two, segments, cotangent,
-):
-    width = tokens.shape[1]
-    length = segments.shape[1]
-    segments = segments.reshape(segments.shape[0], 1, length)
-    bqkv = jnp.concatenate([bqv[:, :width], jnp.zeros_like(bout), bqv[:, width:]], axis=1)
-    qkv, context, lse, normed, inverse = attention_forward(tokens, segments, wqkv, wout, bqkv, bout)
-    zero = jnp.zeros_like(bfin)
-    vectors = jnp.concatenate([gain_one, shift_one, bfin, gain_two, shift_two, zero, zero, zero], axis=0)
-    output, act, slope, gsum_two, gffn, low, gvec_two = feed_forward(
-        normed, cotangent, win, wfin, vectors, bin_, min(512, tokens.shape[0])
-    )
-    dwin, dwfin, gbin, ghid = feed_backward(gffn, low, gsum_two, act, slope, win, wfin, 512)
-    gsum_one, gcon, dwout, gvec_one = project_backward(
-        ghid, normed, inverse, context, wout, gain_one, min(512, tokens.shape[0])
-    )
-    dwqkv, gvec_qv, gtok = attention_backward(qkv, gcon, lse, segments, tokens, wqkv, gsum_one)
-    return (
-        output, gtok, dwqkv, gvec_qv[0:2].reshape(1, -1), dwout, gvec_one[2:3], gvec_one[0:1], gvec_one[1:2],
-        dwin, gbin[0:1], dwfin, gvec_two[2:3], gvec_two[0:1], gvec_two[1:2],
-    )
-
-
-AXES = ("dp", "inner")
+    )(qkv, qkv, qkv, gcon, lse, segments, tokens, wqkv, wqkv, wqkv, gsum, *vectors, *grads)
 
 
 def shards(
+    planes,
     tokens, weight_qkv, bias_qv, weight_out, bias_out, gain_one, shift_one,
     weight_in, bias_in, weight_fin, bias_fin, gain_two, shift_two, segments, cotangent,
 ):
-    vectors = (bias_qv, bias_out, gain_one, shift_one, bias_in, bias_fin, gain_two, shift_two)
-    sizes = [v.shape[0] for v in vectors]
-    joined = jnp.concatenate(vectors).reshape(1, -1)
-    joined = lax.all_gather(joined, AXES, axis=0, tiled=True).astype(F32)
-    rows, start = [], 0
-    for size in sizes:
-        rows.append(joined[:, start : start + size].reshape(1, -1))
-        start += size
-    full = [lax.all_gather(w, AXES, axis=0, tiled=True) for w in (weight_qkv, weight_out, weight_in, weight_fin)]
-    out = layer(
-        tokens, full[0], rows[0], full[1], rows[1], rows[2], rows[3],
-        full[2], rows[4], full[3], rows[5], rows[6], rows[7], segments, cotangent,
+    small = (bias_qv, bias_out, gain_one, shift_one, bias_in, bias_fin, gain_two, shift_two)
+    pieces = tuple(v.shape[0] for v in small)
+    joined = jnp.stack([jnp.pad(v, (0, BLOCK - v.shape[0])) for v in small])
+    weights = [weight_qkv, joined, weight_out, weight_in, weight_fin]
+    if not planes:
+        weights = [lax.all_gather(w, AXES, axis=0, tiled=True) for w in weights]
+    devices = planes * 8 if planes else weights[1].shape[0] // 8
+    segments = segments.reshape(segments.shape[0], 1, segments.shape[1])
+    fulls, rest = attention_forward(planes, tokens, segments, weights, pieces)
+    wqkv, _, wout, win, wfin = fulls
+    qkv, context, lse, normed, inverse, vectors, bin_ = rest
+    tile = min(512, tokens.shape[0])
+    output, act, slope, gsum_two, gffn, low, gvec_two = feed_forward(
+        normed, cotangent, win, wfin, vectors, bin_, tile
     )
-    def scatter(grad, axis=0):
-        return lax.psum_scatter(grad, AXES, scatter_dimension=axis, tiled=True).astype(F32)
-
-    count = joined.shape[0]
-    order = (3, 5, 6, 7, 9, 11, 12, 13)
-    small = jnp.concatenate([out[i].reshape(count, -1) for i in order], axis=1)
-    small = lax.psum_scatter(small, AXES, scatter_dimension=0, tiled=True).reshape(-1)
-    parts, start = {}, 0
-    for index, size in zip(order, sizes):
-        parts[index] = small[start : start + size]
-        start += size
-    dwqkv = scatter(out[2], 1)
-    dwqkv = jnp.concatenate([dwqkv[0], dwqkv[1], dwqkv[2]], axis=1)
+    dwin, dwfin, gbin, ghid = feed_backward(gffn, low, gsum_two, act, slope, win, wfin, 512)
+    gsum_one, gcon, dwout, gvec_one = project_backward(ghid, normed, inverse, context, wout, vectors, tile)
+    gtok, *sums = attention_backward(
+        planes, pieces, devices, qkv, gcon, lse, segments, tokens, wqkv, gsum_one,
+        (gvec_two, gbin, gvec_one), [dwin, dwfin, dwout],
+    )
+    if not planes:
+        sums = [
+            lax.psum_scatter(g.reshape((devices, -1) + g.shape[-1:]), AXES, scatter_dimension=0).astype(F32)
+            for g in (sums[0], dwout, dwin, dwfin, sums[1])
+        ]
+        sums[0] = sums[0].reshape(sums[0].shape[0], -1, 3, BLOCK).swapaxes(1, 2).reshape(sums[0].shape)
+    parts = [sums[4][i, :piece] for i, piece in enumerate(pieces)]
     return (
-        out[0], out[1], dwqkv, parts[3], scatter(out[4]), parts[5], parts[6], parts[7],
-        scatter(out[8]), parts[9], scatter(out[10]), parts[11], parts[12], parts[13],
+        output, gtok, sums[0], parts[0], sums[1], parts[1], parts[2], parts[3],
+        sums[2], parts[4], sums[3], parts[5], parts[6], parts[7],
     )
+
+
+AXES = ("dp", "inner")
 
 
 def solution(mesh):
     row, vec = P(AXES, None), P(AXES)
     in_specs = (row, row, vec, row, vec, vec, vec, row, vec, row, vec, vec, vec, row, row)
     out_specs = (row, row, row, vec, row, vec, vec, vec, row, vec, row, vec, vec, vec)
-    return jax.shard_map(shards, mesh=mesh, in_specs=in_specs, out_specs=out_specs, check_vma=False)
+    planes = mesh.shape["dp"] // 4 if mesh.shape["inner"] == 2 and mesh.shape["dp"] == 16 else 0
+    return jax.shard_map(
+        functools.partial(shards, planes),
+        mesh=mesh, in_specs=in_specs, out_specs=out_specs, check_vma=False,
+    )

time: 821 us -> 468 us (0.57)
  waiting for transfers between devices: 444 us -> 0 us
  Pallas kernels: 249 us -> 442 us
  blocking collectives: 82.3 us -> 0 us
  between operations: 14.3 us -> 0.89 us
    reduce_scatter x3 -> x0, waiting for transfers between devices: 221 us -> none  [scatter(): lax.psum_scatter(grad, AXES, scatter_dimension=axis, tiled=True).astype(F32)]
    pallas_call x2, Pallas kernels: 125 us -> 317 us  [the longest x1 196 us: attention_backward(): pl.pallas_call(functools.partial(attention_back_kernel, planes, pieces, d...]
    all_gather x4 -> x0, waiting for transfers between devices: 144 us -> none  [shards(): lax.all_gather(w, AXES, axis=0, tiled=True)]
    unnamed x2 -> x0, blocking collectives: 82.3 us -> none
    unnamed x9 -> x0, waiting for transfers between devices: 79.5 us -> none
  transfers between devices with their start and end apart: 8 -> 0, of which waited for: 7 -> 0; matrix products, arithmetic and copies ran while one was open for 3% -> 0% of each run, Pallas kernels for 15% -> 0%
where the time goes in v3:
time: 468 us; the launch traced here: 460 us
  Pallas kernels  442 us (94%)
  local copies, waits for them, and re-layouts  17.2 us (4%)
    pallas_call x1, Pallas kernels, attention_backward(): pl.pallas_call(functools.partial(attention_back_kernel, planes, pieces, d...  196 us
    pallas_call x1, Pallas kernels, attention_forward(): pl.pallas_call(functools.partial(attention_kernel, planes, pieces), grid=...  121 us
    pallas_call x1, Pallas kernels, feed_forward(): pl.pallas_call(feed_kernel, grid=(tokens // tile,), in_specs=[rows, rows,...  56 us
    pallas_call x1, Pallas kernels, feed_backward(): pl.pallas_call(feed_back_kernel, grid=(hidden // chunk,), in_specs=[whole...  53.5 us
    pallas_call x1, Pallas kernels, project_backward(): pl.pallas_call(project_back_kernel, grid=(tokens // tile,), in_specs=[row...  14.6 us

profile of v3, /device:TPU:0, one launch (start us, length us, event | category | flops | bytes accessed | tf_op | source)
XLA Modules:
  0.0 459.6 jit_solution(16520629839677100299)
XLA Ops:
  0.6 0.7 pad_bitcast_fusion.6
  1.3 0.7 pad_bitcast_fusion.4
  2.0 0.7 pad_bitcast_fusion.2
  2.7 0.7 pad_bitcast_fusion
  3.4 0.6 stack.35.refs_1_
  4.0 1.3 reshape.40.segment_ref
  5.3 121.0 %attention_forward.1 = (bf16[768,2304]{1,0:T(8,128)(2,1)}, bf16[256,128]{1,0:T(8,128)(2,1)}, bf16[768,768]{1,0:T(8,128)(2,1)}, bf16[768,3072]{1,0:T(8,128)(2,1)}...) custom-call(bf16[2048,768]{1,0:T(8,128)(2,1)} %tokens_ref.3, ...), custom_call_target="tpu_custom_call" | custom-call | tf_op jit(solution)/shard_map/attention_forward/pallas_call | solution.py:655
  126.3 56.0 %feed_forward.1 = (bf16[2048,768]{1,0:T(8,128)(2,1)}, bf16[2048,3072]{1,0:T(8,128)(2,1)}, bf16[2048,3072]{1,0:T(8,128)(2,1)}, f32[2048,768]{1,0:T(8,128)}, bf16[...) custom-call(f32[2048,768]{1,0:T(8,128)} %get-tuple-element.46.normed_ref, ...), custom_call_target="tpu_custom_call" | custom-call | tf_op jit(solution)/shard_map/feed_forward/pallas_call | solution.py:738
  182.3 53.5 %feed_backward.1 = (bf16[768,3072]{1,0:T(8,128)(2,1)}, bf16[3072,768]{1,0:T(8,128)(2,1)}, f32[8,3072]{1,0:T(8,128)}, f32[2048,768]{1,0:T(8,128)}) custom-call(bf16[2048,768]{1,0:T(8,128)(2,1)} %get-tuple-element.53.gffn_ref, bf16[2048,768]{1,0:T(8,128)(2,1)} %get-tuple-element.54.low_ref, f32[2048,768]{1,0:T(8,128)} %get-tuple-element.55.gsum_hbm, ...), custom_call_target="tpu_custom_call" | custom-call | tf_op jit(solution)/shard_map/feed_backward/pallas_call | solution.py:793
  235.8 14.6 %project_backward.1 = (f32[2048,768]{1,0:T(8,128)}, bf16[2048,768]{1,0:T(8,128)(2,1)}, bf16[768,768]{1,0:T(8,128)(2,1)}, f32[8,768]{1,0:T(8,128)}) custom-call(f32[2048,768]{1,0:T(8,128)} %get-tuple-element.58.ghid_ref, f32[2048,768]{1,0:T(8,128)} %get-tuple-element.46.normed_ref, f32[2048,128]{1,0:T(8,128)} %get-tuple-element.59.inverse_ref, ...), custom_call_target="tpu_custom_call" | custom-call | tf_op jit(solution)/shard_map/project_backward/pallas_call | solution.py:856
  250.4 196.4 %attention_backward.1 = (f32[2048,768]{1,0:T(8,128)}, f32[24,2304]{1,0:T(8,128)}, f32[24,768]{1,0:T(8,128)}, f32[24,3072]{1,0:T(8,128)}, f32[96,768]{1,0:T(8,128)}, /*index=5*/f32[8,128]{1,0:T(8,128)}) custom-call(bf16[2048,2304]{1,0:T(8,128)(2,1)} %get-tuple-element.52.q_ref.k_ref.v_ref, bf16[2048,2304]{1,0:T(8,128)(2,1)} %get-tuple-element.52.q_ref.k_ref.v_ref, ...), custom_call_target="tpu_custom_call" | custom-call | tf_op jit(solution)/shard_map/attention_backward/pallas_call | solution.py:1061
  446.8 1.2 slice_bitcast_fusion.3
  448.0 1.2 slice_bitcast_fusion.7
  449.2 1.4 slice_bitcast_fusion
  450.6 0.0 copy-start.1
  450.7 0.0 copy-start
  450.7 6.0 %copy.34 = f32[2048,768]{1,0:T(8,128)} copy(f32[2048,768]{1,0:T(8,128)} %get-tuple-element.107) | data formatting | bytes 12582912
  456.6 0.0 copy-done.2
  456.6 0.7 copy.35
  457.3 0.0 copy-done.3
  457.3 0.6 copy.36
  458.0 0.0 copy-done.1
  458.0 0.7 copy.37
  458.7 0.7 copy.38
  (3 shorter events, 0.0 us)
Async XLA Ops:
  450.6 6.0 %copy-start.2 = (f32[24,2304]{1,0:T(8,128)S(1)}, f32[24,2304]{1,0:T(8,128)}, u32[]{:S(2)}) copy-start(f32[24,2304]{1,0:T(8,128)} %get-tuple-element.108) | copy-start | bytes 663556
  450.6 6.7 %copy-start.3 = (f32[24,768]{1,0:T(8,128)S(1)}, f32[24,768]{1,0:T(8,128)}, u32[]{:S(2)}) copy-start(f32[24,768]{1,0:T(8,128)} %get-tuple-element.110) | copy-start | bytes 221188
  450.6 7.3 %copy-start.1 = (f32[24,3072]{1,0:T(8,128)S(1)}, f32[24,3072]{1,0:T(8,128)}, u32[]{:S(2)}) copy-start(f32[24,3072]{1,0:T(8,128)} %get-tuple-element.114) | copy-start | bytes 884740
  450.7 8.0 %copy-start = (f32[96,768]{1,0:T(8,128)S(1)}, f32[96,768]{1,0:T(8,128)}, u32[]{:S(2)}) copy-start(f32[96,768]{1,0:T(8,128)} %get-tuple-element.116) | copy-start | bytes 884740

commit v4 on v3

--- a/solution.py
+++ b/solution.py
@@ -159,19 +159,17 @@
     def has_below(self):
         return self.z > 0
 
+    @property
+    def diagonal(self):
+        return self.device(x=1 - self.x, y=1 - self.y)
+
     def enter(self):
         barrier = pltpu.get_barrier_semaphore()
-
-        def greet(device):
+        planes = [self.device(z=lax.rem(self.z + i, self.planes)) for i in range(1, self.planes)]
+        devices = [self.across, self.beside, self.diagonal, self.partner] + planes
+        for device in devices:
             pl.semaphore_signal(barrier, inc=1, device_id=device, device_id_type=MESH)
-
-        for device in (self.across, self.beside, self.partner):
-            greet(device)
-        when(self.has_above, lambda: greet(self.above))
-        when(self.has_below, lambda: greet(self.below))
-        pl.semaphore_wait(
-            barrier, 3 + self.has_above.astype(jnp.int32) + self.has_below.astype(jnp.int32)
-        )
+        pl.semaphore_wait(barrier, len(devices))
 
 
 def half_of(ref, half):
@@ -313,18 +311,19 @@
 
 
 class Scatter:
-    def __init__(self, place, index, source, held, bufs, sems, store, via=None):
-        self.place, self.index, self.source, self.via, self.store = place, index, source, via, store
+    def __init__(self, place, index, source, held, bufs, sems, store):
+        self.place, self.index, self.source, self.store = place, index, source, store
         self.held = source.at[:, :, place.c] if held is None else held
         self.loads = held is not None
-        self.from_partner, self.from_diag, self.from_side, self.from_z, self.spare = bufs
+        self.from_partner, self.from_square, self.spare, self.from_z = bufs
         self.send, self.recv, self.local = sems
         self.dtype = source.dtype
 
-    def copy(self, slot, src, dst, device):
+    def copy(self, slot, src, dst, device, arrival=None):
         return pltpu.make_async_remote_copy(
             src_ref=src, dst_ref=dst, send_sem=self.send.at[self.index, slot],
-            recv_sem=self.recv.at[self.index, slot], device_id=device, device_id_type=MESH,
+            recv_sem=self.recv.at[self.index, slot if arrival is None else arrival],
+            device_id=device, device_id_type=MESH,
         )
 
     def own_copy(self):
@@ -336,28 +335,23 @@
         p = self.place
         return self.copy(0, self.source.at[:, :, 1 - p.c], self.from_partner, p.partner)
 
-    def diag_copies(self):
-        p = self.place
-        ref = self.held.at[:, 1 - p.x, 1 - p.y]
-        if self.via is not None:
-            return [self.copy(1, ref, self.from_diag.at[0], p.beside if self.via else p.across)]
+    def square(self):
+        p = self.place
+        return ((1 - p.x, 1 - p.y, p.diagonal), (1 - p.x, p.y, p.across), (p.x, 1 - p.y, p.beside))
+
+    def square_copies(self):
         return [
-            self.copy(1, half_of(ref, 0), self.from_diag.at[0], p.across),
-            self.copy(2, half_of(ref, 1), self.from_diag.at[1], p.beside),
+            self.copy(1 + i, self.held.at[:, x, y], self.from_square.at[i], device)
+            for i, (x, y, device) in enumerate(self.square())
         ]
 
-    def side_copies(self):
-        p = self.place
-        return [
-            self.copy(3, self.held.at[:, 1 - p.x, p.y], self.from_side.at[0], p.across),
-            self.copy(4, self.held.at[:, p.x, 1 - p.y], self.from_side.at[1], p.beside),
-        ]
-
-    def z_copy(self, up, z):
-        p = self.place
-        return self.copy(
-            5 + up * p.planes + z, self.spare.at[z], self.from_z.at[up, z], p.above if up else p.below
-        )
+    def z_copy(self, z):
+        p = self.place
+        return self.copy(4 + z, self.spare.at[z], self.from_z.at[p.z], p.device(z=z), 4 + p.z)
+
+    def z_arrival(self, z):
+        p = self.place
+        return self.copy(4 + z, self.spare.at[z], self.from_z.at[z], p.device(z=z), 4 + z)
 
     def start(self):
         if self.loads:
@@ -378,92 +372,90 @@
 
             lax.fori_loop(0, p.planes, one, 0)
 
-        add(1 - p.x, 1 - p.y)
-        for copy in self.diag_copies():
+        for (x, y, _), copy in zip(self.square(), self.square_copies()):
+            add(x, y)
             copy.start()
-        add(1 - p.x, p.y)
-        add(p.x, 1 - p.y)
         add(p.x, p.y)
 
-    def after_diag(self):
-        p = self.place
-        width = self.source.shape[-1]
-        for copy in self.diag_copies():
-            copy.wait_recv()
-        if self.via is None:
-            parts = ((0, p.x, 1 - p.y, 0, width // 2), (1, 1 - p.x, p.y, width // 2, width))
-        elif self.via:
-            parts = ((0, 1 - p.x, p.y, 0, width),)
-        else:
-            parts = ((0, p.x, 1 - p.y, 0, width),)
-
-        def one(z, _):
-            for index, x, y, low, high in parts:
-                total = self.held[z, x, y, :, low:high].astype(F32) + self.from_diag[index, z].astype(F32)
-                self.held[z, x, y, :, low:high] = total.astype(self.dtype)
-            return 0
-
-        lax.fori_loop(0, p.planes, one, 0)
-        for copy in self.side_copies():
-            copy.start()
-
-    def after_side(self):
-        p = self.place
-        for copy in self.side_copies():
+    def after_square(self):
+        p = self.place
+        for copy in self.square_copies():
             copy.wait_recv()
 
         def one(z, _):
             total = self.held[z, p.x, p.y].astype(F32)
-            total = total + self.from_side[0, z].astype(F32) + self.from_side[1, z].astype(F32)
+            for i in range(3):
+                total = total + self.from_square[i, z].astype(F32)
             self.spare[z] = total.astype(self.dtype)
             return 0
 
         lax.fori_loop(0, p.planes, one, 0)
         for z in range(p.planes):
-            when(jnp.logical_and(jnp.logical_not(p.has_below), z > p.z), lambda: self.z_copy(1, z).start())
-            when(jnp.logical_and(jnp.logical_not(p.has_above), z < p.z), lambda: self.z_copy(0, z).start())
-
-    def along_z(self):
-        p = self.place
-        inside = jnp.logical_and(p.has_below, p.has_above)
+            when(z != p.z, lambda: self.z_copy(z).start())
+
+    def finish(self):
+        p = self.place
+        self.store(self.spare[p.z].astype(F32), False)
         for z in range(p.planes):
-            def onward(up, z=z):
-                self.z_copy(up, z).wait_recv()
-                total = self.spare[z].astype(F32) + self.from_z[up, z].astype(F32)
-                self.spare[z] = total.astype(self.dtype)
-                self.z_copy(up, z).start()
-
-            when(jnp.logical_and(inside, z > p.z), lambda: onward(1))
-            when(jnp.logical_and(inside, z < p.z), lambda: onward(0))
-
-    def finish(self):
-        p = self.place
-        self.store(self.spare[p.z].astype(F32), False)
-        for up, there in ((1, p.has_below), (0, p.has_above)):
-            def arrive(up=up):
-                self.z_copy(up, p.z).wait_recv()
-                self.store(self.from_z[up, p.z].astype(F32), True)
-
-            when(there, arrive)
+            def arrive(z=z):
+                self.z_arrival(z).wait_recv()
+                self.store(self.from_z[z].astype(F32), True)
+
+            when(z != p.z, arrive)
         self.partner_copy().wait_send()
-        for copy in self.diag_copies() + self.side_copies():
+        for copy in self.square_copies():
             copy.wait_send()
         for z in range(p.planes):
-            when(jnp.logical_and(z > p.z, p.has_above), lambda: self.z_copy(1, z).wait_send())
-            when(jnp.logical_and(z < p.z, p.has_below), lambda: self.z_copy(0, z).wait_send())
-
-
-STAGES = ("start", "after_partner", "after_diag", "after_side", "along_z", "finish")
-
-
-def scatter_scratch(planes, rows, width, dtype, held, via):
+            when(z != p.z, lambda: self.z_copy(z).wait_send())
+
+
+STAGES = ("start", "after_partner", "after_square", "finish")
+
+
+def scatter_scratch(planes, rows, width, dtype, held):
     return ([pltpu.VMEM((planes, 2, 2, rows, width), dtype)] if held else []) + [
         pltpu.VMEM((planes, 2, 2, rows, width), dtype),
-        pltpu.VMEM((2, planes, rows, width // 2) if via is None else (1, planes, rows, width), dtype),
-        pltpu.VMEM((2, planes, rows, width), dtype),
-        pltpu.VMEM((2, planes, rows, width), dtype),
+        pltpu.VMEM((3, planes, rows, width), dtype),
+        pltpu.VMEM((planes, rows, width), dtype),
         pltpu.VMEM((planes, rows, width), dtype),
     ]
+
+
+def scatter_sems(planes, number):
+    return [
+        pltpu.SemaphoreType.DMA((number, 4 + planes)),
+        pltpu.SemaphoreType.DMA((number, 4 + planes)),
+        pltpu.SemaphoreType.DMA((number,)),
+    ]
+
+
+class Schedule:
+    def __init__(self, place, sems, scratch, ticks):
+        self.place, self.sems, self.scratch, self.ticks = place, sems, scratch, ticks
+        self.count, self.due, self.late = 0, {}, []
+
+    def add(self, source, load, store, steps):
+        size = 5 if load else 4
+        bufs, self.scratch = self.scratch[:size], self.scratch[size:]
+        held, bufs = (bufs[0], bufs[1:]) if load else (None, bufs)
+        one = Scatter(self.place, self.count, source, held, bufs, self.sems, store)
+        self.count += 1
+        for stage, number in zip(STAGES, steps):
+            if number < self.ticks:
+                self.due.setdefault(number, []).append(getattr(one, stage))
+            else:
+                self.late.append((number, self.count, getattr(one, stage)))
+
+    def tick(self, now):
+        for number, acts in self.due.items():
+            @pl.when(now == number)
+            def _():
+                for act in acts:
+                    act()
+
+    def rest(self):
+        for _, _, act in sorted(self.late, key=lambda entry: entry[:2]):
+            act()
 
 
 def store_to(out, cols=None, rows=None):
@@ -755,127 +747,164 @@
     )(normed, cotangent, win, wfin, vectors, bin_)
 
 
+def fin_grad_kernel(act_ref, gffn_ref, dwfin_ref):
+    dwfin_ref[...] = dot_tn(act_ref[...], gffn_ref[...]).astype(BF16)
+
+
+def fin_grad(act, gffn, chunk):
+    tokens, hidden = act.shape
+    width = gffn.shape[1]
+    return pl.pallas_call(
+        fin_grad_kernel,
+        grid=(hidden // chunk,),
+        in_specs=[pl.BlockSpec((tokens, chunk), lambda i: (0, i)), whole(gffn.shape)],
+        out_specs=pl.BlockSpec((chunk, width), lambda i: (i, 0)),
+        out_shape=jax.ShapeDtypeStruct((hidden, width), BF16),
+        compiler_params=pltpu.CompilerParams(vmem_limit_bytes=VMEM_LIMIT),
+        name="fin_grad",
+    )(act, gffn)
+
+
+FIN_STEPS = ((0, 3, 9, 14), (0, 6, 13, 18), (1, 9, 17, 22), (2, 12, 21, 26))
+FEED_CHUNKS = 6
+
+
 def feed_back_kernel(
-    gffn_ref, low_ref, gsum_hbm, act_ref, slope_ref, win_ref, wfin_ref,
-    dwin_ref, dwfin_ref, gbin_ref, ghid_hbm,
-    low_t_ref, acc_ref, gpre_ref, sem,
+    planes, gffn_ref, low_ref, gsum_hbm, slope_ref, win_ref, wfin_ref,
+    normed_ref, inverse_ref, context_ref, wout_ref, vec_ref, *refs,
 ):
+    sources, refs = refs[: 1 if planes else 0], refs[1 if planes else 0 :]
+    (
+        dwin_ref, gbin_ref, gsum_ref, gcon_ref, dwout_ref, gvec_ref, *outs,
+    ), refs = refs[: 7 if planes else 6], refs[7 if planes else 6 :]
+    low_t_ref, acc_ref, gpre_ref, dwout_acc_ref, sem, *refs = refs
     step = pl.program_id(0)
     tokens = gffn_ref.shape[0]
-    tile = 512
+    tile = normed_ref.shape[0]
+    tiles = tokens // tile
+    if planes:
+        place = Place(planes)
+        schedule = Schedule(place, refs[:3], refs[3:], tiles * (FEED_CHUNKS + 1))
+        rows = sources[0].shape[4] // 4
+        for i in range(4):
+            here = slice(i * rows, (i + 1) * rows)
+            schedule.add(
+                sources[0].at[(slice(None),) * 4 + (here,)], True, store_to(outs[0], rows=here), FIN_STEPS[i]
+            )
 
     @pl.when(step == 0)
     def _():
         copy = pltpu.make_async_copy(gsum_hbm, acc_ref, sem)
         copy.start()
+        if planes:
+            place.enter()
         low_t_ref[...] = jnp.transpose(low_ref[...])
+        gvec_ref[...] = jnp.zeros_like(gvec_ref)
+        dwout_acc_ref[...] = jnp.zeros_like(dwout_acc_ref)
         copy.wait()
 
-    gbin_ref[...] = jnp.zeros_like(gbin_ref)
-    for start in range(0, tokens, tile):
-        here = slice(start, start + tile)
-        gpre = (dot_nt(gffn_ref[here], wfin_ref[...]) * slope_ref[here].astype(F32)).astype(BF16)
-        gpre_ref[here] = gpre
-        gbin_ref[0:1] += column_sum(gpre.astype(F32))
-        acc_ref[here] += dot_nt(gpre, win_ref[...])
-    dwin_ref[...] = dot_nn(low_t_ref[...], gpre_ref[...]).astype(BF16)
-    dwfin_ref[...] = dot_tn(act_ref[...], gffn_ref[...]).astype(BF16)
+    @pl.when(step < FEED_CHUNKS)
+    def _():
+        gbin_ref[...] = jnp.zeros_like(gbin_ref)
+
+        def one_tile(index, _):
+            if planes:
+                schedule.tick(step * tiles + index)
+            here = pl.ds(pl.multiple_of(index * tile, tile), tile)
+            gpre = (dot_nt(gffn_ref[here], wfin_ref[...]) * slope_ref[here].astype(F32)).astype(BF16)
+            gpre_ref[here] = gpre
+            gbin_ref[0:1] += column_sum(gpre.astype(F32))
+            acc_ref[here] += dot_nt(gpre, win_ref[...])
+            return 0
+
+        lax.fori_loop(0, tiles, one_tile, 0)
+        dwin_ref[...] = dot_nn(low_t_ref[...], gpre_ref[...]).astype(BF16)
+
+    @pl.when(step >= FEED_CHUNKS)
+    def _():
+        index = step - FEED_CHUNKS
+        if planes:
+            schedule.tick(tiles * FEED_CHUNKS + index)
+        ghid = acc_ref[pl.ds(pl.multiple_of(index * tile, tile), tile)]
+        normed = normed_ref[...]
+        gvec_ref[0:1] += column_sum(ghid * normed)
+        gvec_ref[1:2] += column_sum(ghid)
+        gsum = normalize_back(ghid * vec_ref[0:1], normed, inverse_ref[:, 0:1])
+        gsum_ref[...] = gsum
+        gattn = gsum.astype(BF16)
+        gvec_ref[2:3] += column_sum(gattn.astype(F32))
+        gcon_ref[...] = dot_nt(gattn, wout_ref[...]).astype(BF16)
+        dwout_acc_ref[...] += dot_tn(context_ref[...], gattn)
 
     @pl.when(step == pl.num_programs(0) - 1)
     def _():
-        pltpu.sync_copy(acc_ref, ghid_hbm)
-
-
-def feed_backward(gffn, low, gsum, act, slope, win, wfin, chunk):
+        dwout_ref[...] = dwout_acc_ref[...].astype(BF16)
+        if planes:
+            schedule.rest()
+
+
+def feed_backward(planes, gffn, low, gsum, slope, win, wfin, normed, inverse, context, wout, vectors, dwfin, tile):
     tokens, width = low.shape
     hidden = win.shape[1]
+    chunk = hidden // FEED_CHUNKS
     any_ = pl.BlockSpec(memory_space=pl.ANY)
+    sources, outs, out_shape, scratch = [], [], [], []
+    if planes:
+        source = dwfin.reshape(planes, 2, 2, 2, -1, width)
+        sources = [source]
+        outs = [whole(source.shape[4:])]
+        out_shape = [jax.ShapeDtypeStruct(source.shape[4:], F32)]
+        scratch = scatter_sems(planes, 4)
+        for _ in range(4):
+            scratch += scatter_scratch(planes, source.shape[4] // 4, width, BF16, True)
+
+    def first(step):
+        return jnp.minimum(step, FEED_CHUNKS - 1)
+
+    def then(columns):
+        return pl.BlockSpec((tile, columns), lambda i: (jnp.maximum(i - FEED_CHUNKS, 0), 0))
+
     return pl.pallas_call(
-        feed_back_kernel,
-        grid=(hidden // chunk,),
+        functools.partial(feed_back_kernel, planes),
+        grid=(FEED_CHUNKS + tokens // tile,),
         in_specs=[
             whole(gffn.shape), whole(low.shape), any_,
-            pl.BlockSpec((tokens, chunk), lambda i: (0, i)),
-            pl.BlockSpec((tokens, chunk), lambda i: (0, i)),
-            pl.BlockSpec((width, chunk), lambda i: (0, i)),
-            pl.BlockSpec((chunk, width), lambda i: (i, 0)),
-        ],
+            pl.BlockSpec((tokens, chunk), lambda i: (0, first(i))),
+            pl.BlockSpec((width, chunk), lambda i: (0, first(i))),
+            pl.BlockSpec((chunk, width), lambda i: (first(i), 0)),
+            then(width), then(BLOCK), then(width), whole(wout.shape), whole(vectors.shape),
+        ] + [any_] * len(sources),
         out_specs=[
-            pl.BlockSpec((width, chunk), lambda i: (0, i)),
-            pl.BlockSpec((chunk, width), lambda i: (i, 0)),
-            pl.BlockSpec((8, chunk), lambda i: (0, i)),
-            any_,
-        ],
+            pl.BlockSpec((width, chunk), lambda i: (0, first(i))),
+            pl.BlockSpec((8, chunk), lambda i: (0, first(i))),
+            then(width), then(width), whole((width, width)), whole((8, width)),
+        ] + outs,
         out_shape=[
             jax.ShapeDtypeStruct((width, hidden), BF16),
-            jax.ShapeDtypeStruct((hidden, width), BF16),
             jax.ShapeDtypeStruct((8, hidden), F32),
             jax.ShapeDtypeStruct((tokens, width), F32),
-        ],
+            jax.ShapeDtypeStruct((tokens, width), BF16),
+            jax.ShapeDtypeStruct((width, width), BF16),
+            jax.ShapeDtypeStruct((8, width), F32),
+        ] + out_shape,
         scratch_shapes=[
             pltpu.VMEM((width, tokens), BF16),
             pltpu.VMEM((tokens, width), F32),
             pltpu.VMEM((tokens, chunk), BF16),
+            pltpu.VMEM((width, width), F32),
             pltpu.SemaphoreType.DMA,
-        ],
-        compiler_params=pltpu.CompilerParams(vmem_limit_bytes=VMEM_LIMIT),
+        ] + scratch,
+        compiler_params=pltpu.CompilerParams(
+            vmem_limit_bytes=VMEM_LIMIT,
+            **(dict(collective_id=2, has_side_effects=True) if planes else {}),
+        ),
         name="feed_backward",
-    )(gffn, low, gsum, act, slope, win, wfin)
-
-
-def project_back_kernel(
-    ghid_ref, normed_ref, inverse_ref, context_ref, wout_ref, gain_ref,
-    gsum_ref, gcon_ref, dwout_ref, gvec_ref, acc_ref,
-):
-    step = pl.program_id(0)
-
-    @pl.when(step == 0)
-    def _():
-        gvec_ref[...] = jnp.zeros_like(gvec_ref)
-        acc_ref[...] = jnp.zeros_like(acc_ref)
-
-    ghid = ghid_ref[...]
-    normed = normed_ref[...]
-    gvec_ref[0:1] += column_sum(ghid * normed)
-    gvec_ref[1:2] += column_sum(ghid)
-    gsum = normalize_back(ghid * gain_ref[0:1], normed, inverse_ref[:, 0:1])
-    gsum_ref[...] = gsum
-    gattn = gsum.astype(BF16)
-    gvec_ref[2:3] += column_sum(gattn.astype(F32))
-    gcon_ref[...] = dot_nt(gattn, wout_ref[...]).astype(BF16)
-    acc_ref[...] += dot_tn(context_ref[...], gattn)
-
-    @pl.when(step == pl.num_programs(0) - 1)
-    def _():
-        dwout_ref[...] = acc_ref[...].astype(BF16)
-
-
-def project_backward(ghid, normed, inverse, context, wout, gain, tile):
-    tokens, width = ghid.shape
-    rows = pl.BlockSpec((tile, width), lambda i: (i, 0))
-    return pl.pallas_call(
-        project_back_kernel,
-        grid=(tokens // tile,),
-        in_specs=[
-            rows, rows, pl.BlockSpec((tile, BLOCK), lambda i: (i, 0)), rows,
-            whole(wout.shape), whole(gain.shape),
-        ],
-        out_specs=[rows, rows, whole((width, width)), pl.BlockSpec((8, width), lambda i: (0, 0))],
-        out_shape=[
-            jax.ShapeDtypeStruct((tokens, width), F32),
-            jax.ShapeDtypeStruct((tokens, width), BF16),
-            jax.ShapeDtypeStruct((width, width), BF16),
-            jax.ShapeDtypeStruct((8, width), F32),
-        ],
-        scratch_shapes=[pltpu.VMEM((width, width), F32)],
-        compiler_params=pltpu.CompilerParams(vmem_limit_bytes=VMEM_LIMIT),
-        name="project_backward",
-    )(ghid, normed, inverse, context, wout, gain)
-
-
-FEED_STEPS = ((0, 2, 4, 7, 8, 11), (0, 5, 8, 11, 12, 15), (1, 9, 12, 15, 16, 19), (5, 13, 16, 19, 20, 23))
-OUT_STEPS = (0, 1, 3, 6, 7, 10)
-PAIR_STEPS = (0, 1, 2, 3, 5, 7)
+    )(gffn, low, gsum, slope, win, wfin, normed, inverse, context, wout, vectors, *sources)
+
+
+IN_STEPS = ((0, 2, 6, 9), (0, 4, 9, 12), (1, 6, 12, 15), (2, 8, 15, 18))
+OUT_STEPS = (3, 10, 17, 20)
+PAIR_STEPS = (0, 1, 5, 9)
 
 
 def attention_back_kernel(
@@ -883,10 +912,10 @@
     q_ref, k_ref, v_ref, gcon_ref, lse_ref, segment_ref, tokens_ref, wq_ref, wk_ref, wv_ref, gsum_hbm,
     gtwo_ref, gbin_ref, gone_ref, *refs,
 ):
-    sources, refs = refs[: 3 if planes else 0], refs[3 if planes else 0 :]
+    sources, refs = refs[: 2 if planes else 0], refs[2 if planes else 0 :]
     gtok_hbm, refs = refs[0], refs[1:]
     if planes:
-        outs, refs = refs[:5], refs[5:]
+        outs, refs = refs[:4], refs[4:]
     else:
         dw_ref, small_ref, refs = refs[0], refs[1], refs[2:]
     tokens_t_ref, acc_ref, mask_ref, grad_ref, dk_ref, dv_ref, gbqv_ref, sem, *refs = refs
@@ -898,36 +927,19 @@
     blocks = length // BLOCK
     offsets, _ = mask_offsets(length)
     tile = 512
-    due, late = {}, []
 
     if planes:
         place = Place(planes)
-        sems, (pair_dw_ref, small_ref), refs = refs[:3], refs[3:5], refs[5:]
-        scatters = []
-
-        def scatter(source, load, store, steps, via=None):
-            nonlocal refs
-            size = 6 if load else 5
-            bufs, refs = refs[:size], refs[size:]
-            held, bufs = (bufs[0], bufs[1:]) if load else (None, bufs)
-            one = Scatter(place, len(scatters), source, held, bufs, sems, store, via)
-            scatters.append(one)
-            for stage, number in zip(STAGES, steps):
-                if number < count * pairs:
-                    due.setdefault(number, []).append(getattr(one, stage))
-                else:
-                    late.append((number, len(scatters), getattr(one, stage)))
-
-        dwin, dwfin, dwout = sources
-        half, wide = dwfin.shape[4] // 2, dwin.shape[5] // 2
-        lead = (slice(None),) * 4
-        for i in range(2):
-            rows = slice(i * half, (i + 1) * half)
-            scatter(dwfin.at[lead + (rows,)], True, store_to(outs[3], rows=rows), FEED_STEPS[i])
-        for i in range(2):
+        pair_dw_ref, small_ref = refs[3:5]
+        schedule = Schedule(place, refs[:3], refs[5:], count * pairs)
+        dwin, dwout = sources
+        wide = dwin.shape[5] // 4
+        for i in range(4):
             cols = slice(i * wide, (i + 1) * wide)
-            scatter(dwin.at[lead + (slice(None), cols)], True, store_to(outs[2], cols=cols), FEED_STEPS[2 + i])
-        scatter(dwout, True, store_to(outs[1]), OUT_STEPS)
+            schedule.add(
+                dwin.at[(slice(None),) * 5 + (cols,)], True, store_to(outs[2], cols=cols), IN_STEPS[i]
+            )
+        schedule.add(dwout, True, store_to(outs[1]), OUT_STEPS)
         for i in range(pairs):
             def store(value, more, i=i):
                 for part in range(3):
@@ -935,12 +947,10 @@
                     here = slice(part * width + i * BLOCK, part * width + (i + 1) * BLOCK)
                     store_to(outs[0], cols=here)(value[:, cols], more)
 
-            scatter(
-                pair_dw_ref.at[i], False, store, [count * (i + 1) + n for n in PAIR_STEPS], via=i % 2
-            )
-        scatter(
-            small_ref.reshape(planes, 2, 2, 2, 8, BLOCK), False, store_to(outs[4]),
-            [count * pairs + n for n in PAIR_STEPS], via=0,
+            schedule.add(pair_dw_ref.at[i], False, store, [count * (i + 1) + n for n in PAIR_STEPS])
+        schedule.add(
+            small_ref.reshape(planes, 2, 2, 2, 8, BLOCK), False, store_to(outs[3]),
+            [count * pairs + n for n in PAIR_STEPS],
         )
 
     @pl.when(pair == 0)
@@ -960,12 +970,8 @@
         copy.wait()
 
     def one_seq(seq, _):
-        for number, acts in due.items():
-            @pl.when(pair * count + seq == number)
-            def _():
-                for act in acts:
-                    act()
-
+        if planes:
+            schedule.tick(pair * count + seq)
         base = pl.multiple_of(seq * length, length)
         dk_ref[...] = jnp.zeros_like(dk_ref)
         dv_ref[...] = jnp.zeros_like(dv_ref)
@@ -1010,8 +1016,8 @@
         copy = pltpu.make_async_copy(acc_ref, gtok_hbm, sem)
         copy.start()
         small_ref[:, 0, :] = collect_vector(gbqv_ref[...], pieces[0], devices)
-        for _, _, act in sorted(late, key=lambda entry: entry[:2]):
-            act()
+        if planes:
+            schedule.rest()
         copy.wait()
 
 
@@ -1038,22 +1044,18 @@
     if planes:
         grads = [g.reshape((planes, 2, 2, 2, -1) + g.shape[1:]) for g in grads]
         rows = width // devices
-        shards = [(rows, 3 * width)] + [grads[i].shape[4:] for i in (2, 0, 1)] + [(8, BLOCK)]
+        shards = [(rows, 3 * width), (rows, width), grads[0].shape[4:], (8, BLOCK)]
         outs = [whole(shape) for shape in shards]
         out_shape = [jax.ShapeDtypeStruct(shape, F32) for shape in shards]
-        number = 6 + pairs
-        scratch += [
-            pltpu.SemaphoreType.DMA((number, 5 + 2 * planes)),
-            pltpu.SemaphoreType.DMA((number, 5 + 2 * planes)),
-            pltpu.SemaphoreType.DMA((number,)),
+        scratch += scatter_sems(planes, 6 + pairs) + [
             pltpu.VMEM((pairs, planes, 2, 2, 2, rows, 3 * BLOCK), BF16),
             pltpu.VMEM(small, F32),
         ]
-        for shape in [(grads[1].shape[4] // 2, width)] * 2 + [(rows, grads[0].shape[5] // 2)] * 2 + [(rows, width)]:
-            scratch += scatter_scratch(planes, *shape, BF16, True, None)
+        for shape in [(rows, grads[0].shape[5] // 4)] * 4 + [(rows, width)]:
+            scratch += scatter_scratch(planes, *shape, BF16, True)
         for _ in range(pairs):
-            scratch += scatter_scratch(planes, rows, 3 * BLOCK, BF16, False, 0)
-        scratch += scatter_scratch(planes, 8, BLOCK, F32, False, 0)
+            scratch += scatter_scratch(planes, rows, 3 * BLOCK, BF16, False)
+        scratch += scatter_scratch(planes, 8, BLOCK, F32, False)
     else:
         grads = []
         outs = [pl.BlockSpec((width, 3 * BLOCK), lambda i: (0, i)), whole(small)]
@@ -1093,26 +1095,29 @@
     fulls, rest = attention_forward(planes, tokens, segments, weights, pieces)
     wqkv, _, wout, win, wfin = fulls
     qkv, context, lse, normed, inverse, vectors, bin_ = rest
-    tile = min(512, tokens.shape[0])
+    tile, width = min(512, tokens.shape[0]), tokens.shape[1]
     output, act, slope, gsum_two, gffn, low, gvec_two = feed_forward(
         normed, cotangent, win, wfin, vectors, bin_, tile
     )
-    dwin, dwfin, gbin, ghid = feed_backward(gffn, low, gsum_two, act, slope, win, wfin, 512)
-    gsum_one, gcon, dwout, gvec_one = project_backward(ghid, normed, inverse, context, wout, vectors, tile)
+    dwfin = fin_grad(act, gffn, width)
+    dwin, gbin, gsum_one, gcon, dwout, gvec_one, *fin = feed_backward(
+        planes, gffn, low, gsum_two, slope, win, wfin, normed, inverse, context, wout, vectors, dwfin, tile
+    )
     gtok, *sums = attention_backward(
         planes, pieces, devices, qkv, gcon, lse, segments, tokens, wqkv, gsum_one,
-        (gvec_two, gbin, gvec_one), [dwin, dwfin, dwout],
+        (gvec_two, gbin, gvec_one), [dwin, dwout],
     )
     if not planes:
         sums = [
             lax.psum_scatter(g.reshape((devices, -1) + g.shape[-1:]), AXES, scatter_dimension=0).astype(F32)
-            for g in (sums[0], dwout, dwin, dwfin, sums[1])
+            for g in (sums[0], dwout, dwin, sums[1], dwfin)
         ]
         sums[0] = sums[0].reshape(sums[0].shape[0], -1, 3, BLOCK).swapaxes(1, 2).reshape(sums[0].shape)
-    parts = [sums[4][i, :piece] for i, piece in enumerate(pieces)]
+        fin = sums[4:]
+    parts = [sums[3][i, :piece] for i, piece in enumerate(pieces)]
     return (
         output, gtok, sums[0], parts[0], sums[1], parts[1], parts[2], parts[3],
-        sums[2], parts[4], sums[3], parts[5], parts[6], parts[7],
+        sums[2], parts[4], fin[0], parts[5], parts[6], parts[7],
     )
 
 

time: 468 us -> 369 us (0.79); the launches traced: 460 us -> 368 us
  Pallas kernels: 442 us -> 351 us
    pallas_call x1, Pallas kernels: 196 us -> 93.2 us  [attention_backward(): pl.pallas_call(functools.partial(attention_back_kernel, planes, pieces, d...]
    pallas_call x2, Pallas kernels: 68.1 us -> 79.2 us  [the longest x1 64.5 us: feed_backward(): pl.pallas_call(functools.partial(feed_back_kernel, planes), grid=(FEED_CH...]
where the time goes in v4:
time: 369 us; the launch traced here: 368 us
  Pallas kernels  351 us (95%)
  local copies, waits for them, and re-layouts  17.1 us (5%)
    pallas_call x1, Pallas kernels, attention_forward(): pl.pallas_call(functools.partial(attention_kernel, planes, pieces), grid=...  122 us
    pallas_call x1, Pallas kernels, attention_backward(): pl.pallas_call(functools.partial(attention_back_kernel, planes, pieces, d...  93.2 us
    pallas_call x1, Pallas kernels, feed_backward(): pl.pallas_call(functools.partial(feed_back_kernel, planes), grid=(FEED_CH...  64.5 us
    pallas_call x1, Pallas kernels, feed_forward(): pl.pallas_call(feed_kernel, grid=(tokens // tile,), in_specs=[rows, rows,...  56 us
    pallas_call x1, Pallas kernels, fin_grad(): pl.pallas_call(fin_grad_kernel, grid=(hidden // chunk,), in_specs=[pl.Blo...  14.8 us
    unnamed x13, local copies, waits for them, and re-layouts  8.73 us

profile of v4, /device:TPU:0, one launch (start us, length us, event | category | flops | bytes accessed | tf_op | source)
XLA Modules:
  0.0 368.4 jit_solution(6215899883377411905)
XLA Ops:
  0.6 0.7 pad_bitcast_fusion.6
  1.3 0.7 pad_bitcast_fusion.4
  2.0 0.7 pad_bitcast_fusion.2
  2.7 0.7 pad_bitcast_fusion
  3.4 0.6 stack.35.refs_1_
  4.0 1.3 reshape.40.segment_ref
  5.3 122.1 %attention_forward.1 = (bf16[768,2304]{1,0:T(8,128)(2,1)}, bf16[256,128]{1,0:T(8,128)(2,1)}, bf16[768,768]{1,0:T(8,128)(2,1)}, bf16[768,3072]{1,0:T(8,128)(2,1)}...) custom-call(bf16[2048,768]{1,0:T(8,128)(2,1)} %tokens_ref.3, ...), custom_call_target="tpu_custom_call" | custom-call | tf_op jit(solution)/shard_map/attention_forward/pallas_call | solution.py:647
  127.4 56.0 %feed_forward.1 = (bf16[2048,768]{1,0:T(8,128)(2,1)}, bf16[2048,3072]{1,0:T(8,128)(2,1)}, bf16[2048,3072]{1,0:T(8,128)(2,1)}, f32[2048,768]{1,0:T(8,128)}, bf16[...) custom-call(f32[2048,768]{1,0:T(8,128)} %get-tuple-element.44.normed_ref, ...), custom_call_target="tpu_custom_call" | custom-call | tf_op jit(solution)/shard_map/feed_forward/pallas_call | solution.py:730
  183.4 14.8 %fin_grad.1 = bf16[3072,768]{1,0:T(8,128)(2,1)} custom-call(bf16[2048,3072]{1,0:T(8,128)(2,1)} %get-tuple-element.58.act_ref, bf16[2048,768]{1,0:T(8,128)(2,1)} %get-tuple-element.51.gffn_ref), custom_call_target="tpu_custom_call" | custom-call | tf_op jit(solution)/shard_map/fin_grad/pallas_call | solution.py:757
  198.2 64.5 %feed_backward.1 = (bf16[768,3072]{1,0:T(8,128)(2,1)}, f32[8,3072]{1,0:T(8,128)}, f32[2048,768]{1,0:T(8,128)}, bf16[2048,768]{1,0:T(8,128)(2,1)}, bf16[768,768]{...) custom-call(bf16[2048,768]{1,0:T(8,128)(2,1)} %get-tuple-element.51.gffn_ref, ...), custom_call_target="tpu_custom_call" | custom-call | tf_op jit(solution)/shard_map/feed_backward/pallas_call | solution.py:867
  262.7 93.2 %attention_backward.1 = (f32[2048,768]{1,0:T(8,128)}, f32[24,2304]{1,0:T(8,128)}, f32[24,768]{1,0:T(8,128)}, f32[24,3072]{1,0:T(8,128)}, f32[8,128]{1,0:T(8,128)}) custom-call(bf16[2048,2304]{1,0:T(8,128)(2,1)} %get-tuple-element.50.q_ref.k_ref.v_ref, bf16[2048,2304]{1,0:T(8,128)(2,1)} %get-tuple-element.50.q_ref.k_ref.v_ref, ...), custom_call_target="tpu_custom_call" | custom-call | tf_op jit(solution)/shard_map/attention_backward/pallas_call | solution.py:1063
  355.9 1.2 slice_bitcast_fusion.3
  357.1 1.2 slice_bitcast_fusion.7
  358.3 1.4 slice_bitcast_fusion
  359.7 0.0 copy-start.1
  359.7 0.0 copy-start
  359.7 6.0 %copy.34 = f32[2048,768]{1,0:T(8,128)} copy(f32[2048,768]{1,0:T(8,128)} %get-tuple-element.103) | data formatting | bytes 12582912
  365.7 0.0 copy-done.2
  365.7 0.7 copy.35
  366.4 0.0 copy-done.3
  366.4 0.6 copy.36
  367.0 0.0 copy-done.1
  367.0 0.7 copy.37
  367.7 0.7 copy.38
  (3 shorter events, 0.0 us)
Async XLA Ops:
  359.7 6.0 %copy-start.2 = (f32[24,2304]{1,0:T(8,128)S(1)}, f32[24,2304]{1,0:T(8,128)}, u32[]{:S(2)}) copy-start(f32[24,2304]{1,0:T(8,128)} %get-tuple-element.104) | copy-start | bytes 663556
  359.7 6.7 %copy-start.3 = (f32[24,768]{1,0:T(8,128)S(1)}, f32[24,768]{1,0:T(8,128)}, u32[]{:S(2)}) copy-start(f32[24,768]{1,0:T(8,128)} %get-tuple-element.106) | copy-start | bytes 221188
  359.7 7.3 %copy-start.1 = (f32[24,3072]{1,0:T(8,128)S(1)}, f32[24,3072]{1,0:T(8,128)}, u32[]{:S(2)}) copy-start(f32[24,3072]{1,0:T(8,128)} %get-tuple-element.110) | copy-start | bytes 884740
  359.7 8.0 %copy-start = (f32[96,768]{1,0:T(8,128)S(1)}, f32[96,768]{1,0:T(8,128)}, u32[]{:S(2)}) copy-start(f32[96,768]{1,0:T(8,128)} %get-tuple-element.112) | copy-start | bytes 884740

commit v5 on v4

--- a/solution.py
+++ b/solution.py
@@ -94,15 +94,8 @@
 
 
 def gelu_parts(pre):
-    size = jnp.abs(pre)
-    t = 1.0 / (1.0 + 0.3275911 * 0.7071067811865476 * size)
-    bell = jnp.exp(-0.5 * pre * pre)
-    series = t * (
-        0.127414796
-        + t * (-0.142248368 + t * (0.7107068705 + t * (-0.7265760135 + t * 0.5307027145)))
-    )
-    tail = series * bell
-    cdf = jnp.where(pre >= 0.0, 1.0 - tail, tail)
+    cdf = 0.5 + 0.5 * lax.erf(pre * 0.7071067811865476)
+    bell = jnp.exp2((-0.7213475204444817 * pre) * pre)
     return (pre * cdf, cdf + pre * (bell * 0.3989422804014327))
 
 
@@ -310,6 +303,80 @@
             getattr(self, name)(*args)
 
 
+class Bundles:
+    def __init__(self, place, index, shard, full, send, recv, local):
+        self.place, self.index, self.shard, self.full = place, index, shard, full
+        self.send, self.recv, self.local = send, recv, local
+
+    def copy(self, slot, src, dst, device, arrival=None):
+        return pltpu.make_async_remote_copy(
+            src_ref=src, dst_ref=dst, send_sem=self.send.at[self.index, slot],
+            recv_sem=self.recv.at[self.index, slot if arrival is None else arrival],
+            device_id=device, device_id_type=MESH,
+        )
+
+    def own_copy(self):
+        p = self.place
+        return pltpu.make_async_copy(
+            self.shard, self.full.at[p.z, p.x, p.c, p.y], self.local.at[self.index]
+        )
+
+    def z_copy(self, z):
+        p = self.place
+        return self.copy(z, self.shard, self.full.at[p.z, p.x, p.c, p.y], p.device(z=z), p.z)
+
+    def z_arrival(self, z):
+        p = self.place
+        return self.copy(z, self.shard, self.full.at[z, p.x, p.c, p.y], p.device(z=z))
+
+    def bundle(self, step, here):
+        p = self.place
+        full = self.full
+        other = {"across": p.across, "beside": p.beside, "partner": p.partner}
+        to, x, y, half = (
+            ("across", 0, 0, 2), ("beside", 0, 0, 2), ("partner", 0, 0, 2),
+            ("beside", 1, 0, 0), ("across", 0, 1, 1), ("partner", 1, 0, 2), ("partner", 0, 1, 2),
+            ("partner", 1, 1, 2),
+        )[step]
+        c = p.c
+        if not here:
+            x = 1 - x if to == "across" else x
+            y = 1 - y if to == "beside" else y
+            c = 1 - c if to == "partner" else c
+        ref = half_of(full.at[:, 1 - p.x if x else p.x, c, 1 - p.y if y else p.y], half)
+        return self.copy(p.planes + step, ref, ref, other[to])
+
+    def first(self):
+        for z in range(self.place.planes):
+            when(z != self.place.z, lambda: self.z_copy(z).start())
+        self.own_copy().start()
+
+    def move(self, arrived, onward):
+        for step in arrived:
+            self.bundle(step, False).wait_recv()
+        for step in onward:
+            self.bundle(step, True).start()
+
+    def after_z(self):
+        for z in range(self.place.planes):
+            when(z != self.place.z, lambda: self.z_arrival(z).wait_recv())
+        self.own_copy().wait()
+        self.move((), (0, 1, 2))
+
+    def after_side(self):
+        self.move((0, 1), (3, 4, 5, 6))
+
+    def after_diagonal(self):
+        self.move((3, 4), (7,))
+
+    def finish(self):
+        self.move((2, 5, 6, 7), ())
+        for z in range(self.place.planes):
+            when(z != self.place.z, lambda: self.z_copy(z).wait_send())
+        for step in range(8):
+            self.bundle(step, True).wait_send()
+
+
 class Scatter:
     def __init__(self, place, index, source, held, bufs, sems, store):
         self.place, self.index, self.source, self.store = place, index, source, store
@@ -496,15 +563,8 @@
     return dot_nt(high, place) + dot_nt(low, place)
 
 
-OUT_TICKS = (
-    (0, "along_z", 1), (0, "across_xy", 0), (0, "along_z", 2), (1, "across_xy", 1), (1, "diagonal", 0),
-    (1, "along_z", 3), (2, "across_xy", 2), (2, "diagonal", 1), (3, "across_xy", 3), (3, "diagonal", 2),
-    (4, "diagonal", 3),
-)
-FEED_TICKS = (
-    (0, "first_xy"), (0, "along_z", 1), (2, "along_z", 2), (4, "across_xy", 0), (5, "along_z", 3),
-    (8, "diagonal", 0), (9, "across_xy", 1), (13, "diagonal", 1), (14, "across_xy", 2),
-    (18, "diagonal", 2), (18, "across_xy", 3), (22, "diagonal", 3),
+GATHER_STEPS = (
+    (11, 17, 21, 23), (-2, 2, 7, 11), (-1, 4, 11, 15), (0, 8, 15, 19), (4, 12, 19, 22),
 )
 
 
@@ -515,8 +575,8 @@
     else:
         fulls = shards
     (
-        qkv_ref, context_ref, lse_ref, normed_ref, inverse_ref, vectors_ref, bin_ref,
-        wqkv_ref, wout_ref, small_ref, bias_ref, mask_ref, load_sem, *sems,
+        qkv_ref, context_ref, lse_ref, vectors_ref, bin_ref,
+        wqkv_ref, small_ref, bias_ref, mask_ref, load_sem, *sems,
     ) = refs
     length, width = tokens_ref.shape
     count = pl.num_programs(0)
@@ -526,8 +586,20 @@
     gathers = []
     if planes:
         place = Place(planes)
-        gathers = [Gather(place, i, shards[i], fulls[i], *sems) for i in range(5)]
-    attn, out, feed = gathers[:2], gathers[2:3], gathers[3:]
+        gathers = [Gather(place, i, shards[i], fulls[i], *sems[:3]) for i in range(2)]
+        cuts = [(2, ()), (3, (slice(None), 0)), (3, (slice(None), 1)), (4, (0,)), (4, (1,))]
+        for i, (array, cut) in enumerate(cuts):
+            shard, full = shards[array], fulls[array]
+            if cut:
+                size = shard.shape[len(cut) - 1] // 2
+                cut = cut[:-1] + (slice(cut[-1] * size, (cut[-1] + 1) * size),)
+                shard, full = shard.at[cut], full.at[(slice(None),) * 4 + cut]
+            gathers.append(Bundles(place, i, shard, full, *sems[3:]))
+    attn, later = gathers[:2], gathers[2:]
+    due = {}
+    for gather, steps in zip(later, GATHER_STEPS):
+        for number, act in zip(steps, (gather.first, gather.after_z, gather.after_side, gather.after_diagonal)):
+            due.setdefault(number, []).append(act)
 
     def load(index, ref):
         return pltpu.make_async_copy(fulls[index], ref, load_sem.at[index])
@@ -536,17 +608,20 @@
     def _():
         if planes:
             place.enter()
-            for gather in attn + out:
+            for gather in attn:
                 gather.run("first_z")
                 gather.run("first_xy")
-            for gather in feed:
-                gather.run("first_z")
+            for act in due.get(-4, []):
+                act()
         for seq in range(segment_ref.shape[0]):
             fill_masks(mask_ref, seq, segment_ref[seq])
         for distance in range(1, planes + 2 if planes else 0):
             for gather in attn:
                 if distance < planes:
                     gather.run("along_z", distance)
+            for act in due.get(distance - 4, []) if distance < 4 else ():
+                act()
+            for gather in attn:
                 if distance - 1 < planes:
                     gather.run("across_xy", distance - 1)
                 if distance >= 2:
@@ -560,19 +635,12 @@
         bqv, bout, gain_one, shift_one, bin_, bfin, gain_two, shift_two = spread_vectors(small, pieces)
         bias_ref[:, :width] = bqv[:, :width]
         bias_ref[:, width : 2 * width] = jnp.zeros_like(bout)
-        bias_ref[:, 2 * width : 3 * width] = bqv[:, width:]
-        bias_ref[:, 3 * width :] = bout
+        bias_ref[:, 2 * width :] = bqv[:, width:]
         bin_ref[...] = bin_
-        for row, vector in enumerate((gain_one, shift_one, bfin, gain_two, shift_two)):
+        for row, vector in enumerate((gain_one, shift_one, bfin, gain_two, shift_two, bout)):
             vectors_ref[row : row + 1] = vector
-        vectors_ref[5:8] = jnp.zeros((3, width), F32)
+        vectors_ref[6:8] = jnp.zeros((2, width), F32)
         load(0, wqkv_ref).wait()
-
-    due = {}
-    for group, ticks in ((out, OUT_TICKS), (feed, FEED_TICKS)):
-        for number, name, *args in ticks:
-            for gather in group:
-                due.setdefault(number, []).append(functools.partial(gather.run, name, *args))
 
     for part in range(3):
         cols = slice(part * width, (part + 1) * width)
@@ -583,6 +651,9 @@
 
     def one_pair(pair, _):
         for number, acts in due.items():
+            if number < 0:
+                continue
+
             @pl.when(step * pairs + pair == number)
             def _():
                 for act in acts:
@@ -591,36 +662,30 @@
         def cols(part):
             return pl.ds(pl.multiple_of(part * width + pair * BLOCK, BLOCK), BLOCK)
 
-        for block, (low, high) in enumerate(windows(length)):
-            here = slice(block * BLOCK, (block + 1) * BLOCK)
-            query = stacked(qkv_ref[here, cols(0)])
-            scores = dot_nt(qkv_ref[low:high, cols(1)], query)
-            scores = scores + twice(mask_ref[step, pl.ds(offsets[block], high - low), :])
-            maxima = jnp.max(scores, axis=0, keepdims=True)
-            exponent = jnp.exp(scores - maxima)
-            totals = jnp.sum(exponent, axis=0, keepdims=True)
-            context = dot_tn(qkv_ref[low:high, cols(2)], exponent.astype(BF16)) * (1.0 / totals)
-            context_ref[here, cols(0)] = unstacked_t(context).astype(BF16)
-            lse_ref[0, pl.ds(pair * (length // BLOCK) + block, 1), :] = maxima + jnp.log(totals)
+        reach = windows(length)
+        here = [slice(block * BLOCK, (block + 1) * BLOCK) for block in range(len(reach))]
+        scores = [
+            dot_nt(qkv_ref[low:high, cols(1)], stacked(qkv_ref[rows, cols(0)]))
+            + twice(mask_ref[step, pl.ds(offsets[block], high - low), :])
+            for block, (rows, (low, high)) in enumerate(zip(here, reach))
+        ]
+        maxima = [jnp.max(score, axis=0, keepdims=True) for score in scores]
+        exponents = [jnp.exp(score - peak) for score, peak in zip(scores, maxima)]
+        totals = [jnp.sum(exponent, axis=0, keepdims=True) for exponent in exponents]
+        contexts = [
+            dot_tn(qkv_ref[low:high, cols(2)], exponent.astype(BF16)) * (1.0 / total)
+            for exponent, total, (low, high) in zip(exponents, totals, reach)
+        ]
+        for block, context in enumerate(contexts):
+            context_ref[here[block], cols(0)] = unstacked_t(context).astype(BF16)
+            lse_ref[0, pl.ds(pair * len(reach) + block, 1), :] = maxima[block] + jnp.log(totals[block])
         return 0
 
     lax.fori_loop(0, pairs, one_pair, 0)
-
-    @pl.when(step == 0)
-    def _():
-        for gather in out:
-            gather.finish()
-        load(2, wout_ref).start()
-        load(2, wout_ref).wait()
-
-    branch = dot_nn(context_ref[...], wout_ref[...]) + bias_ref[:, 3 * width :]
-    normed, inverse = normalize(tokens_ref[...].astype(F32) + branch)
-    normed_ref[...] = normed
-    inverse_ref[...] = jnp.broadcast_to(inverse, inverse_ref.shape)
 
     @pl.when(step == count - 1)
     def _():
-        for gather in feed:
+        for gather in later:
             gather.finish()
 
 
@@ -636,12 +701,18 @@
     lse_rows = (width // BLOCK) * (length // BLOCK)
     hidden = weights[3].shape[-1]
     devices = planes * 8 if planes else weights[1].shape[0] // 8
-    gathered = [(devices * w.shape[0], w.shape[1]) for w in weights] if planes else []
+    gathered = []
+    if planes:
+        gathered = [(devices * w.shape[0], w.shape[1]) for w in weights[:2]]
+        gathered += [(planes, 2, 2, 2) + w.shape for w in weights[2:]]
     sems = []
     if planes:
         sems = [
-            pltpu.SemaphoreType.DMA((5, SENDS)),
-            pltpu.SemaphoreType.DMA((5, planes, 2, 2, 2, 2)),
+            pltpu.SemaphoreType.DMA((2, SENDS)),
+            pltpu.SemaphoreType.DMA((2, planes, 2, 2, 2, 2)),
+            pltpu.SemaphoreType.DMA((2,)),
+            pltpu.SemaphoreType.DMA((5, planes + 8)),
+            pltpu.SemaphoreType.DMA((5, planes + 8)),
             pltpu.SemaphoreType.DMA((5,)),
         ]
     out = pl.pallas_call(
@@ -652,8 +723,6 @@
             pl.BlockSpec((length, 3 * width), lambda i: (i, 0)),
             rows,
             pl.BlockSpec((1, lse_rows, 2 * BLOCK), lambda i: (i, 0, 0)),
-            rows,
-            pl.BlockSpec((length, BLOCK), lambda i: (i, 0)),
             whole((8, width)),
             whole((1, hidden)),
         ],
@@ -661,18 +730,15 @@
             jax.ShapeDtypeStruct((count * length, 3 * width), BF16),
             jax.ShapeDtypeStruct((count * length, width), BF16),
             jax.ShapeDtypeStruct((count, lse_rows, 2 * BLOCK), F32),
-            jax.ShapeDtypeStruct((count * length, width), F32),
-            jax.ShapeDtypeStruct((count * length, BLOCK), F32),
             jax.ShapeDtypeStruct((8, width), F32),
             jax.ShapeDtypeStruct((1, hidden), F32),
         ],
         scratch_shapes=[
             pltpu.VMEM((width, 3 * width), BF16),
-            pltpu.VMEM((width, width), BF16),
             pltpu.VMEM((devices * 8, BLOCK), BF16),
-            pltpu.VMEM((1, 4 * width), F32),
+            pltpu.VMEM((1, 3 * width), F32),
             pltpu.VMEM((count, mask_offsets(length)[1], BLOCK), F32),
-            pltpu.SemaphoreType.DMA((3,)),
+            pltpu.SemaphoreType.DMA((2,)),
         ] + sems,
         compiler_params=pltpu.CompilerParams(
             vmem_limit_bytes=VMEM_LIMIT,
@@ -681,18 +747,22 @@
         name="attention_forward",
     )(tokens, segments, *weights)
     fulls = out[: len(gathered)] if planes else weights
-    return fulls, out[len(gathered) :]
+    return [f.reshape(-1, f.shape[-1]) for f in fulls], out[len(gathered) :]
 
 
 def feed_kernel(
-    normed_ref, cot_ref, win_ref, wfin_ref, vec_ref, bin_ref,
-    out_ref, act_ref, slope_ref, gsum_ref, gffn_ref, low_ref, gvec_ref,
+    tokens_ref, context_ref, cot_ref, wout_ref, win_ref, wfin_ref, vec_ref, bin_ref,
+    normed_ref, inverse_ref, out_ref, act_ref, slope_ref, gsum_ref, gffn_ref, low_ref, gvec_ref,
     hidden_ref,
 ):
-    hidden = normed_ref[...] * vec_ref[0:1] + vec_ref[1:2]
+    branch = dot_nn(context_ref[...], wout_ref[...]) + vec_ref[5:6]
+    normed, inverse = normalize(tokens_ref[...].astype(F32) + branch)
+    normed_ref[...] = normed
+    inverse_ref[...] = jnp.broadcast_to(inverse, inverse_ref.shape)
+    hidden = normed * vec_ref[0:1] + vec_ref[1:2]
     hidden_ref[...] = hidden
     low_ref[...] = hidden.astype(BF16)
-    width = win_ref.shape[0]
+    width = 2 * BLOCK
 
     def one_chunk(chunk, _):
         cols = pl.ds(pl.multiple_of(chunk * width, width), width)
@@ -702,7 +772,7 @@
         slope_ref[:, cols] = slope.astype(BF16)
         return 0
 
-    lax.fori_loop(0, win_ref.shape[1] // width, one_chunk, 0)
+    lax.fori_loop(0, win_ref.shape[1] // width, one_chunk, 0, unroll=True)
     branch = dot_nn(act_ref[...], wfin_ref[...]) + vec_ref[2:3]
     normed, inverse = normalize(hidden_ref[...] + branch)
     gain = vec_ref[3:4]
@@ -722,29 +792,34 @@
     gvec_ref[2:3] += column_sum(gffn.astype(F32))
 
 
-def feed_forward(normed, cotangent, win, wfin, vectors, bin_, tile):
-    tokens, width = normed.shape
+def feed_forward(tokens, context, cotangent, wout, win, wfin, vectors, bin_, tile):
+    total, width = tokens.shape
     hidden = win.shape[1]
     rows = pl.BlockSpec((tile, width), lambda i: (i, 0))
     wide = pl.BlockSpec((tile, hidden), lambda i: (i, 0))
     return pl.pallas_call(
         feed_kernel,
-        grid=(tokens // tile,),
-        in_specs=[rows, rows, whole(win.shape), whole(wfin.shape), whole(vectors.shape), whole(bin_.shape)],
-        out_specs=[rows, wide, wide, rows, rows, rows, pl.BlockSpec((8, width), lambda i: (0, 0))],
+        grid=(total // tile,),
+        in_specs=[rows, rows, rows] + [whole(w.shape) for w in (wout, win, wfin, vectors, bin_)],
+        out_specs=[
+            rows, pl.BlockSpec((tile, BLOCK), lambda i: (i, 0)), rows, wide, wide, rows, rows, rows,
+            pl.BlockSpec((8, width), lambda i: (0, 0)),
+        ],
         out_shape=[
-            jax.ShapeDtypeStruct((tokens, width), BF16),
-            jax.ShapeDtypeStruct((tokens, hidden), BF16),
-            jax.ShapeDtypeStruct((tokens, hidden), BF16),
-            jax.ShapeDtypeStruct((tokens, width), F32),
-            jax.ShapeDtypeStruct((tokens, width), BF16),
-            jax.ShapeDtypeStruct((tokens, width), BF16),
+            jax.ShapeDtypeStruct((total, width), F32),
+            jax.ShapeDtypeStruct((total, BLOCK), F32),
+            jax.ShapeDtypeStruct((total, width), BF16),
+            jax.ShapeDtypeStruct((total, hidden), BF16),
+            jax.ShapeDtypeStruct((total, hidden), BF16),
+            jax.ShapeDtypeStruct((total, width), F32),
+            jax.ShapeDtypeStruct((total, width), BF16),
+            jax.ShapeDtypeStruct((total, width), BF16),
             jax.ShapeDtypeStruct((8, width), F32),
         ],
         scratch_shapes=[pltpu.VMEM((tile, width), F32)],
         compiler_params=pltpu.CompilerParams(vmem_limit_bytes=VMEM_LIMIT),
         name="feed_forward",
-    )(normed, cotangent, win, wfin, vectors, bin_)
+    )(tokens, context, cotangent, wout, win, wfin, vectors, bin_)
 
 
 def fin_grad_kernel(act_ref, gffn_ref, dwfin_ref):
@@ -902,9 +977,9 @@
     )(gffn, low, gsum, slope, win, wfin, normed, inverse, context, wout, vectors, *sources)
 
 
-IN_STEPS = ((0, 2, 6, 9), (0, 4, 9, 12), (1, 6, 12, 15), (2, 8, 15, 18))
-OUT_STEPS = (3, 10, 17, 20)
-PAIR_STEPS = (0, 1, 5, 9)
+IN_STEPS = ((0, 2, 8, 12), (0, 5, 12, 16), (1, 8, 16, 20), (2, 12, 20, 23))
+OUT_STEPS = (4, 14, 22, 24)
+PAIR_STEPS = (0, 1, 6, 10)
 
 
 def attention_back_kernel(
@@ -975,21 +1050,29 @@
         base = pl.multiple_of(seq * length, length)
         dk_ref[...] = jnp.zeros_like(dk_ref)
         dv_ref[...] = jnp.zeros_like(dv_ref)
-        for block, (low, high) in enumerate(windows(length)):
-            here = pl.ds(base + block * BLOCK, BLOCK)
-            reach = pl.ds(base + low, high - low)
-            query = stacked(q_ref[here])
-            grad = stacked(gcon_ref[here])
-            keys = k_ref[reach]
-            scores = dot_nt(keys, query) + twice(mask_ref[seq, pl.ds(offsets[block], high - low), :])
-            probs = jnp.exp(scores - lse_ref[seq, pl.ds(pair * blocks + block, 1), :])
-            gprobs = dot_nt(v_ref[reach], grad)
-            dots = jnp.sum(probs * gprobs, axis=0, keepdims=True)
-            gscores = (probs * (gprobs - dots)).astype(BF16)
-            dv_ref[low:high] += dot_nn(probs.astype(BF16), grad)
-            dk_ref[low:high] += dot_nn(gscores, query)
-            gquery = unstacked_t(dot_tn(keys, gscores)) * HEAD_DIM ** (-0.5)
-            grad_ref[here, 0:BLOCK] = gquery.astype(BF16)
+        span = windows(length)
+        here = [pl.ds(base + block * BLOCK, BLOCK) for block in range(len(span))]
+        reach = [pl.ds(base + low, high - low) for low, high in span]
+        queries = [stacked(q_ref[rows]) for rows in here]
+        grads = [stacked(gcon_ref[rows]) for rows in here]
+        scores = [dot_nt(k_ref[keys], query) for keys, query in zip(reach, queries)]
+        gprobs = [dot_nt(v_ref[keys], grad) for keys, grad in zip(reach, grads)]
+        probs = [
+            jnp.exp(
+                score + twice(mask_ref[seq, pl.ds(offsets[block], score.shape[0]), :])
+                - lse_ref[seq, pl.ds(pair * blocks + block, 1), :]
+            )
+            for block, score in enumerate(scores)
+        ]
+        dots = [jnp.sum(prob * gprob, axis=0, keepdims=True) for prob, gprob in zip(probs, gprobs)]
+        gscores = [
+            (prob * (gprob - dot_)).astype(BF16) for prob, gprob, dot_ in zip(probs, gprobs, dots)
+        ]
+        for block, (low, high) in enumerate(span):
+            dv_ref[low:high] += dot_nn(probs[block].astype(BF16), grads[block])
+            dk_ref[low:high] += dot_nn(gscores[block], queries[block])
+            gquery = unstacked_t(dot_tn(k_ref[reach[block]], gscores[block])) * HEAD_DIM ** (-0.5)
+            grad_ref[here[block], 0:BLOCK] = gquery.astype(BF16)
         rows = pl.ds(base, length)
         grad_ref[rows, BLOCK : 2 * BLOCK] = dk_ref[...].astype(BF16)
         grad_ref[rows, 2 * BLOCK :] = dv_ref[...].astype(BF16)
@@ -1094,10 +1177,10 @@
     segments = segments.reshape(segments.shape[0], 1, segments.shape[1])
     fulls, rest = attention_forward(planes, tokens, segments, weights, pieces)
     wqkv, _, wout, win, wfin = fulls
-    qkv, context, lse, normed, inverse, vectors, bin_ = rest
+    qkv, context, lse, vectors, bin_ = rest
     tile, width = min(512, tokens.shape[0]), tokens.shape[1]
-    output, act, slope, gsum_two, gffn, low, gvec_two = feed_forward(
-        normed, cotangent, win, wfin, vectors, bin_, tile
+    normed, inverse, output, act, slope, gsum_two, gffn, low, gvec_two = feed_forward(
+        tokens, context, cotangent, wout, win, wfin, vectors, bin_, tile
     )
     dwfin = fin_grad(act, gffn, width)
     dwin, gbin, gsum_one, gcon, dwout, gvec_one, *fin = feed_backward(

time: 369 us -> 319 us (0.86)
  Pallas kernels: 351 us -> 301 us
    pallas_call x1, Pallas kernels: 122 us -> 90.4 us  [attention_forward(): pl.pallas_call(functools.partial(attention_kernel, planes, pieces), grid=...]
    pallas_call x1, Pallas kernels: 93.2 us -> 83.5 us  [attention_backward(): pl.pallas_call(functools.partial(attention_back_kernel, planes, pieces, d...]
    pallas_call x1, Pallas kernels: 56 us -> 47.7 us  [feed_forward(): pl.pallas_call(feed_kernel, grid=(total // tile,), in_specs=[rows, rows,...]
where the time goes in v5:
time: 319 us
  Pallas kernels  301 us (94%)
  local copies, waits for them, and re-layouts  17.1 us (5%)
    pallas_call x1, Pallas kernels, attention_forward(): pl.pallas_call(functools.partial(attention_kernel, planes, pieces), grid=...  90.4 us
    pallas_call x1, Pallas kernels, attention_backward(): pl.pallas_call(functools.partial(attention_back_kernel, planes, pieces, d...  83.5 us
    pallas_call x1, Pallas kernels, feed_backward(): pl.pallas_call(functools.partial(feed_back_kernel, planes), grid=(FEED_CH...  64.7 us
    pallas_call x1, Pallas kernels, feed_forward(): pl.pallas_call(feed_kernel, grid=(total // tile,), in_specs=[rows, rows,...  47.7 us
    pallas_call x1, Pallas kernels, fin_grad(): pl.pallas_call(fin_grad_kernel, grid=(hidden // chunk,), in_specs=[pl.Blo...  14.8 us
    unnamed x13, local copies, waits for them, and re-layouts  8.73 us

profile of v5, /device:TPU:0, one launch (start us, length us, event | category | flops | bytes accessed | tf_op | source)
XLA Modules:
  0.0 318.8 jit_solution(2661915004261460882)
XLA Ops:
  0.6 0.7 pad_bitcast_fusion.6
  1.3 0.7 pad_bitcast_fusion.4
  2.0 0.7 pad_bitcast_fusion.2
  2.7 0.7 pad_bitcast_fusion
  3.4 0.6 stack.35.refs_1_
  4.0 1.3 reshape.49.segment_ref
  5.3 90.4 %attention_forward.1 = (bf16[768,2304]{1,0:T(8,128)(2,1)}, bf16[256,128]{1,0:T(8,128)(2,1)}, bf16[4,2,2,2,24,768]{5,4,3,2,1,0:T(8,128)(2,1)}, bf16[4,2,2,2,24,30...) custom-call(bf16[2048,768]{1,0:T(8,128)(2,1)} %tokens_ref.5, ...), custom_call_target="tpu_custom_call" | custom-call | tf_op jit(solution)/shard_map/attention_forward/pallas_call | solution.py:718
  95.6 47.7 %feed_forward.1 = (f32[2048,768]{1,0:T(8,128)}, f32[2048,128]{1,0:T(8,128)}, bf16[2048,768]{1,0:T(8,128)(2,1)}, bf16[2048,3072]{1,0:T(8,128)(2,1)}, bf16[2048,30...) custom-call(bf16[2048,768]{1,0:T(8,128)(2,1)} %tokens_ref.5, ...), custom_call_target="tpu_custom_call" | custom-call | tf_op jit(solution)/shard_map/feed_forward/pallas_call | solution.py:800
  143.3 14.8 %fin_grad.1 = bf16[3072,768]{1,0:T(8,128)(2,1)} custom-call(bf16[2048,3072]{1,0:T(8,128)(2,1)} %get-tuple-element.58.act_ref, bf16[2048,768]{1,0:T(8,128)(2,1)} %get-tuple-element.52.gffn_ref), custom_call_target="tpu_custom_call" | custom-call | tf_op jit(solution)/shard_map/fin_grad/pallas_call | solution.py:832
  158.1 64.7 %feed_backward.1 = (bf16[768,3072]{1,0:T(8,128)(2,1)}, f32[8,3072]{1,0:T(8,128)}, f32[2048,768]{1,0:T(8,128)}, bf16[2048,768]{1,0:T(8,128)(2,1)}, bf16[768,768]{...) custom-call(bf16[2048,768]{1,0:T(8,128)(2,1)} %get-tuple-element.52.gffn_ref, ...), custom_call_target="tpu_custom_call" | custom-call | tf_op jit(solution)/shard_map/feed_backward/pallas_call | solution.py:942
  222.8 83.5 %attention_backward.1 = (f32[2048,768]{1,0:T(8,128)}, f32[24,2304]{1,0:T(8,128)}, f32[24,768]{1,0:T(8,128)}, f32[24,3072]{1,0:T(8,128)}, f32[8,128]{1,0:T(8,128)}) custom-call(bf16[2048,2304]{1,0:T(8,128)(2,1)} %get-tuple-element.51.q_ref.k_ref.v_ref, bf16[2048,2304]{1,0:T(8,128)(2,1)} %get-tuple-element.51.q_ref.k_ref.v_ref, ...), custom_call_target="tpu_custom_call" | custom-call | tf_op jit(solution)/shard_map/attention_backward/pallas_call | solution.py:1146
  306.3 1.2 slice_bitcast_fusion.3
  307.5 1.2 slice_bitcast_fusion.7
  308.7 1.4 slice_bitcast_fusion
  310.1 0.0 copy-start.1
  310.1 0.0 copy-start
  310.1 6.0 %copy.34 = f32[2048,768]{1,0:T(8,128)} copy(f32[2048,768]{1,0:T(8,128)} %get-tuple-element.103) | data formatting | bytes 12582912
  316.1 0.0 copy-done.2
  316.1 0.7 copy.35
  316.8 0.0 copy-done.3
  316.8 0.6 copy.36
  317.4 0.0 copy-done.1
  317.4 0.7 copy.37
  318.1 0.7 copy.38
  (3 shorter events, 0.0 us)
Async XLA Ops:
  310.1 6.0 %copy-start.2 = (f32[24,2304]{1,0:T(8,128)S(1)}, f32[24,2304]{1,0:T(8,128)}, u32[]{:S(2)}) copy-start(f32[24,2304]{1,0:T(8,128)} %get-tuple-element.104) | copy-start | bytes 663556
  310.1 6.7 %copy-start.3 = (f32[24,768]{1,0:T(8,128)S(1)}, f32[24,768]{1,0:T(8,128)}, u32[]{:S(2)}) copy-start(f32[24,768]{1,0:T(8,128)} %get-tuple-element.106) | copy-start | bytes 221188
  310.1 7.3 %copy-start.1 = (f32[24,3072]{1,0:T(8,128)S(1)}, f32[24,3072]{1,0:T(8,128)}, u32[]{:S(2)}) copy-start(f32[24,3072]{1,0:T(8,128)} %get-tuple-element.110) | copy-start | bytes 884740
  310.1 8.0 %copy-start = (f32[96,768]{1,0:T(8,128)S(1)}, f32[96,768]{1,0:T(8,128)}, u32[]{:S(2)}) copy-start(f32[96,768]{1,0:T(8,128)} %get-tuple-element.112) | copy-start | bytes 884740

commit v6 on v5

--- a/solution.py
+++ b/solution.py
@@ -516,6 +516,16 @@
     def tick(self, now):
         for number, acts in self.due.items():
             @pl.when(now == number)
+            def _():
+                for act in acts:
+                    act()
+
+    def tick_at(self, step, size, index):
+        for number, acts in self.due.items():
+            if number % size != index:
+                continue
+
+            @pl.when(step == number // size)
             def _():
                 for act in acts:
                     act()
@@ -840,7 +850,7 @@
     )(act, gffn)
 
 
-FIN_STEPS = ((0, 3, 9, 14), (0, 6, 13, 18), (1, 9, 17, 22), (2, 12, 21, 26))
+FIN_STEPS = ((0, 2, 9, 14), (0, 6, 13, 18), (1, 10, 18, 23), (2, 14, 23, 27))
 FEED_CHUNKS = 6
 
 
@@ -882,17 +892,14 @@
     def _():
         gbin_ref[...] = jnp.zeros_like(gbin_ref)
 
-        def one_tile(index, _):
+        for index in range(tiles):
             if planes:
-                schedule.tick(step * tiles + index)
-            here = pl.ds(pl.multiple_of(index * tile, tile), tile)
+                schedule.tick_at(step, tiles, index)
+            here = slice(index * tile, (index + 1) * tile)
             gpre = (dot_nt(gffn_ref[here], wfin_ref[...]) * slope_ref[here].astype(F32)).astype(BF16)
             gpre_ref[here] = gpre
             gbin_ref[0:1] += column_sum(gpre.astype(F32))
             acc_ref[here] += dot_nt(gpre, win_ref[...])
-            return 0
-
-        lax.fori_loop(0, tiles, one_tile, 0)
         dwin_ref[...] = dot_nn(low_t_ref[...], gpre_ref[...]).astype(BF16)
 
     @pl.when(step >= FEED_CHUNKS)

time: 319 us -> 316 us (level)
    pallas_call x1, Pallas kernels: 64.7 us -> 61.4 us  [feed_backward(): pl.pallas_call(functools.partial(feed_back_kernel, planes), grid=(FEED_CH...]
where the time goes in v6:
time: 316 us
  Pallas kernels  298 us (94%)
  local copies, waits for them, and re-layouts  17.1 us (5%)
    pallas_call x1, Pallas kernels, attention_forward(): pl.pallas_call(functools.partial(attention_kernel, planes, pieces), grid=...  90.4 us
    pallas_call x1, Pallas kernels, attention_backward(): pl.pallas_call(functools.partial(attention_back_kernel, planes, pieces, d...  83.5 us
    pallas_call x1, Pallas kernels, feed_backward(): pl.pallas_call(functools.partial(feed_back_kernel, planes), grid=(FEED_CH...  61.4 us
    pallas_call x1, Pallas kernels, feed_forward(): pl.pallas_call(feed_kernel, grid=(total // tile,), in_specs=[rows, rows,...  47.7 us
    pallas_call x1, Pallas kernels, fin_grad(): pl.pallas_call(fin_grad_kernel, grid=(hidden // chunk,), in_specs=[pl.Blo...  14.8 us
    unnamed x13, local copies, waits for them, and re-layouts  8.73 us

profile of v6, /device:TPU:0, one launch (start us, length us, event | category | flops | bytes accessed | tf_op | source)
XLA Modules:
  0.0 315.5 jit_solution(2937200801997784013)
XLA Ops:
  0.6 0.7 pad_bitcast_fusion.6
  1.3 0.7 pad_bitcast_fusion.4
  2.0 0.7 pad_bitcast_fusion.2
  2.7 0.7 pad_bitcast_fusion
  3.4 0.6 stack.35.refs_1_
  4.0 1.3 reshape.49.segment_ref
  5.3 90.4 %attention_forward.1 = (bf16[768,2304]{1,0:T(8,128)(2,1)}, bf16[256,128]{1,0:T(8,128)(2,1)}, bf16[4,2,2,2,24,768]{5,4,3,2,1,0:T(8,128)(2,1)}, bf16[4,2,2,2,24,30...) custom-call(bf16[2048,768]{1,0:T(8,128)(2,1)} %tokens_ref.5, ...), custom_call_target="tpu_custom_call" | custom-call | tf_op jit(solution)/shard_map/attention_forward/pallas_call | solution.py:728
  95.6 47.7 %feed_forward.1 = (f32[2048,768]{1,0:T(8,128)}, f32[2048,128]{1,0:T(8,128)}, bf16[2048,768]{1,0:T(8,128)(2,1)}, bf16[2048,3072]{1,0:T(8,128)(2,1)}, bf16[2048,30...) custom-call(bf16[2048,768]{1,0:T(8,128)(2,1)} %tokens_ref.5, ...), custom_call_target="tpu_custom_call" | custom-call | tf_op jit(solution)/shard_map/feed_forward/pallas_call | solution.py:810
  143.3 14.8 %fin_grad.1 = bf16[3072,768]{1,0:T(8,128)(2,1)} custom-call(bf16[2048,3072]{1,0:T(8,128)(2,1)} %get-tuple-element.58.act_ref, bf16[2048,768]{1,0:T(8,128)(2,1)} %get-tuple-element.52.gffn_ref), custom_call_target="tpu_custom_call" | custom-call | tf_op jit(solution)/shard_map/fin_grad/pallas_call | solution.py:842
  158.1 61.4 %feed_backward.1 = (bf16[768,3072]{1,0:T(8,128)(2,1)}, f32[8,3072]{1,0:T(8,128)}, f32[2048,768]{1,0:T(8,128)}, bf16[2048,768]{1,0:T(8,128)(2,1)}, bf16[768,768]{...) custom-call(bf16[2048,768]{1,0:T(8,128)(2,1)} %get-tuple-element.52.gffn_ref, ...), custom_call_target="tpu_custom_call" | custom-call | tf_op jit(solution)/shard_map/feed_backward/pallas_call | solution.py:949
  219.5 83.5 %attention_backward.1 = (f32[2048,768]{1,0:T(8,128)}, f32[24,2304]{1,0:T(8,128)}, f32[24,768]{1,0:T(8,128)}, f32[24,3072]{1,0:T(8,128)}, f32[8,128]{1,0:T(8,128)}) custom-call(bf16[2048,2304]{1,0:T(8,128)(2,1)} %get-tuple-element.51.q_ref.k_ref.v_ref, bf16[2048,2304]{1,0:T(8,128)(2,1)} %get-tuple-element.51.q_ref.k_ref.v_ref, ...), custom_call_target="tpu_custom_call" | custom-call | tf_op jit(solution)/shard_map/attention_backward/pallas_call | solution.py:1153
  303.0 1.2 slice_bitcast_fusion.3
  304.2 1.2 slice_bitcast_fusion.7
  305.4 1.4 slice_bitcast_fusion
  306.8 0.0 copy-start.1
  306.8 0.0 copy-start
  306.8 6.0 %copy.34 = f32[2048,768]{1,0:T(8,128)} copy(f32[2048,768]{1,0:T(8,128)} %get-tuple-element.103) | data formatting | bytes 12582912
  312.8 0.0 copy-done.2
  312.8 0.7 copy.35
  313.5 0.6 copy.36
  314.1 0.0 copy-done.1
  314.1 0.7 copy.37
  314.8 0.0 copy-done
  314.8 0.7 copy.38
  (3 shorter events, 0.0 us)
Async XLA Ops:
  306.8 6.0 %copy-start.2 = (f32[24,2304]{1,0:T(8,128)S(1)}, f32[24,2304]{1,0:T(8,128)}, u32[]{:S(2)}) copy-start(f32[24,2304]{1,0:T(8,128)} %get-tuple-element.104) | copy-start | bytes 663556
  306.8 6.7 %copy-start.3 = (f32[24,768]{1,0:T(8,128)S(1)}, f32[24,768]{1,0:T(8,128)}, u32[]{:S(2)}) copy-start(f32[24,768]{1,0:T(8,128)} %get-tuple-element.106) | copy-start | bytes 221188
  306.8 7.3 %copy-start.1 = (f32[24,3072]{1,0:T(8,128)S(1)}, f32[24,3072]{1,0:T(8,128)}, u32[]{:S(2)}) copy-start(f32[24,3072]{1,0:T(8,128)} %get-tuple-element.110) | copy-start | bytes 884740
  306.8 8.0 %copy-start = (f32[96,768]{1,0:T(8,128)S(1)}, f32[96,768]{1,0:T(8,128)}, u32[]{:S(2)}) copy-start(f32[96,768]{1,0:T(8,128)} %get-tuple-element.112) | copy-start | bytes 884740
